TPU v7x, 32 devices: a whole 2x2x4 slice. The times are simulated.
32 devices in a mesh: section: 4 (over y, x), strip: 4 (over z), mirror: 2 (over core).
Axes of the slice: x: 2, y: 2, z: 4, core: 2. Of those that a mesh axis runs over, the one named last changes fastest.
Arguments:
- grad_top: bfloat16 [2, 4, 32, 16, 256], P('mirror', None, 'strip'), may hold values from -6 to 6
- acts: bfloat16 [2, 4, 4, 32, 16, 256], P('mirror', 'section', None, 'strip'), may hold values from -6 to 6
- masks: int32 [2, 4, 4, 32, 16, 256], P('mirror', 'section', None, 'strip'), may hold values 0 or 1
- kernels: bfloat16 [2, 4, 3, 3, 256, 256], P('mirror', 'section'), as said below
Outputs:
- input_grads: bfloat16 [2, 4, 4, 32, 16, 256], P('mirror', 'section', None, 'strip')
- kernel_grads: float32 [2, 4, 2304, 256], P('mirror', 'section', 'strip')
Inputs may be any that keep to these rules, and one draw needn't show every extreme that they name: kernels[1, s] equals kernels[0, 3 - s]: both replicas hold the same layers, in opposite order over the section positions.
All inputs are finite; a program needn't handle non-finite values. No bound on the sum of `masks` on one device may be relied on, other than what follows from the above.
Results may differ from a plain program's by a relative error of at most 0.015.
Values may be sent and summed in bfloat16 or wider, within the bound.
No kernel may reach another device: no remote copies, remote signals or barrier semaphores. Data moves between devices by JAX's collectives and lax.ppermute only.
A program may use at most 64 MiB of HBM per device.

v0:
```python
import math

import jax
import jax.numpy as jnp
from jax import lax
from jax.sharding import PartitionSpec as P


def with_halo(block, sides, width):
    for axis, dim in sides:
        count = lax.axis_size(axis)
        forward = [(i, i + 1) for i in range(count - 1)]
        backward = [(target, source) for source, target in forward]
        low = lax.ppermute(
            lax.slice_in_dim(block, block.shape[dim] - width, None, axis=dim), axis, forward
        )
        high = lax.ppermute(lax.slice_in_dim(block, 0, width, axis=dim), axis, backward)
        block = jnp.concatenate([low, block, high], axis=dim)
    return block


def from_behind(block, axis, distance):
    devices = range(lax.axis_size(axis))
    route = [(i - distance, i) for i in devices if i - distance in devices]
    return lax.ppermute(block, axis, route)


def swapped(shard, axis, bit):
    return lax.ppermute(shard, axis, [(i, i ^ 1 << bit) for i in range(lax.axis_size(axis))])


def unfold(padded, height, tile_width, flipped):
    pieces = []
    for row_shift in range(3):
        for col_shift in range(3):
            if flipped:
                row_start = 2 - row_shift
                col_start = 2 - col_shift
            else:
                row_start = row_shift
                col_start = col_shift
            pieces.append(
                padded[row_start : row_start + height, col_start : col_start + tile_width]
            )
    stacked = jnp.concatenate(pieces, axis=-1)
    return stacked.reshape(height * tile_width, stacked.shape[-1])


def shards(grad_top, acts, masks, kernels):
    sections = lax.axis_size("section")
    strips = lax.axis_size("strip")
    section_id = lax.axis_index("section")
    mirror_id = lax.axis_index("mirror")
    layer_id = jnp.where(mirror_id == 0, section_id, sections - 1 - section_id)
    delay_ticks = sections - 1 - layer_id
    top_grads = grad_top[0]
    inputs_all = acts[0, 0]
    masks_all = masks[0, 0]
    kernel = kernels[0, 0]
    micros, tile_rows, tile_width, channels = inputs_all.shape
    kernel_t = jnp.transpose(kernel, (0, 1, 3, 2)).reshape(9 * channels, channels)
    width_pad = ((0, 0), (1, 1), (0, 0))

    def compute(operands):
        grad_rim, input_rim, grad_out, kernel_acc = operands
        grad_pre = grad_rim[1:-1]
        input_patch = unfold(jnp.pad(input_rim, width_pad), tile_rows, tile_width, False)
        grad_patch = unfold(jnp.pad(grad_rim, width_pad), tile_rows, tile_width, True)
        kernel_acc = kernel_acc + lax.dot_general(
            input_patch,
            grad_pre.reshape(tile_rows * tile_width, channels),
            (((0,), (0,)), ((), ())),
            preferred_element_type=jnp.float32,
        )
        branch = jnp.dot(grad_patch, kernel_t, preferred_element_type=jnp.float32)
        grad_in = grad_out.astype(jnp.float32) + branch.reshape(tile_rows, tile_width, channels)
        return (grad_in.astype(jnp.bfloat16), kernel_acc)

    def skipped(operands):
        return (jnp.zeros_like(operands[2]), operands[3])

    def backward(tick_id, carried):
        incoming, kernel_acc, results = carried
        micro_id = tick_id - delay_ticks
        active = jnp.logical_and(micro_id >= 0, micro_id < micros)
        clipped = jnp.clip(micro_id, 0, micros - 1)
        from_top = lax.dynamic_index_in_dim(top_grads, clipped, 0, keepdims=False)
        grad_out = jnp.where(layer_id == sections - 1, from_top, incoming)
        relu_mask = lax.dynamic_index_in_dim(masks_all, clipped, 0, keepdims=False)
        grad_pre = (grad_out.astype(jnp.float32) * relu_mask.astype(jnp.float32)).astype(
            jnp.bfloat16
        )
        inputs = lax.dynamic_index_in_dim(inputs_all, clipped, 0, keepdims=False)
        rimmed = with_halo(jnp.stack([grad_pre, inputs]), (("strip", 1),), 1)
        grad_rim = rimmed[0]
        input_rim = rimmed[1]
        grad_in, kernel_acc = lax.cond(
            active, compute, skipped, (grad_rim, input_rim, grad_out, kernel_acc)
        )
        current = lax.dynamic_index_in_dim(results, clipped, 0, keepdims=False)
        stored = jnp.where(active, grad_in, current)
        results = lax.dynamic_update_index_in_dim(results, stored, clipped, 0)
        from_below = from_behind(grad_in, "section", -1)
        higher = from_behind(grad_in, "section", 1)
        incoming = jnp.where(mirror_id == 0, from_below, higher)
        return (incoming, kernel_acc, results)

    initial = (
        jnp.zeros((tile_rows, tile_width, channels), jnp.bfloat16),
        jnp.zeros((9 * channels, channels), jnp.float32),
        jnp.zeros((micros, tile_rows, tile_width, channels), jnp.bfloat16),
    )
    incoming, kernel_acc, results = lax.fori_loop(0, micros + sections - 1, backward, initial)
    share_rows = 9 * channels // strips
    own_share = lax.psum_scatter(kernel_acc, "strip", scatter_dimension=0, tiled=True)
    blocks = own_share.reshape(sections, share_rows * channels // sections)
    spread = lax.all_to_all(blocks, "section", split_axis=0, concat_axis=0, tiled=True)
    across = swapped(spread.astype(jnp.bfloat16), "mirror", 0).astype(spread.dtype)
    combined = spread + jnp.flip(across, 0)
    returned = lax.all_to_all(combined, "section", split_axis=0, concat_axis=0, tiled=True)
    summed_share = returned.reshape(share_rows, channels)
    factor = 1.0 / math.sqrt(2.0 * micros * tile_rows * strips * tile_width)
    kernel_grads = (summed_share * factor)[None, None]
    input_grads = results[None, None]
    return (input_grads, kernel_grads)


def solution(mesh):
    return jax.shard_map(
        shards,
        mesh=mesh,
        in_specs=(
            P("mirror", None, "strip", None, None),
            P("mirror", "section", None, "strip", None, None),
            P("mirror", "section", None, "strip", None, None),
            P("mirror", "section", None, None, None, None),
        ),
        out_specs=(
            P("mirror", "section", None, "strip", None, None),
            P("mirror", "section", "strip", None),
        ),
        check_vma=False,
    )
```

profile of v0, /device:TPU:0, one launch (start us, length us, event | category | flops | bytes accessed | tf_op | source)
XLA Modules:
  0.0 257.3 jit_solution(16138252822325862380)
XLA Ops:
  10.4 149.0 %while.23 = (s32[]{:T(128)}, bf16[8,16,256]{2,1,0:T(8,128)(2,1)S(1)}, f32[2304,256]{1,0:T(8,128)}, bf16[4,8,16,256]{3,2,1,0:T(8,128)(2,1)S(1)}, pred[]{:T(512)},...) while((s32[]{:T(128)}, ...), condition=%wide.region_3.4_spmd.clone, body=%wide.region_0.3_spmd.clone.sunk | while | flops 303202304 | bytes 31228396 | solution.py:113
  13.5 5.6 %collective-permute-start.1 = (bf16[2,1,16,256]{3,2,1,0:T(8,128)(2,1)S(1)}, bf16[2,1,16,256]{3,2,1,0:T(8,128)(2,1)S(1)}, u32[]{:S(2)}, u32[]{:S(2)}) collective-permute-start(bf16[2,1,16,256]{3,2,1,0:T(8,128)(2,1)S(1)} %get-tuple-element.435), channel_id=1, source_target_pairs={{0,2},{2,4},{4,6},{1,3},{3,5},{5,7},{8,10},{10,12},{12,14},{9,11},... | collective-permute-start | bytes 49160 | tf_op jit(solution)/shard_map/while/body/eval_jaxpr/ppermute | solution.py:14
  21.9 4.5 %collective-permute-start.3 = (bf16[8,16,256]{2,1,0:T(8,128)(2,1)S(1)}, bf16[8,16,256]{2,1,0:T(8,128)(2,1)S(1)}, u32[]{:S(2)}, u32[]{:S(2)}) collective-permute-start(bf16[8,16,256]{2,1,0:T(8,128)(2,1)S(1)} %get-tuple-element.436), channel_id=1, source_target_pairs={{0,8},{8,16},{16,24},{1,9},{9,17},{17,25},{2,10},{10,18},{18,26},{... | collective-permute-start | bytes 196616 | tf_op jit(solution)/shard_map/while/body/eval_jaxpr/ppermute | solution.py:25
  26.8 1.6 collective-permute-done.3
  31.5 4.8 %collective-permute-start.1 = (bf16[2,1,16,256]{3,2,1,0:T(8,128)(2,1)S(1)}, bf16[2,1,16,256]{3,2,1,0:T(8,128)(2,1)S(1)}, u32[]{:S(2)}, u32[]{:S(2)}) collective-permute-start(bf16[2,1,16,256]{3,2,1,0:T(8,128)(2,1)S(1)} %get-tuple-element.435), channel_id=1, source_target_pairs={{0,2},{2,4},{4,6},{1,3},{3,5},{5,7},{8,10},{10,12},{12,14},{9,11},... | collective-permute-start | bytes 49160 | tf_op jit(solution)/shard_map/while/body/eval_jaxpr/ppermute | solution.py:14
  39.2 5.4 %collective-permute-start.3 = (bf16[8,16,256]{2,1,0:T(8,128)(2,1)S(1)}, bf16[8,16,256]{2,1,0:T(8,128)(2,1)S(1)}, u32[]{:S(2)}, u32[]{:S(2)}) collective-permute-start(bf16[8,16,256]{2,1,0:T(8,128)(2,1)S(1)} %get-tuple-element.436), channel_id=1, source_target_pairs={{0,8},{8,16},{16,24},{1,9},{9,17},{17,25},{2,10},{10,18},{18,26},{... | collective-permute-start | bytes 196616 | tf_op jit(solution)/shard_map/while/body/eval_jaxpr/ppermute | solution.py:25
  44.8 1.6 collective-permute-done.3
  49.6 4.8 %collective-permute-start.1 = (bf16[2,1,16,256]{3,2,1,0:T(8,128)(2,1)S(1)}, bf16[2,1,16,256]{3,2,1,0:T(8,128)(2,1)S(1)}, u32[]{:S(2)}, u32[]{:S(2)}) collective-permute-start(bf16[2,1,16,256]{3,2,1,0:T(8,128)(2,1)S(1)} %get-tuple-element.435), channel_id=1, source_target_pairs={{0,2},{2,4},{4,6},{1,3},{3,5},{5,7},{8,10},{10,12},{12,14},{9,11},... | collective-permute-start | bytes 49160 | tf_op jit(solution)/shard_map/while/body/eval_jaxpr/ppermute | solution.py:14
  57.2 13.1 %collective-permute-start.3 = (bf16[8,16,256]{2,1,0:T(8,128)(2,1)S(1)}, bf16[8,16,256]{2,1,0:T(8,128)(2,1)S(1)}, u32[]{:S(2)}, u32[]{:S(2)}) collective-permute-start(bf16[8,16,256]{2,1,0:T(8,128)(2,1)S(1)} %get-tuple-element.436), channel_id=1, source_target_pairs={{0,8},{8,16},{16,24},{1,9},{9,17},{17,25},{2,10},{10,18},{18,26},{... | collective-permute-start | bytes 196616 | tf_op jit(solution)/shard_map/while/body/eval_jaxpr/ppermute | solution.py:25
  70.6 1.6 collective-permute-done.3
  75.3 4.8 %collective-permute-start.1 = (bf16[2,1,16,256]{3,2,1,0:T(8,128)(2,1)S(1)}, bf16[2,1,16,256]{3,2,1,0:T(8,128)(2,1)S(1)}, u32[]{:S(2)}, u32[]{:S(2)}) collective-permute-start(bf16[2,1,16,256]{3,2,1,0:T(8,128)(2,1)S(1)} %get-tuple-element.435), channel_id=1, source_target_pairs={{0,2},{2,4},{4,6},{1,3},{3,5},{5,7},{8,10},{10,12},{12,14},{9,11},... | collective-permute-start | bytes 49160 | tf_op jit(solution)/shard_map/while/body/eval_jaxpr/ppermute | solution.py:14
  81.6 3.7 %conditional.3 = (bf16[8,16,256]{2,1,0:T(8,128)(2,1)S(1)}, f32[2304,256]{1,0:T(8,128)}) conditional(s32[]{:T(128)} %convert_element_type.80, f32[2304,256]{1,0:T(8,128)} %get-tuple-element.459, (bf16[8,16,256]{2,1,0:T(8,128)(2,1)S(1)}, bf16[2,10,16,256]{3,2,1,0:T(8,128)(2,1)S(1)}, bf16[2304,256]{1,0:T(8,128)(2,1)S(1)}, f32[2304,256]{1,0:T(8,128)}) %tuple.70), branch_computations={%region_1.1_spmd, %region_2.2_spmd} | conditional | flops 302678016 | bytes 29032520 | solution.py:97
  86.6 5.8 %collective-permute-start.3 = (bf16[8,16,256]{2,1,0:T(8,128)(2,1)S(1)}, bf16[8,16,256]{2,1,0:T(8,128)(2,1)S(1)}, u32[]{:S(2)}, u32[]{:S(2)}) collective-permute-start(bf16[8,16,256]{2,1,0:T(8,128)(2,1)S(1)} %get-tuple-element.436), channel_id=1, source_target_pairs={{0,8},{8,16},{16,24},{1,9},{9,17},{17,25},{2,10},{10,18},{18,26},{... | collective-permute-start | bytes 196616 | tf_op jit(solution)/shard_map/while/body/eval_jaxpr/ppermute | solution.py:25
  92.7 1.6 collective-permute-done.3
  97.4 4.8 %collective-permute-start.1 = (bf16[2,1,16,256]{3,2,1,0:T(8,128)(2,1)S(1)}, bf16[2,1,16,256]{3,2,1,0:T(8,128)(2,1)S(1)}, u32[]{:S(2)}, u32[]{:S(2)}) collective-permute-start(bf16[2,1,16,256]{3,2,1,0:T(8,128)(2,1)S(1)} %get-tuple-element.435), channel_id=1, source_target_pairs={{0,2},{2,4},{4,6},{1,3},{3,5},{5,7},{8,10},{10,12},{12,14},{9,11},... | collective-permute-start | bytes 49160 | tf_op jit(solution)/shard_map/while/body/eval_jaxpr/ppermute | solution.py:14
  103.7 3.7 %conditional.3 = (bf16[8,16,256]{2,1,0:T(8,128)(2,1)S(1)}, f32[2304,256]{1,0:T(8,128)}) conditional(s32[]{:T(128)} %convert_element_type.80, f32[2304,256]{1,0:T(8,128)} %get-tuple-element.459, (bf16[8,16,256]{2,1,0:T(8,128)(2,1)S(1)}, bf16[2,10,16,256]{3,2,1,0:T(8,128)(2,1)S(1)}, bf16[2304,256]{1,0:T(8,128)(2,1)S(1)}, f32[2304,256]{1,0:T(8,128)}) %tuple.70), branch_computations={%region_1.1_spmd, %region_2.2_spmd} | conditional | flops 302678016 | bytes 29032520 | solution.py:97
  108.7 5.8 %collective-permute-start.3 = (bf16[8,16,256]{2,1,0:T(8,128)(2,1)S(1)}, bf16[8,16,256]{2,1,0:T(8,128)(2,1)S(1)}, u32[]{:S(2)}, u32[]{:S(2)}) collective-permute-start(bf16[8,16,256]{2,1,0:T(8,128)(2,1)S(1)} %get-tuple-element.436), channel_id=1, source_target_pairs={{0,8},{8,16},{16,24},{1,9},{9,17},{17,25},{2,10},{10,18},{18,26},{... | collective-permute-start | bytes 196616 | tf_op jit(solution)/shard_map/while/body/eval_jaxpr/ppermute | solution.py:25
  114.8 1.6 collective-permute-done.3
  119.6 4.8 %collective-permute-start.1 = (bf16[2,1,16,256]{3,2,1,0:T(8,128)(2,1)S(1)}, bf16[2,1,16,256]{3,2,1,0:T(8,128)(2,1)S(1)}, u32[]{:S(2)}, u32[]{:S(2)}) collective-permute-start(bf16[2,1,16,256]{3,2,1,0:T(8,128)(2,1)S(1)} %get-tuple-element.435), channel_id=1, source_target_pairs={{0,2},{2,4},{4,6},{1,3},{3,5},{5,7},{8,10},{10,12},{12,14},{9,11},... | collective-permute-start | bytes 49160 | tf_op jit(solution)/shard_map/while/body/eval_jaxpr/ppermute | solution.py:14
  125.9 3.7 %conditional.3 = (bf16[8,16,256]{2,1,0:T(8,128)(2,1)S(1)}, f32[2304,256]{1,0:T(8,128)}) conditional(s32[]{:T(128)} %convert_element_type.80, f32[2304,256]{1,0:T(8,128)} %get-tuple-element.459, (bf16[8,16,256]{2,1,0:T(8,128)(2,1)S(1)}, bf16[2,10,16,256]{3,2,1,0:T(8,128)(2,1)S(1)}, bf16[2304,256]{1,0:T(8,128)(2,1)S(1)}, f32[2304,256]{1,0:T(8,128)}) %tuple.70), branch_computations={%region_1.1_spmd, %region_2.2_spmd} | conditional | flops 302678016 | bytes 29032520 | solution.py:97
  130.8 5.8 %collective-permute-start.3 = (bf16[8,16,256]{2,1,0:T(8,128)(2,1)S(1)}, bf16[8,16,256]{2,1,0:T(8,128)(2,1)S(1)}, u32[]{:S(2)}, u32[]{:S(2)}) collective-permute-start(bf16[8,16,256]{2,1,0:T(8,128)(2,1)S(1)} %get-tuple-element.436), channel_id=1, source_target_pairs={{0,8},{8,16},{16,24},{1,9},{9,17},{17,25},{2,10},{10,18},{18,26},{... | collective-permute-start | bytes 196616 | tf_op jit(solution)/shard_map/while/body/eval_jaxpr/ppermute | solution.py:25
  137.0 1.6 collective-permute-done.3
  141.7 4.8 %collective-permute-start.1 = (bf16[2,1,16,256]{3,2,1,0:T(8,128)(2,1)S(1)}, bf16[2,1,16,256]{3,2,1,0:T(8,128)(2,1)S(1)}, u32[]{:S(2)}, u32[]{:S(2)}) collective-permute-start(bf16[2,1,16,256]{3,2,1,0:T(8,128)(2,1)S(1)} %get-tuple-element.435), channel_id=1, source_target_pairs={{0,2},{2,4},{4,6},{1,3},{3,5},{5,7},{8,10},{10,12},{12,14},{9,11},... | collective-permute-start | bytes 49160 | tf_op jit(solution)/shard_map/while/body/eval_jaxpr/ppermute | solution.py:14
  148.0 3.7 %conditional.3 = (bf16[8,16,256]{2,1,0:T(8,128)(2,1)S(1)}, f32[2304,256]{1,0:T(8,128)}) conditional(s32[]{:T(128)} %convert_element_type.80, f32[2304,256]{1,0:T(8,128)} %get-tuple-element.459, (bf16[8,16,256]{2,1,0:T(8,128)(2,1)S(1)}, bf16[2,10,16,256]{3,2,1,0:T(8,128)(2,1)S(1)}, bf16[2304,256]{1,0:T(8,128)(2,1)S(1)}, f32[2304,256]{1,0:T(8,128)}) %tuple.70), branch_computations={%region_1.1_spmd, %region_2.2_spmd} | conditional | flops 302678016 | bytes 29032520 | solution.py:97
  153.0 4.5 %collective-permute-start.3 = (bf16[8,16,256]{2,1,0:T(8,128)(2,1)S(1)}, bf16[8,16,256]{2,1,0:T(8,128)(2,1)S(1)}, u32[]{:S(2)}, u32[]{:S(2)}) collective-permute-start(bf16[8,16,256]{2,1,0:T(8,128)(2,1)S(1)} %get-tuple-element.436), channel_id=1, source_target_pairs={{0,8},{8,16},{16,24},{1,9},{9,17},{17,25},{2,10},{10,18},{18,26},{... | collective-permute-start | bytes 196616 | tf_op jit(solution)/shard_map/while/body/eval_jaxpr/ppermute | solution.py:25
  157.8 1.6 collective-permute-done.3
  159.5 51.3 %reduce-scatter.2.cloned.1.call-done = f32[576,256]{1,0:T(8,128)} async-done(((f32[2304,256]{1,0:T(8,128)}), f32[576,256]{1,0:T(8,128)}) %reduce-scatter.2.cloned.1.call-update) | async-done | bytes 589840 | tf_op jit(solution)/shard_map/reduce_scatter | solution.py:115
  210.7 1.7 all_to_all.14
  212.4 12.4 %all_to_all.21 = f32[4,1,36864]{2,1,0:T(1,128)S(1)} all-to-all(f32[4,1,36864]{2,1,0:T(1,128)S(1)} %all_to_all.14), channel_id=1, replica_groups=mesh['section'=4,'strip'=4,'mirror'=2] {'section'}, dimensions={0} | all-to-all | bytes 1179648 | tf_op jit(solution)/shard_map/all_to_all | solution.py:117
  226.9 7.1 %rev.4 = f32[4,36864]{1,0:T(4,128)S(1)} reverse(bf16[4,36864]{1,0:T(4,128)(2,1)S(1)} %collective-permute-done.4), dimensions={0} | reverse | bytes 884736 | tf_op jit(solution)/shard_map/jit(_flip)/rev | solution.py:119
  235.1 12.4 %all_to_all.22 = f32[4,1,36864]{2,1,0:T(1,128)S(1)} all-to-all(f32[4,1,36864]{2,1,0:T(1,128)S(1)} %copy.8), channel_id=1, replica_groups=mesh['section'=4,'strip'=4,'mirror'=2] {'section'}, dimensions={0} | all-to-all | bytes 1179648 | tf_op jit(solution)/shard_map/all_to_all | solution.py:120
  247.5 1.8 multiply_reduce_fusion
  (188 shorter events, 64.6 us)
Async XLA Ops:
  7.2 203.6 %reduce-scatter.2.cloned.1.call-start = ((), (), s32[]{:S(2)}) async-start(), calls=%async_computation.3 | async-start | bytes 2949120 | tf_op jit(solution)/shard_map/reduce_scatter | solution.py:115
  12.2 6.9 %collective-permute-start = (bf16[2,1,16,256]{3,2,1,0:T(8,128)(2,1)S(1)}, bf16[2,1,16,256]{3,2,1,0:T(8,128)(2,1)S(1)}, u32[]{:S(2)}, u32[]{:S(2)}) collective-permute-start(bf16[2,1,16,256]{3,2,1,0:T(8,128)(2,1)S(1)} %get-tuple-element.434), channel_id=1, source_target_pairs={{2,0},{4,2},{6,4},{3,1},{5,3},{7,5},{10,8},{12,10},{14,12},{11,9},... | collective-permute-start | bytes 49160 | tf_op jit(solution)/shard_map/while/body/eval_jaxpr/ppermute | solution.py:17
  13.5 7.0 %collective-permute-start.1 = (bf16[2,1,16,256]{3,2,1,0:T(8,128)(2,1)S(1)}, bf16[2,1,16,256]{3,2,1,0:T(8,128)(2,1)S(1)}, u32[]{:S(2)}, u32[]{:S(2)}) collective-permute-start(bf16[2,1,16,256]{3,2,1,0:T(8,128)(2,1)S(1)} %get-tuple-element.435), channel_id=1, source_target_pairs={{0,2},{2,4},{4,6},{1,3},{3,5},{5,7},{8,10},{10,12},{12,14},{9,11},... | collective-permute-start | bytes 49160 | tf_op jit(solution)/shard_map/while/body/eval_jaxpr/ppermute | solution.py:14
  20.6 6.2 %collective-permute-start.2 = (bf16[8,16,256]{2,1,0:T(8,128)(2,1)S(1)}, bf16[8,16,256]{2,1,0:T(8,128)(2,1)S(1)}, u32[]{:S(2)}, u32[]{:S(2)}) collective-permute-start(bf16[8,16,256]{2,1,0:T(8,128)(2,1)S(1)} %get-tuple-element.436), channel_id=1, source_target_pairs={{8,0},{16,8},{24,16},{9,1},{17,9},{25,17},{10,2},{18,10},{26,18},{... | collective-permute-start | bytes 196616 | tf_op jit(solution)/shard_map/while/body/eval_jaxpr/ppermute | solution.py:25
  21.9 6.4 %collective-permute-start.3 = (bf16[8,16,256]{2,1,0:T(8,128)(2,1)S(1)}, bf16[8,16,256]{2,1,0:T(8,128)(2,1)S(1)}, u32[]{:S(2)}, u32[]{:S(2)}) collective-permute-start(bf16[8,16,256]{2,1,0:T(8,128)(2,1)S(1)} %get-tuple-element.436), channel_id=1, source_target_pairs={{0,8},{8,16},{16,24},{1,9},{9,17},{17,25},{2,10},{10,18},{18,26},{... | collective-permute-start | bytes 196616 | tf_op jit(solution)/shard_map/while/body/eval_jaxpr/ppermute | solution.py:25
  30.2 6.2 %collective-permute-start = (bf16[2,1,16,256]{3,2,1,0:T(8,128)(2,1)S(1)}, bf16[2,1,16,256]{3,2,1,0:T(8,128)(2,1)S(1)}, u32[]{:S(2)}, u32[]{:S(2)}) collective-permute-start(bf16[2,1,16,256]{3,2,1,0:T(8,128)(2,1)S(1)} %get-tuple-element.434), channel_id=1, source_target_pairs={{2,0},{4,2},{6,4},{3,1},{5,3},{7,5},{10,8},{12,10},{14,12},{11,9},... | collective-permute-start | bytes 49160 | tf_op jit(solution)/shard_map/while/body/eval_jaxpr/ppermute | solution.py:17
  31.5 6.3 %collective-permute-start.1 = (bf16[2,1,16,256]{3,2,1,0:T(8,128)(2,1)S(1)}, bf16[2,1,16,256]{3,2,1,0:T(8,128)(2,1)S(1)}, u32[]{:S(2)}, u32[]{:S(2)}) collective-permute-start(bf16[2,1,16,256]{3,2,1,0:T(8,128)(2,1)S(1)} %get-tuple-element.435), channel_id=1, source_target_pairs={{0,2},{2,4},{4,6},{1,3},{3,5},{5,7},{8,10},{10,12},{12,14},{9,11},... | collective-permute-start | bytes 49160 | tf_op jit(solution)/shard_map/while/body/eval_jaxpr/ppermute | solution.py:14
  37.9 7.0 %collective-permute-start.2 = (bf16[8,16,256]{2,1,0:T(8,128)(2,1)S(1)}, bf16[8,16,256]{2,1,0:T(8,128)(2,1)S(1)}, u32[]{:S(2)}, u32[]{:S(2)}) collective-permute-start(bf16[8,16,256]{2,1,0:T(8,128)(2,1)S(1)} %get-tuple-element.436), channel_id=1, source_target_pairs={{8,0},{16,8},{24,16},{9,1},{17,9},{25,17},{10,2},{18,10},{26,18},{... | collective-permute-start | bytes 196616 | tf_op jit(solution)/shard_map/while/body/eval_jaxpr/ppermute | solution.py:25
  39.2 7.3 %collective-permute-start.3 = (bf16[8,16,256]{2,1,0:T(8,128)(2,1)S(1)}, bf16[8,16,256]{2,1,0:T(8,128)(2,1)S(1)}, u32[]{:S(2)}, u32[]{:S(2)}) collective-permute-start(bf16[8,16,256]{2,1,0:T(8,128)(2,1)S(1)} %get-tuple-element.436), channel_id=1, source_target_pairs={{0,8},{8,16},{16,24},{1,9},{9,17},{17,25},{2,10},{10,18},{18,26},{... | collective-permute-start | bytes 196616 | tf_op jit(solution)/shard_map/while/body/eval_jaxpr/ppermute | solution.py:25
  48.3 6.2 %collective-permute-start = (bf16[2,1,16,256]{3,2,1,0:T(8,128)(2,1)S(1)}, bf16[2,1,16,256]{3,2,1,0:T(8,128)(2,1)S(1)}, u32[]{:S(2)}, u32[]{:S(2)}) collective-permute-start(bf16[2,1,16,256]{3,2,1,0:T(8,128)(2,1)S(1)} %get-tuple-element.434), channel_id=1, source_target_pairs={{2,0},{4,2},{6,4},{3,1},{5,3},{7,5},{10,8},{12,10},{14,12},{11,9},... | collective-permute-start | bytes 49160 | tf_op jit(solution)/shard_map/while/body/eval_jaxpr/ppermute | solution.py:17
  49.6 6.3 %collective-permute-start.1 = (bf16[2,1,16,256]{3,2,1,0:T(8,128)(2,1)S(1)}, bf16[2,1,16,256]{3,2,1,0:T(8,128)(2,1)S(1)}, u32[]{:S(2)}, u32[]{:S(2)}) collective-permute-start(bf16[2,1,16,256]{3,2,1,0:T(8,128)(2,1)S(1)} %get-tuple-element.435), channel_id=1, source_target_pairs={{0,2},{2,4},{4,6},{1,3},{3,5},{5,7},{8,10},{10,12},{12,14},{9,11},... | collective-permute-start | bytes 49160 | tf_op jit(solution)/shard_map/while/body/eval_jaxpr/ppermute | solution.py:14
  55.9 14.7 %collective-permute-start.2 = (bf16[8,16,256]{2,1,0:T(8,128)(2,1)S(1)}, bf16[8,16,256]{2,1,0:T(8,128)(2,1)S(1)}, u32[]{:S(2)}, u32[]{:S(2)}) collective-permute-start(bf16[8,16,256]{2,1,0:T(8,128)(2,1)S(1)} %get-tuple-element.436), channel_id=1, source_target_pairs={{8,0},{16,8},{24,16},{9,1},{17,9},{25,17},{10,2},{18,10},{26,18},{... | collective-permute-start | bytes 196616 | tf_op jit(solution)/shard_map/while/body/eval_jaxpr/ppermute | solution.py:25
  57.2 15.0 %collective-permute-start.3 = (bf16[8,16,256]{2,1,0:T(8,128)(2,1)S(1)}, bf16[8,16,256]{2,1,0:T(8,128)(2,1)S(1)}, u32[]{:S(2)}, u32[]{:S(2)}) collective-permute-start(bf16[8,16,256]{2,1,0:T(8,128)(2,1)S(1)} %get-tuple-element.436), channel_id=1, source_target_pairs={{0,8},{8,16},{16,24},{1,9},{9,17},{17,25},{2,10},{10,18},{18,26},{... | collective-permute-start | bytes 196616 | tf_op jit(solution)/shard_map/while/body/eval_jaxpr/ppermute | solution.py:25
  74.0 6.2 %collective-permute-start = (bf16[2,1,16,256]{3,2,1,0:T(8,128)(2,1)S(1)}, bf16[2,1,16,256]{3,2,1,0:T(8,128)(2,1)S(1)}, u32[]{:S(2)}, u32[]{:S(2)}) collective-permute-start(bf16[2,1,16,256]{3,2,1,0:T(8,128)(2,1)S(1)} %get-tuple-element.434), channel_id=1, source_target_pairs={{2,0},{4,2},{6,4},{3,1},{5,3},{7,5},{10,8},{12,10},{14,12},{11,9},... | collective-permute-start | bytes 49160 | tf_op jit(solution)/shard_map/while/body/eval_jaxpr/ppermute | solution.py:17
  75.3 6.3 %collective-permute-start.1 = (bf16[2,1,16,256]{3,2,1,0:T(8,128)(2,1)S(1)}, bf16[2,1,16,256]{3,2,1,0:T(8,128)(2,1)S(1)}, u32[]{:S(2)}, u32[]{:S(2)}) collective-permute-start(bf16[2,1,16,256]{3,2,1,0:T(8,128)(2,1)S(1)} %get-tuple-element.435), channel_id=1, source_target_pairs={{0,2},{2,4},{4,6},{1,3},{3,5},{5,7},{8,10},{10,12},{12,14},{9,11},... | collective-permute-start | bytes 49160 | tf_op jit(solution)/shard_map/while/body/eval_jaxpr/ppermute | solution.py:14
  81.6 1.7 copy-start
  85.3 7.4 %collective-permute-start.2 = (bf16[8,16,256]{2,1,0:T(8,128)(2,1)S(1)}, bf16[8,16,256]{2,1,0:T(8,128)(2,1)S(1)}, u32[]{:S(2)}, u32[]{:S(2)}) collective-permute-start(bf16[8,16,256]{2,1,0:T(8,128)(2,1)S(1)} %get-tuple-element.436), channel_id=1, source_target_pairs={{8,0},{16,8},{24,16},{9,1},{17,9},{25,17},{10,2},{18,10},{26,18},{... | collective-permute-start | bytes 196616 | tf_op jit(solution)/shard_map/while/body/eval_jaxpr/ppermute | solution.py:25
  86.6 7.7 %collective-permute-start.3 = (bf16[8,16,256]{2,1,0:T(8,128)(2,1)S(1)}, bf16[8,16,256]{2,1,0:T(8,128)(2,1)S(1)}, u32[]{:S(2)}, u32[]{:S(2)}) collective-permute-start(bf16[8,16,256]{2,1,0:T(8,128)(2,1)S(1)} %get-tuple-element.436), channel_id=1, source_target_pairs={{0,8},{8,16},{16,24},{1,9},{9,17},{17,25},{2,10},{10,18},{18,26},{... | collective-permute-start | bytes 196616 | tf_op jit(solution)/shard_map/while/body/eval_jaxpr/ppermute | solution.py:25
  96.1 6.2 %collective-permute-start = (bf16[2,1,16,256]{3,2,1,0:T(8,128)(2,1)S(1)}, bf16[2,1,16,256]{3,2,1,0:T(8,128)(2,1)S(1)}, u32[]{:S(2)}, u32[]{:S(2)}) collective-permute-start(bf16[2,1,16,256]{3,2,1,0:T(8,128)(2,1)S(1)} %get-tuple-element.434), channel_id=1, source_target_pairs={{2,0},{4,2},{6,4},{3,1},{5,3},{7,5},{10,8},{12,10},{14,12},{11,9},... | collective-permute-start | bytes 49160 | tf_op jit(solution)/shard_map/while/body/eval_jaxpr/ppermute | solution.py:17
  97.4 6.3 %collective-permute-start.1 = (bf16[2,1,16,256]{3,2,1,0:T(8,128)(2,1)S(1)}, bf16[2,1,16,256]{3,2,1,0:T(8,128)(2,1)S(1)}, u32[]{:S(2)}, u32[]{:S(2)}) collective-permute-start(bf16[2,1,16,256]{3,2,1,0:T(8,128)(2,1)S(1)} %get-tuple-element.435), channel_id=1, source_target_pairs={{0,2},{2,4},{4,6},{1,3},{3,5},{5,7},{8,10},{10,12},{12,14},{9,11},... | collective-permute-start | bytes 49160 | tf_op jit(solution)/shard_map/while/body/eval_jaxpr/ppermute | solution.py:14
  107.4 7.4 %collective-permute-start.2 = (bf16[8,16,256]{2,1,0:T(8,128)(2,1)S(1)}, bf16[8,16,256]{2,1,0:T(8,128)(2,1)S(1)}, u32[]{:S(2)}, u32[]{:S(2)}) collective-permute-start(bf16[8,16,256]{2,1,0:T(8,128)(2,1)S(1)} %get-tuple-element.436), channel_id=1, source_target_pairs={{8,0},{16,8},{24,16},{9,1},{17,9},{25,17},{10,2},{18,10},{26,18},{... | collective-permute-start | bytes 196616 | tf_op jit(solution)/shard_map/while/body/eval_jaxpr/ppermute | solution.py:25
  108.7 7.7 %collective-permute-start.3 = (bf16[8,16,256]{2,1,0:T(8,128)(2,1)S(1)}, bf16[8,16,256]{2,1,0:T(8,128)(2,1)S(1)}, u32[]{:S(2)}, u32[]{:S(2)}) collective-permute-start(bf16[8,16,256]{2,1,0:T(8,128)(2,1)S(1)} %get-tuple-element.436), channel_id=1, source_target_pairs={{0,8},{8,16},{16,24},{1,9},{9,17},{17,25},{2,10},{10,18},{18,26},{... | collective-permute-start | bytes 196616 | tf_op jit(solution)/shard_map/while/body/eval_jaxpr/ppermute | solution.py:25
  118.3 6.2 %collective-permute-start = (bf16[2,1,16,256]{3,2,1,0:T(8,128)(2,1)S(1)}, bf16[2,1,16,256]{3,2,1,0:T(8,128)(2,1)S(1)}, u32[]{:S(2)}, u32[]{:S(2)}) collective-permute-start(bf16[2,1,16,256]{3,2,1,0:T(8,128)(2,1)S(1)} %get-tuple-element.434), channel_id=1, source_target_pairs={{2,0},{4,2},{6,4},{3,1},{5,3},{7,5},{10,8},{12,10},{14,12},{11,9},... | collective-permute-start | bytes 49160 | tf_op jit(solution)/shard_map/while/body/eval_jaxpr/ppermute | solution.py:17
  119.6 6.3 %collective-permute-start.1 = (bf16[2,1,16,256]{3,2,1,0:T(8,128)(2,1)S(1)}, bf16[2,1,16,256]{3,2,1,0:T(8,128)(2,1)S(1)}, u32[]{:S(2)}, u32[]{:S(2)}) collective-permute-start(bf16[2,1,16,256]{3,2,1,0:T(8,128)(2,1)S(1)} %get-tuple-element.435), channel_id=1, source_target_pairs={{0,2},{2,4},{4,6},{1,3},{3,5},{5,7},{8,10},{10,12},{12,14},{9,11},... | collective-permute-start | bytes 49160 | tf_op jit(solution)/shard_map/while/body/eval_jaxpr/ppermute | solution.py:14
  129.6 7.4 %collective-permute-start.2 = (bf16[8,16,256]{2,1,0:T(8,128)(2,1)S(1)}, bf16[8,16,256]{2,1,0:T(8,128)(2,1)S(1)}, u32[]{:S(2)}, u32[]{:S(2)}) collective-permute-start(bf16[8,16,256]{2,1,0:T(8,128)(2,1)S(1)} %get-tuple-element.436), channel_id=1, source_target_pairs={{8,0},{16,8},{24,16},{9,1},{17,9},{25,17},{10,2},{18,10},{26,18},{... | collective-permute-start | bytes 196616 | tf_op jit(solution)/shard_map/while/body/eval_jaxpr/ppermute | solution.py:25
  130.8 7.7 %collective-permute-start.3 = (bf16[8,16,256]{2,1,0:T(8,128)(2,1)S(1)}, bf16[8,16,256]{2,1,0:T(8,128)(2,1)S(1)}, u32[]{:S(2)}, u32[]{:S(2)}) collective-permute-start(bf16[8,16,256]{2,1,0:T(8,128)(2,1)S(1)} %get-tuple-element.436), channel_id=1, source_target_pairs={{0,8},{8,16},{16,24},{1,9},{9,17},{17,25},{2,10},{10,18},{18,26},{... | collective-permute-start | bytes 196616 | tf_op jit(solution)/shard_map/while/body/eval_jaxpr/ppermute | solution.py:25
  140.4 6.2 %collective-permute-start = (bf16[2,1,16,256]{3,2,1,0:T(8,128)(2,1)S(1)}, bf16[2,1,16,256]{3,2,1,0:T(8,128)(2,1)S(1)}, u32[]{:S(2)}, u32[]{:S(2)}) collective-permute-start(bf16[2,1,16,256]{3,2,1,0:T(8,128)(2,1)S(1)} %get-tuple-element.434), channel_id=1, source_target_pairs={{2,0},{4,2},{6,4},{3,1},{5,3},{7,5},{10,8},{12,10},{14,12},{11,9},... | collective-permute-start | bytes 49160 | tf_op jit(solution)/shard_map/while/body/eval_jaxpr/ppermute | solution.py:17
  141.7 6.3 %collective-permute-start.1 = (bf16[2,1,16,256]{3,2,1,0:T(8,128)(2,1)S(1)}, bf16[2,1,16,256]{3,2,1,0:T(8,128)(2,1)S(1)}, u32[]{:S(2)}, u32[]{:S(2)}) collective-permute-start(bf16[2,1,16,256]{3,2,1,0:T(8,128)(2,1)S(1)} %get-tuple-element.435), channel_id=1, source_target_pairs={{0,2},{2,4},{4,6},{1,3},{3,5},{5,7},{8,10},{10,12},{12,14},{9,11},... | collective-permute-start | bytes 49160 | tf_op jit(solution)/shard_map/while/body/eval_jaxpr/ppermute | solution.py:14
  151.7 6.1 %collective-permute-start.2 = (bf16[8,16,256]{2,1,0:T(8,128)(2,1)S(1)}, bf16[8,16,256]{2,1,0:T(8,128)(2,1)S(1)}, u32[]{:S(2)}, u32[]{:S(2)}) collective-permute-start(bf16[8,16,256]{2,1,0:T(8,128)(2,1)S(1)} %get-tuple-element.436), channel_id=1, source_target_pairs={{8,0},{16,8},{24,16},{9,1},{17,9},{25,17},{10,2},{18,10},{26,18},{... | collective-permute-start | bytes 196616 | tf_op jit(solution)/shard_map/while/body/eval_jaxpr/ppermute | solution.py:25
  153.0 6.4 %collective-permute-start.3 = (bf16[8,16,256]{2,1,0:T(8,128)(2,1)S(1)}, bf16[8,16,256]{2,1,0:T(8,128)(2,1)S(1)}, u32[]{:S(2)}, u32[]{:S(2)}) collective-permute-start(bf16[8,16,256]{2,1,0:T(8,128)(2,1)S(1)} %get-tuple-element.436), channel_id=1, source_target_pairs={{0,8},{8,16},{16,24},{1,9},{9,17},{17,25},{2,10},{10,18},{18,26},{... | collective-permute-start | bytes 196616 | tf_op jit(solution)/shard_map/while/body/eval_jaxpr/ppermute | solution.py:25
  159.4 65.4 %copy-start.2 = (bf16[4,8,16,256]{3,2,1,0:T(8,128)(2,1)}, bf16[4,8,16,256]{3,2,1,0:T(8,128)(2,1)S(1)}, u32[]{:S(2)}) copy-start(bf16[4,8,16,256]{3,2,1,0:T(8,128)(2,1)S(1)} %get-tuple-element.283) | copy-start | bytes 786436
  225.2 1.6 collective-permute-start.4
  (7 other events, 10.7 us)
Sparse Core Ops, SparseCore 0:
  159.6 51.1 reduce-scatter.1
where the time goes:
time: 259 us; the launch traced here: 257 us
  starting transfers between devices  97.6 us (38%)
  waiting for transfers between devices  75.5 us (29%)
  local copies, waits for them, and re-layouts  30.8 us (12%)
  blocking collectives  24.8 us (10%)
  between operations  14.1 us (5%)
  other arithmetic  9.28 us (4%)
  matrix products  3.63 us (1%)
    ppermute x14, starting transfers between devices, from_behind(): return lax.ppermute(block, axis, route)  53.9 us
    reduce_scatter x1, waiting for transfers between devices, shards(): lax.psum_scatter(kernel_acc, 'strip', scatter_dimension=0, tiled=True)  51.3 us
    ppermute x7, starting transfers between devices, with_halo(): lax.ppermute(lax.slice_in_dim(block, block.shape[dim] - width, None, axis...  34.6 us
    ppermute x14, waiting for transfers between devices, from_behind(): return lax.ppermute(block, axis, route)  13 us
    all_to_all x1, blocking collectives, shards(): lax.all_to_all(blocks, 'section', split_axis=0, concat_axis=0, tiled=True)  12.4 us
    all_to_all x1, blocking collectives, shards(): lax.all_to_all(combined, 'section', split_axis=0, concat_axis=0, tiled=True)  12.4 us
    cond x64, local copies, waits for them, and re-layouts  10.3 us
    ppermute x7, waiting for transfers between devices, with_halo(): lax.ppermute(lax.slice_in_dim(block, block.shape[dim] - width, None, axis...  9.68 us
  transfers between devices with their start and end apart: 30, of which 23 were waited for; matrix products, arithmetic and copies ran while one was open for 0% of the time, Pallas kernels for 0%

commit v1 on v0

--- a/solution.py
+++ b/solution.py
@@ -46,7 +46,7 @@
     return stacked.reshape(height * tile_width, stacked.shape[-1])
 
 
-def shards(grad_top, acts, masks, kernels):
+def pipelined(grad_top, acts, masks, kernels):
     sections = lax.axis_size("section")
     strips = lax.axis_size("strip")
     section_id = lax.axis_index("section")
@@ -110,7 +110,7 @@
         jnp.zeros((9 * channels, channels), jnp.float32),
         jnp.zeros((micros, tile_rows, tile_width, channels), jnp.bfloat16),
     )
-    incoming, kernel_acc, results = lax.fori_loop(0, micros + sections - 1, backward, initial)
+    _, kernel_acc, results = lax.fori_loop(0, micros + sections - 1, backward, initial)
     share_rows = 9 * channels // strips
     own_share = lax.psum_scatter(kernel_acc, "strip", scatter_dimension=0, tiled=True)
     blocks = own_share.reshape(sections, share_rows * channels // sections)
@@ -125,7 +125,229 @@
     return (input_grads, kernel_grads)
 
 
+AXES = ("section", "strip", "mirror")
+
+
+def after(value, *others):
+    return lax.optimization_barrier((value, *others))[0]
+
+
+def folded(grad_top, acts, masks, kernels):
+    sections = lax.axis_size("section")
+    strips = lax.axis_size("strip")
+    half = sections // 2
+    section_id = lax.axis_index("section")
+    strip_id = lax.axis_index("strip")
+    mirror_id = lax.axis_index("mirror")
+    replica = jnp.where(section_id >= half, 0, 1)
+    major = mirror_id == replica
+    depth = jnp.where(section_id >= half, sections - 1 - section_id, section_id)
+    bf16 = jnp.bfloat16
+
+    def flat(s, z, m):
+        return (s * strips + z) * 2 + m
+
+    def is_major(s, m):
+        return m == (0 if s >= half else 1)
+
+    cells = [(s, m) for s in range(sections) for m in range(2)]
+
+    def permuted(block, target, wanted=lambda s, m: True):
+        route = []
+        for s, m in cells:
+            if wanted(s, m):
+                t, n = target(s, m)
+                route.extend((flat(s, z, m), flat(t, z, n)) for z in range(strips))
+        return lax.ppermute(block, AXES, route)
+
+    def mirrored(block):
+        return lax.ppermute(block, "mirror", [(0, 1), (1, 0)])
+
+    def partnered(block, lower):
+        return permuted(
+            block,
+            lambda s, m: (sections - 1 - s, 1 - m),
+            lambda s, m: is_major(s, m) != bool(lower),
+        )
+
+    def cored(block, lower):
+        return permuted(block, lambda s, m: (s, 1 - m), lambda s, m: is_major(s, m) == bool(lower))
+
+    def minor_to_major(block):
+        return permuted(block, lambda s, m: (sections - 1 - s, m), lambda s, m: not is_major(s, m))
+
+    def stripped(block, step, wanted=lambda s, m: True):
+        route = [
+            (flat(s, z, m), flat(s, z ^ step, m))
+            for s, m in cells
+            if wanted(s, m)
+            for z in range(strips)
+        ]
+        return lax.ppermute(block, AXES, route)
+
+    def hopped(block, position):
+        inner = [min(q, sections - 1 - q) for q in (position, position + 1)]
+        swap = {inner[0]: inner[1], inner[1]: inner[0]}
+        swap.update({sections - 1 - a: sections - 1 - b for a, b in list(swap.items())})
+        return permuted(block, lambda s, m: (swap[s], m), lambda s, m: s in swap)
+
+    even = strip_id % 2 == 0
+
+    def rims(first, last):
+        near = [(z, z + 1) for z in range(0, strips - 1, 2)]
+        far = [(z, z + 1) for z in range(1, strips - 1, 2)]
+        near, far = [pairs + [(b, a) for a, b in pairs] for pairs in (near, far)]
+        from_near = lax.ppermute(jnp.where(even, last, first), "strip", near)
+        from_far = lax.ppermute(jnp.where(even, first, last), "strip", far)
+        return jnp.where(even, from_far, from_near), jnp.where(even, from_near, from_far)
+
+    def across_strips(block):
+        return jnp.concatenate([block, stripped(block, 1)])
+
+    top_grads = grad_top[0]
+    inputs_all = acts[0, 0]
+    masks_int = masks[0, 0]
+    micros, tile_rows, tile_width, channels = inputs_all.shape
+    count = micros // 2
+    pixels = tile_rows * tile_width
+    rows = 9 * channels // strips
+
+    mine = jnp.stack([top_grads[:count], masks_int[:count].astype(bf16)])
+    theirs = jnp.stack([top_grads[count:], masks_int[count:].astype(bf16)])
+    mine = jnp.where(major, mine, mirrored(theirs))
+    low, high = rims(mine[:, :, :sections], mine[:, :, tile_rows - sections :])
+    top_ext, high_masks = jnp.concatenate([low, mine, high], axis=2)
+
+    own_kernel = jnp.transpose(kernels[0, 0], (0, 1, 3, 2)).reshape(9 * channels, channels)
+    other_kernel = mirrored(own_kernel)
+    high_kernel = jnp.where(major, own_kernel, other_kernel)
+    low_kernel = jnp.where(major, other_kernel, own_kernel)
+
+    low_all = after(jnp.stack([masks_int.astype(bf16), inputs_all]), mine)
+    moved = jnp.where(major, minor_to_major(low_all[:, :count]), partnered(low_all[:, count:], 1))
+    given_inputs = mirrored(after(inputs_all[count:], mine))
+    high_inputs = jnp.where(major, inputs_all[:count], given_inputs)
+
+    def later_rims():
+        block = jnp.concatenate([moved, high_inputs[None]])
+        first = jnp.concatenate([block[0, :, :half], block[1, :, :1], block[2, :, :1]], axis=1)
+        end = tile_rows
+        last = jnp.concatenate(
+            [block[0, :, end - half :], block[1, :, end - 1 :], block[2, :, end - 1 :]], axis=1
+        )
+        low, high = rims(first, last)
+        low_masks = jnp.concatenate([low[:, :half], block[0], high[:, :half]], axis=1)
+        low_inputs = [low[:, half : half + 1], block[1], high[:, half : half + 1]]
+        high_inputs_ext = [low[:, half + 1 :], block[2], high[:, half + 1 :]]
+        inputs = jnp.concatenate(
+            [jnp.concatenate(high_inputs_ext, axis=1), jnp.concatenate(low_inputs, axis=1)]
+        )
+        return low_masks, across_strips(inputs[None])
+
+    column, upper_strip = strip_id % 2, strip_id // 2
+
+    def unfolded(tall):
+        wide = jnp.pad(tall, ((0, 0), (0, 0), (0, 0), (1, 1), (0, 0)))
+
+        def tap(index):
+            a, b = divmod(index, 3)
+            return wide[:, :, a : a + tile_rows, b : b + tile_width]
+
+        pieces = [
+            jnp.where(column == 1, tap(first + 2), tap(first)) for first in (0, 1, 2, 4, 5, 6)
+        ]
+        joined = jnp.concatenate(pieces, axis=-1).reshape(2, 2, count * pixels, 6 * channels)
+        return joined.swapaxes(0, 1).reshape(2, 2 * count * pixels, 6 * channels)
+
+    def kept_rows(taps):
+        start = column * (channels // 4)
+        near = lax.dynamic_slice_in_dim(taps, start, rows)
+        far = lax.dynamic_slice_in_dim(taps[3 * channels :], start + channels // 2, rows)
+        return near, far
+
+    def layer_back(grad_out, mask, kernel):
+        height = grad_out.shape[0] - 2
+        grad_pre = grad_out * mask
+        padded = jnp.pad(grad_pre, ((0, 0), (1, 1), (0, 0)))
+        patch = unfold(padded, height, tile_width, True)
+        branch = jnp.dot(patch, kernel, preferred_element_type=jnp.float32)
+        grad_in = grad_out[1:-1].astype(jnp.float32) + branch.reshape(height, tile_width, channels)
+        return grad_in.astype(bf16), grad_pre
+
+    grads = [top_ext[k] for k in range(count)]
+    pres = [[None] * count for _ in range(sections)]
+    outs = [[None] * count for _ in range(sections)]
+    low_masks = inputs = None
+    for position in range(sections):
+        for k in range(count):
+            lower = position >= half
+            trim = position - half if lower else position
+            mask = (low_masks if lower else high_masks)[k]
+            mask = mask[trim : mask.shape[0] - trim]
+            kernel = low_kernel if lower else high_kernel
+            grad_in, grad_pre = layer_back(grads[k], mask, kernel)
+            rim = sections - position
+            pres[position][k] = grad_pre[rim : rim + tile_rows]
+            outs[position][k] = grad_in[rim - 1 : rim - 1 + tile_rows]
+            grads[k] = grad_in
+            if position + 1 < sections and position + 1 != half:
+                hop = hopped(grad_in, position)
+                grads[k] = hop if position else jnp.where(depth == 0, grad_in, hop)
+        if position == 0:
+            low_masks, inputs = later_rims()
+
+    def at_depth(pieces):
+        chosen = pieces[0]
+        for q in range(1, half):
+            chosen = jnp.where(depth == q, pieces[q], chosen)
+        return chosen
+
+    def side(table, lower, k):
+        return at_depth([table[sections - 1 - q if lower else q][k] for q in range(half)])
+
+    results = [jnp.stack([side(outs, lower, k) for k in range(count)]) for lower in range(2)]
+    given = mirrored(jnp.where(major, results[1], results[0]))
+    kept = jnp.concatenate([results[0], given])
+    returned = partnered(jnp.concatenate([given, results[1]]), 1)
+    input_grads = jnp.where(major, kept, returned)
+
+    patches = unfolded(inputs)
+    sums = []
+    for lower in range(2):
+        holds = lambda s, m: is_major(s, m) != bool(lower)
+        block = jnp.stack([side(pres, lower, k) for k in range(count)])[None]
+        own = lax.dot_general(
+            patches[lower],
+            across_strips(block).reshape(-1, channels),
+            (((0,), (0,)), ((), ())),
+            preferred_element_type=jnp.float32,
+        )
+        own = jnp.stack(kept_rows(own))
+        own = own + cored(own.astype(bf16), lower).astype(jnp.float32)
+        other = jnp.where(upper_strip == 0, own[1], own[0]).astype(bf16)
+        own = jnp.where(upper_strip == 0, own[0], own[1])
+        own = own + stripped(other, 2, holds).astype(jnp.float32)
+        sums.append(own + partnered(own.astype(bf16), lower).astype(jnp.float32))
+    factor = 1.0 / math.sqrt(2.0 * micros * tile_rows * strips * tile_width)
+    kernel_grads = jnp.where(major, sums[0], sums[1]) * factor
+    return (input_grads[None, None], kernel_grads[None, None])
+
+
+def shards(grad_top, acts, masks, kernels):
+    sections = lax.axis_size("section")
+    strips = lax.axis_size("strip")
+    tile_rows, channels = acts.shape[3], acts.shape[5]
+    paired = sections % 2 == 0 and acts.shape[2] % 2 == 0 and strips == 4
+    if paired and sections <= tile_rows and 9 * channels % strips == 0:
+        return folded(grad_top, acts, masks, kernels)
+    return pipelined(grad_top, acts, masks, kernels)
+
+
 def solution(mesh):
+    return mapped(mesh)
+
+
+def mapped(mesh):
     return jax.shard_map(
         shards,
         mesh=mesh,

time: 259 us -> 97.4 us (0.38)
  starting transfers between devices: 97.6 us -> 41.5 us
  waiting for transfers between devices: 75.5 us -> 38.6 us
  local copies, waits for them, and re-layouts: 30.8 us -> 2.75 us
  blocking collectives: 24.8 us -> 0 us
  between operations: 14.1 us -> 1.88 us
    ppermute x29 -> x24, starting transfers between devices: 97.6 us -> 41.5 us  [the longest x11 20.9 us: permuted(): return lax.ppermute(block, AXES, route)]
    reduce_scatter x1 -> x0, waiting for transfers between devices: 51.3 us -> none  [shards(): lax.psum_scatter(kernel_acc, 'strip', scatter_dimension=0, tiled=True)]
    all_to_all x2 -> x0, blocking collectives: 24.8 us -> none  [the longest x1 12.4 us: shards(): lax.all_to_all(blocks, 'section', split_axis=0, concat_axis=0, tiled=True)]
    ppermute x29 -> x24, waiting for transfers between devices: 24.2 us -> 38.6 us  [the longest x11 20.3 us: permuted(): return lax.ppermute(block, AXES, route)]
    cond x64 -> x0, local copies, waits for them, and re-layouts: 10.3 us -> none
    rev x1 -> x0, local copies, waits for them, and re-layouts: 7.12 us -> none  [shards(): combined = spread + jnp.flip(across, 0)]
    dynamic_slice x14 -> x0, local copies, waits for them, and re-layouts: 6.04 us -> none  [the longest x7 5.94 us: backward(): inputs = lax.dynamic_index_in_dim(inputs_all, clipped, 0, keepdims=False)]
    another operation x7 -> x9, other arithmetic: 6.58 us -> 2.09 us  [backward(): rimmed = with_halo(jnp.stack([grad_pre, inputs]), (('strip', 1),), 1)]
  transfers between devices with their start and end apart: 30 -> 24, of which waited for: 23 -> 13; matrix products, arithmetic and copies ran while one was open for 0% -> 10% of each run, Pallas kernels for 0% -> 0%
where the time goes in v1:
time: 97.4 us; the launch traced here: 97 us
  starting transfers between devices  41.5 us (43%)
  waiting for transfers between devices  38.6 us (40%)
  other arithmetic  8.02 us (8%)
  matrix products  4.32 us (4%)
  local copies, waits for them, and re-layouts  2.75 us (3%)
  between operations  1.88 us (2%)
    ppermute x11, starting transfers between devices, permuted(): return lax.ppermute(block, AXES, route)  20.9 us
    ppermute x11, waiting for transfers between devices, permuted(): return lax.ppermute(block, AXES, route)  20.3 us
    ppermute x5, waiting for transfers between devices, stripped(): return lax.ppermute(block, AXES, route)  15.1 us
    ppermute x5, starting transfers between devices, stripped(): return lax.ppermute(block, AXES, route)  9.03 us
    ppermute x2, starting transfers between devices, rims(): from_near = lax.ppermute(jnp.where(even, last, first), 'strip', near)  8.38 us
    dot_general x8, matrix products, layer_back(): branch = jnp.dot(patch, kernel, preferred_element_type=jnp.float32)  3.09 us
    ppermute x2, waiting for transfers between devices, rims(): from_near = lax.ppermute(jnp.where(even, last, first), 'strip', near)  2.68 us
  transfers between devices with their start and end apart: 24, of which 13 were waited for; matrix products, arithmetic and copies ran while one was open for 10% of the time, Pallas kernels for 0%

profile of v1, /device:TPU:0, one launch (start us, length us, event | category | flops | bytes accessed | tf_op | source)
XLA Modules:
  0.0 97.0 jit_solution(14754791452178976268)
XLA Ops:
  0.6 1.2 %copy_convert_fusion = bf16[1,1,4,8,16,256]{5,4,2,3,1,0:T(8,128)(2,1)S(1)} fusion(s32[1,1,4,8,16,256]{5,4,3,2,1,0:T(8,128)} %param.6), kind=kLoop, calls=%fused_computation.67 | loop fusion | flops 131072 | bytes 786432 | tf_op jit(solution)/shard_map/convert.3
  1.9 0.7 pad_maximum_fusion.5
  3.1 0.7 copy.25
  4.6 1.0 %maximum_select_fusion = bf16[2,2,8,16,256]{4,3,1,2,0:T(8,128)(2,1)S(1)} fusion(bf16[2,2,8,16,256]{4,3,1,2,0:T(8,128)(2,1)} %collective-permute-done, bf16[1,2,8,16,256]{4,3,1,2,0:T(8,128)(2,1)S(1)} %get-tuple-element.36, pred[]{:T(512)S(6)} %eq.15, bf16[1,2,8,16,256]{4,3,2,1,0:T(8,128)(2,1)S(1)} %get-tuple-element.34), kind=kLoop, calls=%fused_computation.73 | loop fusion | flops 655360 | bytes 786433 | tf_op jit(solution)/shard_map/jit(_where)/select_n | solution.py:217
  6.5 5.8 %collective-permute-start.2 = (bf16[2,2,4,16,256]{4,3,1,2,0:T(8,128)(2,1)S(1)}, bf16[2,2,4,16,256]{4,3,1,2,0:T(8,128)(2,1)S(1)}, u32[]{:S(2)}, u32[]{:S(2)}) collective-permute-start(bf16[2,2,4,16,256]{4,3,1,2,0:T(8,128)(2,1)S(1)} %get-tuple-element.29), channel_id=1, source_target_pairs={{0,2},{4,6},{2,0},{6,4},{1,3},{5,7},{3,1},{7,5},{8,10},{12,14},{10... | collective-permute-start | bytes 393224 | tf_op jit(solution)/shard_map/ppermute | solution.py:200
  12.3 4.5 %collective-permute-start.6 = (bf16[2,2,8,16,256]{4,3,1,2,0:T(8,128)(2,1)S(1)}, bf16[2,2,8,16,256]{4,3,1,2,0:T(8,128)(2,1)S(1)}, u32[]{:S(2)}, u32[]{:S(2)}) collective-permute-start(bf16[2,2,8,16,256]{4,3,1,2,0:T(8,128)(2,1)S(1)} %get-tuple-element.23), channel_id=1, source_target_pairs={{0,24},{2,26},{4,28},{6,30},{8,16},{10,18},{12,20},{14,22},{17,9},... | collective-permute-start | bytes 786440 | tf_op jit(solution)/shard_map/ppermute | solution.py:161
  16.8 1.9 %collective-permute-start.7 = (bf16[2,2,8,16,256]{4,3,1,2,0:T(8,128)(2,1)S(1)}, bf16[2,2,8,16,256]{4,3,1,2,0:T(8,128)(2,1)S(1)}, u32[]{:S(2)}, u32[]{:S(2)}) collective-permute-start(bf16[2,2,8,16,256]{4,3,1,2,0:T(8,128)(2,1)S(1)} %get-tuple-element.22), channel_id=1, source_target_pairs={{0,25},{2,27},{4,29},{6,31},{8,17},{10,19},{12,21},{14,23},{17,8},... | collective-permute-start | bytes 786440 | tf_op jit(solution)/shard_map/ppermute | solution.py:161
  19.5 1.2 %collective-permute-done.6 = bf16[2,2,8,16,256]{4,3,1,2,0:T(8,128)(2,1)S(1)} collective-permute-done((bf16[2,2,8,16,256]{4,3,1,2,0:T(8,128)(2,1)S(1)}, bf16[2,2,8,16,256]{4,3,1,2,0:T(8,128)(2,1)S(1)}, u32[]{:S(2)}, u32[]{:S(2)}) %collective-permute-start.6) | collective-permute-done | bytes 262176 | tf_op jit(solution)/shard_map/ppermute | solution.py:161
  20.7 4.7 %collective-permute-done.7 = bf16[2,2,8,16,256]{4,3,1,2,0:T(8,128)(2,1)S(1)} collective-permute-done((bf16[2,2,8,16,256]{4,3,1,2,0:T(8,128)(2,1)S(1)}, bf16[2,2,8,16,256]{4,3,1,2,0:T(8,128)(2,1)S(1)}, u32[]{:S(2)}, u32[]{:S(2)}) %collective-permute-start.7) | collective-permute-done | bytes 262176 | tf_op jit(solution)/shard_map/ppermute | solution.py:161
  26.2 2.6 %collective-permute-start.10 = (bf16[2,4,16,256]{3,2,1,0:T(8,128)(2,1)S(1)}, bf16[2,4,16,256]{3,2,1,0:T(8,128)(2,1)S(1)}, u32[]{:S(2)}, u32[]{:S(2)}) collective-permute-start(bf16[2,4,16,256]{3,2,1,0:T(8,128)(2,1)S(1)} %get-tuple-element.45), channel_id=1, source_target_pairs={{0,2},{4,6},{2,0},{6,4},{1,3},{5,7},{3,1},{7,5},{8,10},{12,14},{10... | collective-permute-start | bytes 196616 | tf_op jit(solution)/shard_map/ppermute | solution.py:200
  28.8 2.7 %collective-permute-done.10 = bf16[2,4,16,256]{3,2,1,0:T(8,128)(2,1)S(1)} collective-permute-done((bf16[2,4,16,256]{3,2,1,0:T(8,128)(2,1)S(1)}, bf16[2,4,16,256]{3,2,1,0:T(8,128)(2,1)S(1)}, u32[]{:S(2)}, u32[]{:S(2)}) %collective-permute-start.10) | collective-permute-done | bytes 65568 | tf_op jit(solution)/shard_map/ppermute | solution.py:200
  31.5 1.6 %collective-permute-start.15 = (bf16[1,4,10,16,256]{4,3,2,1,0:T(8,128)(2,1)S(1)}, bf16[1,4,10,16,256]{4,3,2,1,0:T(8,128)(2,1)S(1)}, u32[]{:S(2)}, u32[]{:S(2)}) collective-permute-start(bf16[1,4,10,16,256]{4,3,2,1,0:T(8,128)(2,1)S(1)} %maximum_bitcast_fusion), channel_id=1, source_target_pairs={{0,2},{2,0},{4,6},{6,4},{1,3},{3,1},{5,7},{7,5},{8,10},{10,8},{12,... | collective-permute-start | bytes 983048 | tf_op jit(solution)/shard_map/ppermute | solution.py:186
  33.2 5.4 %collective-permute-done.15 = bf16[1,4,10,16,256]{4,3,2,1,0:T(8,128)(2,1)S(1)} collective-permute-done((bf16[1,4,10,16,256]{4,3,2,1,0:T(8,128)(2,1)S(1)}, bf16[1,4,10,16,256]{4,3,2,1,0:T(8,128)(2,1)S(1)}, u32[]{:S(2)}, u32[]{:S(2)}) %collective-permute-start.15) | collective-permute-done | bytes 327712 | tf_op jit(solution)/shard_map/ppermute | solution.py:186
  41.0 1.6 %collective-permute-start.4 = (bf16[14,16,256]{2,1,0:T(8,128)(2,1)S(1)}, bf16[14,16,256]{2,1,0:T(8,128)(2,1)S(1)}, u32[]{:S(2)}, u32[]{:S(2)}) collective-permute-start(bf16[14,16,256]{2,1,0:T(8,128)(2,1)S(1)} %fusion.25), channel_id=1, source_target_pairs={{0,8},{2,10},{4,12},{6,14},{1,9},{3,11},{5,13},{7,15},{8,0},{10,2}... | collective-permute-start | bytes 344072 | tf_op jit(solution)/shard_map/ppermute | solution.py:161
  43.8 2.6 %collective-permute-done.4 = bf16[14,16,256]{2,1,0:T(8,128)(2,1)S(1)} collective-permute-done((bf16[14,16,256]{2,1,0:T(8,128)(2,1)S(1)}, bf16[14,16,256]{2,1,0:T(8,128)(2,1)S(1)}, u32[]{:S(2)}, u32[]{:S(2)}) %collective-permute-start.4) | collective-permute-done | bytes 114720 | tf_op jit(solution)/shard_map/ppermute | solution.py:161
  46.4 1.6 %collective-permute-done.5 = bf16[14,16,256]{2,1,0:T(8,128)(2,1)S(1)} collective-permute-done((bf16[14,16,256]{2,1,0:T(8,128)(2,1)S(1)}, bf16[14,16,256]{2,1,0:T(8,128)(2,1)S(1)}, u32[]{:S(2)}, u32[]{:S(2)}) %collective-permute-start.5) | collective-permute-done | bytes 114720 | tf_op jit(solution)/shard_map/ppermute | solution.py:161
  50.1 1.5 %collective-permute-start.12 = (bf16[10,16,256]{2,1,0:T(8,128)(2,1)S(1)}, bf16[10,16,256]{2,1,0:T(8,128)(2,1)S(1)}, u32[]{:S(2)}, u32[]{:S(2)}) collective-permute-start(bf16[10,16,256]{2,1,0:T(8,128)(2,1)S(1)} %fusion.34), channel_id=1, source_target_pairs={{0,8},{2,10},{4,12},{6,14},{1,9},{3,11},{5,13},{7,15},{8,0},{10,2}... | collective-permute-start | bytes 245768 | tf_op jit(solution)/shard_map/ppermute | solution.py:161
  52.9 1.6 %collective-permute-start.16 = (bf16[1,2,8,16,256]{4,3,2,1,0:T(8,128)(2,1)S(1)}, bf16[1,2,8,16,256]{4,3,2,1,0:T(8,128)(2,1)S(1)}, u32[]{:S(2)}, u32[]{:S(2)}) collective-permute-start(bf16[1,2,8,16,256]{4,3,2,1,0:T(8,128)(2,1)S(1)} %maximum_bitcast_fusion.1), channel_id=1, source_target_pairs={{0,2},{2,0},{4,6},{6,4},{1,3},{3,1},{5,7},{7,5},{8,10},{10,8},{12,... | collective-permute-start | bytes 393224 | tf_op jit(solution)/shard_map/ppermute | solution.py:186
  54.6 2.1 %collective-permute-done.11 = bf16[10,16,256]{2,1,0:T(8,128)(2,1)S(1)} collective-permute-done((bf16[10,16,256]{2,1,0:T(8,128)(2,1)S(1)}, bf16[10,16,256]{2,1,0:T(8,128)(2,1)S(1)}, u32[]{:S(2)}, u32[]{:S(2)}) %collective-permute-start.11) | collective-permute-done | bytes 81952 | tf_op jit(solution)/shard_map/ppermute | solution.py:161
  57.2 1.1 %collective-permute-start.20 = (bf16[1,2,8,16,256]{4,3,2,1,0:T(8,128)(2,1)S(1)}, bf16[1,2,8,16,256]{4,3,2,1,0:T(8,128)(2,1)S(1)}, u32[]{:S(2)}, u32[]{:S(2)}) collective-permute-start(bf16[1,2,8,16,256]{4,3,2,1,0:T(8,128)(2,1)S(1)} %maximum_bitcast_fusion.2), channel_id=1, source_target_pairs={{0,2},{2,0},{4,6},{6,4},{1,3},{3,1},{5,7},{7,5},{8,10},{10,8},{12,... | collective-permute-start | bytes 393224 | tf_op jit(solution)/shard_map/ppermute | solution.py:186
  59.9 1.3 %collective-permute-start.17 = (bf16[2,576,256]{2,1,0:T(8,128)(2,1)S(1)}, bf16[2,576,256]{2,1,0:T(8,128)(2,1)S(1)}, u32[]{:S(2)}, u32[]{:S(2)}) collective-permute-start(bf16[2,576,256]{2,1,0:T(8,128)(2,1)S(1)} %fusion.41), channel_id=1, source_target_pairs={{0,1},{2,3},{4,5},{6,7},{8,9},{10,11},{12,13},{14,15},{17,16},{19,... | collective-permute-start | bytes 1769480 | tf_op jit(solution)/shard_map/ppermute | solution.py:161
  61.2 1.0 collective-permute-done.20
  63.1 1.3 %collective-permute-start.21 = (bf16[2,576,256]{2,1,0:T(8,128)(2,1)S(1)}, bf16[2,576,256]{2,1,0:T(8,128)(2,1)S(1)}, u32[]{:S(2)}, u32[]{:S(2)}) collective-permute-start(bf16[2,576,256]{2,1,0:T(8,128)(2,1)S(1)} %fusion.40), channel_id=1, source_target_pairs={{1,0},{3,2},{5,4},{7,6},{9,8},{11,10},{13,12},{15,14},{16,17},{18,... | collective-permute-start | bytes 1769480 | tf_op jit(solution)/shard_map/ppermute | solution.py:161
  64.4 1.2 %collective-permute-start.13 = (bf16[2,8,16,256]{3,2,1,0:T(8,128)(2,1)S(1)}, bf16[2,8,16,256]{3,2,1,0:T(8,128)(2,1)S(1)}, u32[]{:S(2)}, u32[]{:S(2)}) collective-permute-start(bf16[2,8,16,256]{3,2,1,0:T(8,128)(2,1)S(1)} %maximum_select_fusion.2), channel_id=1, source_target_pairs={{0,1},{1,0},{2,3},{3,2},{4,5},{5,4},{6,7},{7,6},{8,9},{9,8},{10,11... | collective-permute-start | bytes 393224 | tf_op jit(solution)/shard_map/ppermute | solution.py:164
  65.9 0.7 collective-permute-start.18
  67.2 4.0 %collective-permute-start.22 = (bf16[576,256]{1,0:T(8,128)(2,1)S(1)}, bf16[576,256]{1,0:T(8,128)(2,1)S(1)}, u32[]{:S(2)}, u32[]{:S(2)}) collective-permute-start(bf16[576,256]{1,0:T(8,128)(2,1)S(1)} %fusion.54), channel_id=1, source_target_pairs={{0,4},{2,6},{4,0},{6,2},{8,12},{10,14},{12,8},{14,10},{17,21},{19,... | collective-permute-start | bytes 884744 | tf_op jit(solution)/shard_map/ppermute | solution.py:186
  71.3 3.0 %collective-permute-start.14 = (bf16[4,8,16,256]{3,2,1,0:T(8,128)(2,1)S(1)}, bf16[4,8,16,256]{3,2,1,0:T(8,128)(2,1)S(1)}, u32[]{:S(2)}, u32[]{:S(2)}) collective-permute-start(bf16[4,8,16,256]{3,2,1,0:T(8,128)(2,1)S(1)} %pad_maximum_fusion.6), channel_id=1, source_target_pairs={{0,25},{2,27},{4,29},{6,31},{8,17},{10,19},{12,21},{14,23},{17,8},... | collective-permute-start | bytes 786440 | tf_op jit(solution)/shard_map/ppermute | solution.py:161
  75.2 8.7 %collective-permute-done.22 = bf16[576,256]{1,0:T(8,128)(2,1)S(1)} collective-permute-done((bf16[576,256]{1,0:T(8,128)(2,1)S(1)}, bf16[576,256]{1,0:T(8,128)(2,1)S(1)}, u32[]{:S(2)}, u32[]{:S(2)}) %collective-permute-start.22) | collective-permute-done | bytes 294944 | tf_op jit(solution)/shard_map/ppermute | solution.py:186
  84.0 3.8 %collective-permute-start.23 = (bf16[576,256]{1,0:T(8,128)(2,1)S(1)}, bf16[576,256]{1,0:T(8,128)(2,1)S(1)}, u32[]{:S(2)}, u32[]{:S(2)}) collective-permute-start(bf16[576,256]{1,0:T(8,128)(2,1)S(1)} %fusion.77), channel_id=1, source_target_pairs={{0,25},{2,27},{4,29},{6,31},{8,17},{10,19},{12,21},{14,23},{17,8},... | collective-permute-start | bytes 884744 | tf_op jit(solution)/shard_map/ppermute | solution.py:161
  87.8 0.8 fusion.55
  88.6 7.4 %collective-permute-done.23 = bf16[576,256]{1,0:T(8,128)(2,1)S(1)} collective-permute-done((bf16[576,256]{1,0:T(8,128)(2,1)S(1)}, bf16[576,256]{1,0:T(8,128)(2,1)S(1)}, u32[]{:S(2)}, u32[]{:S(2)}) %collective-permute-start.23) | collective-permute-done | bytes 294944 | tf_op jit(solution)/shard_map/ppermute | solution.py:161
  96.0 1.0 %multiply_bitcast_fusion = f32[1,1,576,256]{3,2,1,0:T(8,128)} fusion(bf16[576,256]{1,0:T(8,128)(2,1)S(1)} %collective-permute-done.23, bf16[576,256]{1,0:T(8,128)(2,1)S(1)} %collective-permute-done.19, pred[]{:T(512)S(6)} %eq.15, bf16[576,256]{1,0:T(8,128)(2,1)S(1)} %collective-permute-done.18, f32[2,576,256]{2,1,0:T(8,128)S(1)} %convert_add_fusion.1, ...), kind=kLoop, calls=%fused_computation.47 | loop fusion | flops 1769472 | bytes 4128770 | tf_op jit(solution)/shard_map/broadcast_in_dim | solution.py:333
  (170 shorter events, 14.7 us)
Async XLA Ops:
  0.6 1.2 %copy-start.3 = (bf16[1,4,8,16,256]{4,3,2,1,0:T(8,128)(2,1)S(1)}, bf16[1,4,8,16,256]{4,3,2,1,0:T(8,128)(2,1)}, u32[]{:S(2)}) copy-start(bf16[1,4,8,16,256]{4,3,2,1,0:T(8,128)(2,1)} %param.4) | copy-start | bytes 786436
  0.6 2.5 %copy-start.1 = (bf16[1,1,3,3,256,256]{5,4,3,2,1,0:T(8,128)(2,1)S(1)}, bf16[1,1,3,3,256,256]{5,4,3,2,1,0:T(8,128)(2,1)}, u32[]{:S(2)}) copy-start(bf16[1,1,3,3,256,256]{5,4,3,2,1,0:T(8,128)(2,1)} %param.7) | copy-start | bytes 3538948
  2.6 1.3 %copy-start = (s32[1,1,4,8,16,256]{5,4,3,2,1,0:T(8,128)S(1)}, s32[1,1,4,8,16,256]{5,4,3,2,1,0:T(8,128)}, u32[]{:S(2)}) copy-start(s32[1,1,4,8,16,256]{5,4,3,2,1,0:T(8,128)} %param.6) | copy-start | bytes 1572868
  2.6 1.4 %copy-start.2 = (bf16[1,1,4,8,16,256]{5,4,3,2,1,0:T(8,128)(2,1)S(1)}, bf16[1,1,4,8,16,256]{5,4,3,2,1,0:T(8,128)(2,1)}, u32[]{:S(2)}) copy-start(bf16[1,1,4,8,16,256]{5,4,3,2,1,0:T(8,128)(2,1)} %param.5) | copy-start | bytes 786436
  2.6 2.0 %collective-permute-start = (bf16[2,2,8,16,256]{4,3,1,2,0:T(8,128)(2,1)}, bf16[2,2,8,16,256]{4,3,1,2,0:T(8,128)(2,1)}, u32[]{:S(2)}, u32[]{:S(2)}) collective-permute-start(bf16[2,2,8,16,256]{4,3,1,2,0:T(8,128)(2,1)} %pad_maximum_fusion.5), channel_id=1, source_target_pairs={{0,1},{1,0},{2,3},{3,2},{4,5},{5,4},{6,7},{7,6},{8,9},{9,8},{10,11... | collective-permute-start | bytes 786440 | tf_op jit(solution)/shard_map/ppermute | solution.py:164
  3.9 36.4 %collective-permute-start.3 = (bf16[2304,256]{1,0:T(8,128)(2,1)S(1)}, bf16[2304,256]{1,0:T(8,128)(2,1)S(1)}, u32[]{:S(2)}, u32[]{:S(2)}) collective-permute-start(bf16[2304,256]{1,0:T(8,128)(2,1)S(1)} %bitcast.262), channel_id=1, source_target_pairs={{0,1},{1,0},{2,3},{3,2},{4,5},{5,4},{6,7},{7,6},{8,9},{9,8},{10,11... | collective-permute-start | bytes 3538952 | tf_op jit(solution)/shard_map/ppermute | solution.py:164
  5.7 13.7 %collective-permute-start.8 = (bf16[2,8,16,256]{3,2,1,0:T(8,128)(2,1)S(1)}, bf16[2,8,16,256]{3,2,1,0:T(8,128)(2,1)S(1)}, u32[]{:S(2)}, u32[]{:S(2)}) collective-permute-start(bf16[2,8,16,256]{3,2,1,0:T(8,128)(2,1)S(1)} %slice_bitcast_fusion.8), channel_id=1, source_target_pairs={{0,1},{1,0},{2,3},{3,2},{4,5},{5,4},{6,7},{7,6},{8,9},{9,8},{10,11... | collective-permute-start | bytes 393224 | tf_op jit(solution)/shard_map/ppermute | solution.py:164
  5.8 11.0 %collective-permute-start.1 = (bf16[2,2,4,16,256]{4,3,1,2,0:T(8,128)(2,1)S(1)}, bf16[2,2,4,16,256]{4,3,1,2,0:T(8,128)(2,1)S(1)}, u32[]{:S(2)}, u32[]{:S(2)}) collective-permute-start(bf16[2,2,4,16,256]{4,3,1,2,0:T(8,128)(2,1)S(1)} %get-tuple-element.28), channel_id=1, source_target_pairs={{2,4},{4,2},{3,5},{5,3},{10,12},{12,10},{11,13},{13,11},{18,20},{2... | collective-permute-start | bytes 393224 | tf_op jit(solution)/shard_map/ppermute | solution.py:201
  6.5 12.3 %collective-permute-start.2 = (bf16[2,2,4,16,256]{4,3,1,2,0:T(8,128)(2,1)S(1)}, bf16[2,2,4,16,256]{4,3,1,2,0:T(8,128)(2,1)S(1)}, u32[]{:S(2)}, u32[]{:S(2)}) collective-permute-start(bf16[2,2,4,16,256]{4,3,1,2,0:T(8,128)(2,1)S(1)} %get-tuple-element.29), channel_id=1, source_target_pairs={{0,2},{4,6},{2,0},{6,4},{1,3},{5,7},{3,1},{7,5},{8,10},{12,14},{10... | collective-permute-start | bytes 393224 | tf_op jit(solution)/shard_map/ppermute | solution.py:200
  12.3 8.3 %collective-permute-start.6 = (bf16[2,2,8,16,256]{4,3,1,2,0:T(8,128)(2,1)S(1)}, bf16[2,2,8,16,256]{4,3,1,2,0:T(8,128)(2,1)S(1)}, u32[]{:S(2)}, u32[]{:S(2)}) collective-permute-start(bf16[2,2,8,16,256]{4,3,1,2,0:T(8,128)(2,1)S(1)} %get-tuple-element.23), channel_id=1, source_target_pairs={{0,24},{2,26},{4,28},{6,30},{8,16},{10,18},{12,20},{14,22},{17,9},... | collective-permute-start | bytes 786440 | tf_op jit(solution)/shard_map/ppermute | solution.py:161
  16.8 8.6 %collective-permute-start.7 = (bf16[2,2,8,16,256]{4,3,1,2,0:T(8,128)(2,1)S(1)}, bf16[2,2,8,16,256]{4,3,1,2,0:T(8,128)(2,1)S(1)}, u32[]{:S(2)}, u32[]{:S(2)}) collective-permute-start(bf16[2,2,8,16,256]{4,3,1,2,0:T(8,128)(2,1)S(1)} %get-tuple-element.22), channel_id=1, source_target_pairs={{0,25},{2,27},{4,29},{6,31},{8,17},{10,19},{12,21},{14,23},{17,8},... | collective-permute-start | bytes 786440 | tf_op jit(solution)/shard_map/ppermute | solution.py:161
  25.5 3.3 %collective-permute-start.9 = (bf16[2,4,16,256]{3,2,1,0:T(8,128)(2,1)S(1)}, bf16[2,4,16,256]{3,2,1,0:T(8,128)(2,1)S(1)}, u32[]{:S(2)}, u32[]{:S(2)}) collective-permute-start(bf16[2,4,16,256]{3,2,1,0:T(8,128)(2,1)S(1)} %get-tuple-element.44), channel_id=1, source_target_pairs={{2,4},{4,2},{3,5},{5,3},{10,12},{12,10},{11,13},{13,11},{18,20},{2... | collective-permute-start | bytes 196616 | tf_op jit(solution)/shard_map/ppermute | solution.py:201
  26.2 5.3 %collective-permute-start.10 = (bf16[2,4,16,256]{3,2,1,0:T(8,128)(2,1)S(1)}, bf16[2,4,16,256]{3,2,1,0:T(8,128)(2,1)S(1)}, u32[]{:S(2)}, u32[]{:S(2)}) collective-permute-start(bf16[2,4,16,256]{3,2,1,0:T(8,128)(2,1)S(1)} %get-tuple-element.45), channel_id=1, source_target_pairs={{0,2},{4,6},{2,0},{6,4},{1,3},{5,7},{3,1},{7,5},{8,10},{12,14},{10... | collective-permute-start | bytes 196616 | tf_op jit(solution)/shard_map/ppermute | solution.py:200
  31.5 7.1 %collective-permute-start.15 = (bf16[1,4,10,16,256]{4,3,2,1,0:T(8,128)(2,1)S(1)}, bf16[1,4,10,16,256]{4,3,2,1,0:T(8,128)(2,1)S(1)}, u32[]{:S(2)}, u32[]{:S(2)}) collective-permute-start(bf16[1,4,10,16,256]{4,3,2,1,0:T(8,128)(2,1)S(1)} %maximum_bitcast_fusion), channel_id=1, source_target_pairs={{0,2},{2,0},{4,6},{6,4},{1,3},{3,1},{5,7},{7,5},{8,10},{10,8},{12,... | collective-permute-start | bytes 983048 | tf_op jit(solution)/shard_map/ppermute | solution.py:186
  41.0 5.4 %collective-permute-start.4 = (bf16[14,16,256]{2,1,0:T(8,128)(2,1)S(1)}, bf16[14,16,256]{2,1,0:T(8,128)(2,1)S(1)}, u32[]{:S(2)}, u32[]{:S(2)}) collective-permute-start(bf16[14,16,256]{2,1,0:T(8,128)(2,1)S(1)} %fusion.25), channel_id=1, source_target_pairs={{0,8},{2,10},{4,12},{6,14},{1,9},{3,11},{5,13},{7,15},{8,0},{10,2}... | collective-permute-start | bytes 344072 | tf_op jit(solution)/shard_map/ppermute | solution.py:161
  43.0 5.0 %collective-permute-start.5 = (bf16[14,16,256]{2,1,0:T(8,128)(2,1)S(1)}, bf16[14,16,256]{2,1,0:T(8,128)(2,1)S(1)}, u32[]{:S(2)}, u32[]{:S(2)}) collective-permute-start(bf16[14,16,256]{2,1,0:T(8,128)(2,1)S(1)} %fusion.22), channel_id=1, source_target_pairs={{0,8},{2,10},{4,12},{6,14},{1,9},{3,11},{5,13},{7,15},{8,0},{10,2}... | collective-permute-start | bytes 344072 | tf_op jit(solution)/shard_map/ppermute | solution.py:161
  50.1 4.5 %collective-permute-start.12 = (bf16[10,16,256]{2,1,0:T(8,128)(2,1)S(1)}, bf16[10,16,256]{2,1,0:T(8,128)(2,1)S(1)}, u32[]{:S(2)}, u32[]{:S(2)}) collective-permute-start(bf16[10,16,256]{2,1,0:T(8,128)(2,1)S(1)} %fusion.34), channel_id=1, source_target_pairs={{0,8},{2,10},{4,12},{6,14},{1,9},{3,11},{5,13},{7,15},{8,0},{10,2}... | collective-permute-start | bytes 245768 | tf_op jit(solution)/shard_map/ppermute | solution.py:161
  52.2 4.5 %collective-permute-start.11 = (bf16[10,16,256]{2,1,0:T(8,128)(2,1)S(1)}, bf16[10,16,256]{2,1,0:T(8,128)(2,1)S(1)}, u32[]{:S(2)}, u32[]{:S(2)}) collective-permute-start(bf16[10,16,256]{2,1,0:T(8,128)(2,1)S(1)} %fusion.37), channel_id=1, source_target_pairs={{0,8},{2,10},{4,12},{6,14},{1,9},{3,11},{5,13},{7,15},{8,0},{10,2}... | collective-permute-start | bytes 245768 | tf_op jit(solution)/shard_map/ppermute | solution.py:161
  52.9 6.1 %collective-permute-start.16 = (bf16[1,2,8,16,256]{4,3,2,1,0:T(8,128)(2,1)S(1)}, bf16[1,2,8,16,256]{4,3,2,1,0:T(8,128)(2,1)S(1)}, u32[]{:S(2)}, u32[]{:S(2)}) collective-permute-start(bf16[1,2,8,16,256]{4,3,2,1,0:T(8,128)(2,1)S(1)} %maximum_bitcast_fusion.1), channel_id=1, source_target_pairs={{0,2},{2,0},{4,6},{6,4},{1,3},{3,1},{5,7},{7,5},{8,10},{10,8},{12,... | collective-permute-start | bytes 393224 | tf_op jit(solution)/shard_map/ppermute | solution.py:186
  57.2 5.0 %collective-permute-start.20 = (bf16[1,2,8,16,256]{4,3,2,1,0:T(8,128)(2,1)S(1)}, bf16[1,2,8,16,256]{4,3,2,1,0:T(8,128)(2,1)S(1)}, u32[]{:S(2)}, u32[]{:S(2)}) collective-permute-start(bf16[1,2,8,16,256]{4,3,2,1,0:T(8,128)(2,1)S(1)} %maximum_bitcast_fusion.2), channel_id=1, source_target_pairs={{0,2},{2,0},{4,6},{6,4},{1,3},{3,1},{5,7},{7,5},{8,10},{10,8},{12,... | collective-permute-start | bytes 393224 | tf_op jit(solution)/shard_map/ppermute | solution.py:186
  59.9 5.8 %collective-permute-start.17 = (bf16[2,576,256]{2,1,0:T(8,128)(2,1)S(1)}, bf16[2,576,256]{2,1,0:T(8,128)(2,1)S(1)}, u32[]{:S(2)}, u32[]{:S(2)}) collective-permute-start(bf16[2,576,256]{2,1,0:T(8,128)(2,1)S(1)} %fusion.41), channel_id=1, source_target_pairs={{0,1},{2,3},{4,5},{6,7},{8,9},{10,11},{12,13},{14,15},{17,16},{19,... | collective-permute-start | bytes 1769480 | tf_op jit(solution)/shard_map/ppermute | solution.py:161
  63.1 3.9 %collective-permute-start.21 = (bf16[2,576,256]{2,1,0:T(8,128)(2,1)S(1)}, bf16[2,576,256]{2,1,0:T(8,128)(2,1)S(1)}, u32[]{:S(2)}, u32[]{:S(2)}) collective-permute-start(bf16[2,576,256]{2,1,0:T(8,128)(2,1)S(1)} %fusion.40), channel_id=1, source_target_pairs={{1,0},{3,2},{5,4},{7,6},{9,8},{11,10},{13,12},{15,14},{16,17},{18,... | collective-permute-start | bytes 1769480 | tf_op jit(solution)/shard_map/ppermute | solution.py:161
  64.4 6.8 %collective-permute-start.13 = (bf16[2,8,16,256]{3,2,1,0:T(8,128)(2,1)S(1)}, bf16[2,8,16,256]{3,2,1,0:T(8,128)(2,1)S(1)}, u32[]{:S(2)}, u32[]{:S(2)}) collective-permute-start(bf16[2,8,16,256]{3,2,1,0:T(8,128)(2,1)S(1)} %maximum_select_fusion.2), channel_id=1, source_target_pairs={{0,1},{1,0},{2,3},{3,2},{4,5},{5,4},{6,7},{7,6},{8,9},{9,8},{10,11... | collective-permute-start | bytes 393224 | tf_op jit(solution)/shard_map/ppermute | solution.py:164
  65.9 8.5 %collective-permute-start.18 = (bf16[576,256]{1,0:T(8,128)(2,1)S(1)}, bf16[576,256]{1,0:T(8,128)(2,1)S(1)}, u32[]{:S(2)}, u32[]{:S(2)}) collective-permute-start(bf16[576,256]{1,0:T(8,128)(2,1)S(1)} %fusion.53), channel_id=1, source_target_pairs={{1,5},{3,7},{5,1},{7,3},{9,13},{11,15},{13,9},{15,11},{16,20},{18,... | collective-permute-start | bytes 884744 | tf_op jit(solution)/shard_map/ppermute | solution.py:186
  67.2 16.7 %collective-permute-start.22 = (bf16[576,256]{1,0:T(8,128)(2,1)S(1)}, bf16[576,256]{1,0:T(8,128)(2,1)S(1)}, u32[]{:S(2)}, u32[]{:S(2)}) collective-permute-start(bf16[576,256]{1,0:T(8,128)(2,1)S(1)} %fusion.54), channel_id=1, source_target_pairs={{0,4},{2,6},{4,0},{6,2},{8,12},{10,14},{12,8},{14,10},{17,21},{19,... | collective-permute-start | bytes 884744 | tf_op jit(solution)/shard_map/ppermute | solution.py:186
  71.3 16.5 %collective-permute-start.14 = (bf16[4,8,16,256]{3,2,1,0:T(8,128)(2,1)S(1)}, bf16[4,8,16,256]{3,2,1,0:T(8,128)(2,1)S(1)}, u32[]{:S(2)}, u32[]{:S(2)}) collective-permute-start(bf16[4,8,16,256]{3,2,1,0:T(8,128)(2,1)S(1)} %pad_maximum_fusion.6), channel_id=1, source_target_pairs={{0,25},{2,27},{4,29},{6,31},{8,17},{10,19},{12,21},{14,23},{17,8},... | collective-permute-start | bytes 786440 | tf_op jit(solution)/shard_map/ppermute | solution.py:161
  74.5 14.1 %collective-permute-start.19 = (bf16[576,256]{1,0:T(8,128)(2,1)S(1)}, bf16[576,256]{1,0:T(8,128)(2,1)S(1)}, u32[]{:S(2)}, u32[]{:S(2)}) collective-permute-start(bf16[576,256]{1,0:T(8,128)(2,1)S(1)} %fusion.76), channel_id=1, source_target_pairs={{1,24},{3,26},{5,28},{7,30},{9,16},{11,18},{13,20},{15,22},{16,9},... | collective-permute-start | bytes 884744 | tf_op jit(solution)/shard_map/ppermute | solution.py:161
  84.0 11.9 %collective-permute-start.23 = (bf16[576,256]{1,0:T(8,128)(2,1)S(1)}, bf16[576,256]{1,0:T(8,128)(2,1)S(1)}, u32[]{:S(2)}, u32[]{:S(2)}) collective-permute-start(bf16[576,256]{1,0:T(8,128)(2,1)S(1)} %fusion.77), channel_id=1, source_target_pairs={{0,25},{2,27},{4,29},{6,31},{8,17},{10,19},{12,21},{14,23},{17,8},... | collective-permute-start | bytes 884744 | tf_op jit(solution)/shard_map/ppermute | solution.py:161

commit v2 on v1

--- a/solution.py
+++ b/solution.py
@@ -128,10 +128,6 @@
 AXES = ("section", "strip", "mirror")
 
 
-def after(value, *others):
-    return lax.optimization_barrier((value, *others))[0]
-
-
 def folded(grad_top, acts, masks, kernels):
     sections = lax.axis_size("section")
     strips = lax.axis_size("strip")
@@ -163,18 +159,11 @@
     def mirrored(block):
         return lax.ppermute(block, "mirror", [(0, 1), (1, 0)])
 
-    def partnered(block, lower):
-        return permuted(
-            block,
-            lambda s, m: (sections - 1 - s, 1 - m),
-            lambda s, m: is_major(s, m) != bool(lower),
-        )
-
-    def cored(block, lower):
-        return permuted(block, lambda s, m: (s, 1 - m), lambda s, m: is_major(s, m) == bool(lower))
-
-    def minor_to_major(block):
-        return permuted(block, lambda s, m: (sections - 1 - s, m), lambda s, m: not is_major(s, m))
+    def partnered(block, wanted=lambda s, m: True):
+        return permuted(block, lambda s, m: (sections - 1 - s, 1 - m), wanted)
+
+    def opposite(block):
+        return permuted(block, lambda s, m: (sections - 1 - s, m))
 
     def stripped(block, step, wanted=lambda s, m: True):
         route = [
@@ -213,8 +202,10 @@
     rows = 9 * channels // strips
 
     mine = jnp.stack([top_grads[:count], masks_int[:count].astype(bf16)])
+    own_data = jnp.stack([masks_int.astype(bf16), inputs_all])
     theirs = jnp.stack([top_grads[count:], masks_int[count:].astype(bf16)])
-    mine = jnp.where(major, mine, mirrored(theirs))
+    received = mirrored(jnp.where(major, theirs, own_data[:, count:]))
+    mine = jnp.where(major, mine, received)
     low, high = rims(mine[:, :, :sections], mine[:, :, tile_rows - sections :])
     top_ext, high_masks = jnp.concatenate([low, mine, high], axis=2)
 
@@ -223,9 +214,8 @@
     high_kernel = jnp.where(major, own_kernel, other_kernel)
     low_kernel = jnp.where(major, other_kernel, own_kernel)
 
-    low_all = after(jnp.stack([masks_int.astype(bf16), inputs_all]), mine)
-    moved = jnp.where(major, minor_to_major(low_all[:, :count]), partnered(low_all[:, count:], 1))
-    given_inputs = mirrored(after(inputs_all[count:], mine))
+    moved = opposite(jnp.where(major, received, own_data[:, :count]))
+    given_inputs = mirrored(inputs_all[count:])
     high_inputs = jnp.where(major, inputs_all[:count], given_inputs)
 
     def later_rims():
@@ -277,7 +267,7 @@
     grads = [top_ext[k] for k in range(count)]
     pres = [[None] * count for _ in range(sections)]
     outs = [[None] * count for _ in range(sections)]
-    low_masks = inputs = None
+    low_masks, inputs = later_rims()
     for position in range(sections):
         for k in range(count):
             lower = position >= half
@@ -293,8 +283,6 @@
             if position + 1 < sections and position + 1 != half:
                 hop = hopped(grad_in, position)
                 grads[k] = hop if position else jnp.where(depth == 0, grad_in, hop)
-        if position == 0:
-            low_masks, inputs = later_rims()
 
     def at_depth(pieces):
         chosen = pieces[0]
@@ -308,28 +296,33 @@
     results = [jnp.stack([side(outs, lower, k) for k in range(count)]) for lower in range(2)]
     given = mirrored(jnp.where(major, results[1], results[0]))
     kept = jnp.concatenate([results[0], given])
-    returned = partnered(jnp.concatenate([given, results[1]]), 1)
+    returned = partnered(jnp.concatenate([given, results[1]]), lambda s, m: not is_major(s, m))
     input_grads = jnp.where(major, kept, returned)
 
     patches = unfolded(inputs)
     sums = []
     for lower in range(2):
-        holds = lambda s, m: is_major(s, m) != bool(lower)
         block = jnp.stack([side(pres, lower, k) for k in range(count)])[None]
+        block = across_strips(block).reshape(-1, channels)
         own = lax.dot_general(
-            patches[lower],
-            across_strips(block).reshape(-1, channels),
-            (((0,), (0,)), ((), ())),
-            preferred_element_type=jnp.float32,
-        )
-        own = jnp.stack(kept_rows(own))
-        own = own + cored(own.astype(bf16), lower).astype(jnp.float32)
+            patches[lower], block, (((0,), (0,)), ((), ())), preferred_element_type=jnp.float32
+        )
+        own = jnp.stack(kept_rows(own)).reshape(2, 2, rows // 2, channels)
+        first, second = own[:, 0], own[:, 1]
+        other = jnp.where(major, second, first).astype(bf16)
+        own = jnp.where(major, first, second)
+        own = own + mirrored(other).astype(jnp.float32)
         other = jnp.where(upper_strip == 0, own[1], own[0]).astype(bf16)
         own = jnp.where(upper_strip == 0, own[0], own[1])
-        own = own + stripped(other, 2, holds).astype(jnp.float32)
-        sums.append(own + partnered(own.astype(bf16), lower).astype(jnp.float32))
+        own = own + stripped(other, 2).astype(jnp.float32)
+        sums.append(own + partnered(own.astype(bf16)).astype(jnp.float32))
     factor = 1.0 / math.sqrt(2.0 * micros * tile_rows * strips * tile_width)
-    kernel_grads = jnp.where(major, sums[0], sums[1]) * factor
+    other = mirrored(jnp.where(major, sums[1], sums[0]).astype(bf16)).astype(jnp.float32)
+    own = jnp.where(major, sums[0], sums[1])
+    kernel_grads = jnp.where(
+        major, jnp.concatenate([own, other]), jnp.concatenate([other, own])
+    )
+    kernel_grads = kernel_grads * factor
     return (input_grads[None, None], kernel_grads[None, None])
 
 

time: 97.4 us -> 92 us (0.945)
  starting transfers between devices: 41.5 us -> 33.4 us
  local copies, waits for them, and re-layouts: 2.75 us -> 5.75 us
    ppermute x11 -> x8, starting transfers between devices: 20.9 us -> 13 us  [permuted(): return lax.ppermute(block, AXES, route)]
    ppermute x11 -> x8, waiting for transfers between devices: 20.3 us -> 15.5 us  [permuted(): return lax.ppermute(block, AXES, route)]
    ppermute x5, waiting for transfers between devices: 15.1 us -> 19.3 us  [stripped(): return lax.ppermute(block, AXES, route)]
    another operation x3 -> x1, other arithmetic: 1.98 us -> 0.05 us
    slice x2 -> x1, local copies, waits for them, and re-layouts: 0.05 us -> 1.63 us  [folded(): given_inputs = mirrored(inputs_all[count:])]
    unnamed x71, local copies, waits for them, and re-layouts: 1.91 us -> 3.33 us
    ppermute x5, starting transfers between devices: 9.03 us -> 10.2 us  [stripped(): return lax.ppermute(block, AXES, route)]
    broadcast_in_dim x2 -> x1, other arithmetic: 1.8 us -> 0.74 us  [folded(): return (input_grads[None, None], kernel_grads[None, None])]
  transfers between devices with their start and end apart: 24 -> 24, of which waited for: 13 -> 13; matrix products, arithmetic and copies ran while one was open for 10% -> 13% of each run, Pallas kernels for 0% -> 0%
where the time goes in v2:
time: 92 us; the launch traced here: 91.7 us
  waiting for transfers between devices  38.8 us (42%)
  starting transfers between devices  33.4 us (36%)
  other arithmetic  7.63 us (8%)
  local copies, waits for them, and re-layouts  5.75 us (6%)
  matrix products  4.32 us (5%)
  between operations  1.79 us (2%)
    ppermute x5, waiting for transfers between devices, stripped(): return lax.ppermute(block, AXES, route)  19.3 us
    ppermute x8, waiting for transfers between devices, permuted(): return lax.ppermute(block, AXES, route)  15.5 us
    ppermute x8, starting transfers between devices, permuted(): return lax.ppermute(block, AXES, route)  13 us
    ppermute x5, starting transfers between devices, stripped(): return lax.ppermute(block, AXES, route)  10.2 us
    ppermute x2, starting transfers between devices, rims(): from_near = lax.ppermute(jnp.where(even, last, first), 'strip', near)  7.7 us
    ppermute x2, waiting for transfers between devices, rims(): from_near = lax.ppermute(jnp.where(even, last, first), 'strip', near)  3.51 us
    unnamed x71, local copies, waits for them, and re-layouts  3.33 us
    dot_general x8, matrix products, layer_back(): branch = jnp.dot(patch, kernel, preferred_element_type=jnp.float32)  3.1 us
  transfers between devices with their start and end apart: 24, of which 13 were waited for; matrix products, arithmetic and copies ran while one was open for 13% of the time, Pallas kernels for 0%

profile of v2, /device:TPU:0, one launch (start us, length us, event | category | flops | bytes accessed | tf_op | source)
XLA Modules:
  0.0 91.7 jit_solution(990062489968105338)
XLA Ops:
  0.6 1.6 %slice_bitcast_fusion.8 = bf16[2,8,16,256]{3,2,1,0:T(8,128)(2,1)} fusion(bf16[1,1,4,8,16,256]{5,4,3,2,1,0:T(8,128)(2,1)} %param.5), kind=kLoop, calls=%fused_computation.234 | loop fusion | bytes 262144 | tf_op jit(solution)/shard_map/slice | solution.py:218
  2.8 1.0 %copy.63 = bf16[1,1,4,8,16,256]{5,4,2,3,1,0:T(8,128)(2,1)S(1)} copy(bf16[1,1,4,8,16,256]{5,4,3,2,1,0:T(8,128)(2,1)} %param.5) | data formatting | bytes 524288 | tf_op args[1]
  3.7 1.1 %fusion.106 = bf16[1,4,8,16,256]{4,3,1,2,0:T(8,128)(2,1)S(1)} fusion(s32[1,1,4,8,16,256]{5,4,3,2,1,0:T(8,128)} %param.6), kind=kLoop, calls=%fused_computation.303 | loop fusion | flops 131072 | bytes 786432 | tf_op jit(solution)/shard_map/convert_element_type | solution.py:205
  5.0 0.8 fusion.57
  7.7 1.1 %maximum_select_fusion.1 = (bf16[2,2,8,16,256]{4,3,1,2,0:T(8,128)(2,1)S(1)}, bf16[2,2,8,16,256]{4,3,1,2,0:T(8,128)(2,1)S(1)}) fusion(bf16[2,2,8,16,256]{4,3,1,2,0:T(8,128)(2,1)} %collective-permute-done, bf16[1,2,8,16,256]{4,3,1,2,0:T(8,128)(2,1)S(1)} %get-tuple-element.34, pred[]{:T(512)S(6)} %eq.15, bf16[1,4,8,16,256]{4,3,1,2,0:T(8,128)(2,1)S(1)} %bitcast.274, ...), kind=kLoop, calls=%fused_computation.85 | loop fusion | flops 1310720 | bytes 1572865 | tf_op jit(solution)/shard_map/jit(_where)/select_n | solution.py:208
  9.5 5.6 %collective-permute-start.2 = (bf16[2,2,4,16,256]{4,3,1,2,0:T(8,128)(2,1)S(1)}, bf16[2,2,4,16,256]{4,3,1,2,0:T(8,128)(2,1)S(1)}, u32[]{:S(2)}, u32[]{:S(2)}) collective-permute-start(bf16[2,2,4,16,256]{4,3,1,2,0:T(8,128)(2,1)S(1)} %get-tuple-element.29), channel_id=1, source_target_pairs={{0,2},{4,6},{2,0},{6,4},{1,3},{5,7},{3,1},{7,5},{8,10},{12,14},{10... | collective-permute-start | bytes 393224 | tf_op jit(solution)/shard_map/ppermute | solution.py:189
  15.1 2.4 %collective-permute-start.6 = (bf16[2,2,8,16,256]{4,3,1,2,0:T(8,128)(2,1)S(1)}, bf16[2,2,8,16,256]{4,3,1,2,0:T(8,128)(2,1)S(1)}, u32[]{:S(2)}, u32[]{:S(2)}) collective-permute-start(bf16[2,2,8,16,256]{4,3,1,2,0:T(8,128)(2,1)S(1)} %get-tuple-element.31), channel_id=1, source_target_pairs={{0,24},{2,26},{4,28},{6,30},{1,25},{3,27},{5,29},{7,31},{8,16},{10... | collective-permute-start | bytes 786440 | tf_op jit(solution)/shard_map/ppermute | solution.py:157
  17.5 1.3 %collective-permute-done.2 = bf16[2,2,4,16,256]{4,3,1,2,0:T(8,128)(2,1)S(1)} collective-permute-done((bf16[2,2,4,16,256]{4,3,1,2,0:T(8,128)(2,1)S(1)}, bf16[2,2,4,16,256]{4,3,1,2,0:T(8,128)(2,1)S(1)}, u32[]{:S(2)}, u32[]{:S(2)}) %collective-permute-start.2) | collective-permute-done | bytes 131104 | tf_op jit(solution)/shard_map/ppermute | solution.py:189
  19.5 4.5 %collective-permute-done.6 = bf16[2,2,8,16,256]{4,3,1,2,0:T(8,128)(2,1)S(1)} collective-permute-done((bf16[2,2,8,16,256]{4,3,1,2,0:T(8,128)(2,1)S(1)}, bf16[2,2,8,16,256]{4,3,1,2,0:T(8,128)(2,1)S(1)}, u32[]{:S(2)}, u32[]{:S(2)}) %collective-permute-start.6) | collective-permute-done | bytes 262176 | tf_op jit(solution)/shard_map/ppermute | solution.py:157
  24.7 2.1 %collective-permute-start.9 = (bf16[2,4,16,256]{3,2,1,0:T(8,128)(2,1)S(1)}, bf16[2,4,16,256]{3,2,1,0:T(8,128)(2,1)S(1)}, u32[]{:S(2)}, u32[]{:S(2)}) collective-permute-start(bf16[2,4,16,256]{3,2,1,0:T(8,128)(2,1)S(1)} %get-tuple-element.47), channel_id=1, source_target_pairs={{0,2},{4,6},{2,0},{6,4},{1,3},{5,7},{3,1},{7,5},{8,10},{12,14},{10... | collective-permute-start | bytes 196616 | tf_op jit(solution)/shard_map/ppermute | solution.py:189
  26.9 2.2 %collective-permute-done.9 = bf16[2,4,16,256]{3,2,1,0:T(8,128)(2,1)S(1)} collective-permute-done((bf16[2,4,16,256]{3,2,1,0:T(8,128)(2,1)S(1)}, bf16[2,4,16,256]{3,2,1,0:T(8,128)(2,1)S(1)}, u32[]{:S(2)}, u32[]{:S(2)}) %collective-permute-start.9) | collective-permute-done | bytes 65568 | tf_op jit(solution)/shard_map/ppermute | solution.py:189
  29.2 2.1 %collective-permute-start.14 = (bf16[1,4,10,16,256]{4,3,2,1,0:T(8,128)(2,1)S(1)}, bf16[1,4,10,16,256]{4,3,2,1,0:T(8,128)(2,1)S(1)}, u32[]{:S(2)}, u32[]{:S(2)}) collective-permute-start(bf16[1,4,10,16,256]{4,3,2,1,0:T(8,128)(2,1)S(1)} %maximum_bitcast_fusion), channel_id=1, source_target_pairs={{0,2},{2,0},{4,6},{6,4},{1,3},{3,1},{5,7},{7,5},{8,10},{10,8},{12,... | collective-permute-start | bytes 983048 | tf_op jit(solution)/shard_map/ppermute | solution.py:175
  31.3 5.6 %collective-permute-done.14 = bf16[1,4,10,16,256]{4,3,2,1,0:T(8,128)(2,1)S(1)} collective-permute-done((bf16[1,4,10,16,256]{4,3,2,1,0:T(8,128)(2,1)S(1)}, bf16[1,4,10,16,256]{4,3,2,1,0:T(8,128)(2,1)S(1)}, u32[]{:S(2)}, u32[]{:S(2)}) %collective-permute-start.14) | collective-permute-done | bytes 327712 | tf_op jit(solution)/shard_map/ppermute | solution.py:175
  39.3 1.6 %collective-permute-start.4 = (bf16[14,16,256]{2,1,0:T(8,128)(2,1)S(1)}, bf16[14,16,256]{2,1,0:T(8,128)(2,1)S(1)}, u32[]{:S(2)}, u32[]{:S(2)}) collective-permute-start(bf16[14,16,256]{2,1,0:T(8,128)(2,1)S(1)} %fusion.25), channel_id=1, source_target_pairs={{0,8},{2,10},{4,12},{6,14},{1,9},{3,11},{5,13},{7,15},{8,0},{10,2}... | collective-permute-start | bytes 344072 | tf_op jit(solution)/shard_map/ppermute | solution.py:157
  42.1 2.0 %collective-permute-done.4 = bf16[14,16,256]{2,1,0:T(8,128)(2,1)S(1)} collective-permute-done((bf16[14,16,256]{2,1,0:T(8,128)(2,1)S(1)}, bf16[14,16,256]{2,1,0:T(8,128)(2,1)S(1)}, u32[]{:S(2)}, u32[]{:S(2)}) %collective-permute-start.4) | collective-permute-done | bytes 114720 | tf_op jit(solution)/shard_map/ppermute | solution.py:157
  44.1 2.0 %collective-permute-done.5 = bf16[14,16,256]{2,1,0:T(8,128)(2,1)S(1)} collective-permute-done((bf16[14,16,256]{2,1,0:T(8,128)(2,1)S(1)}, bf16[14,16,256]{2,1,0:T(8,128)(2,1)S(1)}, u32[]{:S(2)}, u32[]{:S(2)}) %collective-permute-start.5) | collective-permute-done | bytes 114720 | tf_op jit(solution)/shard_map/ppermute | solution.py:157
  48.2 0.8 collective-permute-start.11
  49.6 1.4 %collective-permute-start.10 = (bf16[10,16,256]{2,1,0:T(8,128)(2,1)S(1)}, bf16[10,16,256]{2,1,0:T(8,128)(2,1)S(1)}, u32[]{:S(2)}, u32[]{:S(2)}) collective-permute-start(bf16[10,16,256]{2,1,0:T(8,128)(2,1)S(1)} %fusion.37), channel_id=1, source_target_pairs={{0,8},{2,10},{4,12},{6,14},{1,9},{3,11},{5,13},{7,15},{8,0},{10,2}... | collective-permute-start | bytes 245768 | tf_op jit(solution)/shard_map/ppermute | solution.py:157
  51.0 1.8 %collective-permute-start.15 = (bf16[1,2,8,16,256]{4,3,2,1,0:T(8,128)(2,1)S(1)}, bf16[1,2,8,16,256]{4,3,2,1,0:T(8,128)(2,1)S(1)}, u32[]{:S(2)}, u32[]{:S(2)}) collective-permute-start(bf16[1,2,8,16,256]{4,3,2,1,0:T(8,128)(2,1)S(1)} %maximum_bitcast_fusion.1), channel_id=1, source_target_pairs={{0,2},{2,0},{4,6},{6,4},{1,3},{3,1},{5,7},{7,5},{8,10},{10,8},{12,... | collective-permute-start | bytes 393224 | tf_op jit(solution)/shard_map/ppermute | solution.py:175
  52.8 1.3 %collective-permute-done.10 = bf16[10,16,256]{2,1,0:T(8,128)(2,1)S(1)} collective-permute-done((bf16[10,16,256]{2,1,0:T(8,128)(2,1)S(1)}, bf16[10,16,256]{2,1,0:T(8,128)(2,1)S(1)}, u32[]{:S(2)}, u32[]{:S(2)}) %collective-permute-start.10) | collective-permute-done | bytes 81952 | tf_op jit(solution)/shard_map/ppermute | solution.py:157
  55.4 1.8 %collective-permute-start.19 = (bf16[1,2,8,16,256]{4,3,2,1,0:T(8,128)(2,1)S(1)}, bf16[1,2,8,16,256]{4,3,2,1,0:T(8,128)(2,1)S(1)}, u32[]{:S(2)}, u32[]{:S(2)}) collective-permute-start(bf16[1,2,8,16,256]{4,3,2,1,0:T(8,128)(2,1)S(1)} %maximum_bitcast_fusion.2), channel_id=1, source_target_pairs={{0,2},{2,0},{4,6},{6,4},{1,3},{3,1},{5,7},{7,5},{8,10},{10,8},{12,... | collective-permute-start | bytes 393224 | tf_op jit(solution)/shard_map/ppermute | solution.py:175
  58.3 3.0 %collective-permute-done.19 = bf16[1,2,8,16,256]{4,3,2,1,0:T(8,128)(2,1)S(1)} collective-permute-done((bf16[1,2,8,16,256]{4,3,2,1,0:T(8,128)(2,1)S(1)}, bf16[1,2,8,16,256]{4,3,2,1,0:T(8,128)(2,1)S(1)}, u32[]{:S(2)}, u32[]{:S(2)}) %collective-permute-start.19) | collective-permute-done | bytes 131104 | tf_op jit(solution)/shard_map/ppermute | solution.py:175
  62.5 3.1 %collective-permute-start.17 = (bf16[288,256]{1,0:T(8,128)(2,1)S(1)}, bf16[288,256]{1,0:T(8,128)(2,1)S(1)}, u32[]{:S(2)}, u32[]{:S(2)}) collective-permute-start(bf16[288,256]{1,0:T(8,128)(2,1)S(1)} %fusion.60), channel_id=1, source_target_pairs={{0,4},{2,6},{4,0},{6,2},{1,5},{3,7},{5,1},{7,3},{8,12},{10,14},{12... | collective-permute-start | bytes 442376 | tf_op jit(solution)/shard_map/ppermute | solution.py:175
  65.7 1.4 %collective-permute-start.21 = (bf16[288,256]{1,0:T(8,128)(2,1)S(1)}, bf16[288,256]{1,0:T(8,128)(2,1)S(1)}, u32[]{:S(2)}, u32[]{:S(2)}) collective-permute-start(bf16[288,256]{1,0:T(8,128)(2,1)S(1)} %fusion.61), channel_id=1, source_target_pairs={{0,4},{2,6},{4,0},{6,2},{1,5},{3,7},{5,1},{7,3},{8,12},{10,14},{12... | collective-permute-start | bytes 442376 | tf_op jit(solution)/shard_map/ppermute | solution.py:175
  67.1 9.5 %collective-permute-done.17 = bf16[288,256]{1,0:T(8,128)(2,1)S(1)} collective-permute-done((bf16[288,256]{1,0:T(8,128)(2,1)S(1)}, bf16[288,256]{1,0:T(8,128)(2,1)S(1)}, u32[]{:S(2)}, u32[]{:S(2)}) %collective-permute-start.17) | collective-permute-done | bytes 147488 | tf_op jit(solution)/shard_map/ppermute | solution.py:175
  76.6 1.6 %collective-permute-start.18 = (bf16[288,256]{1,0:T(8,128)(2,1)S(1)}, bf16[288,256]{1,0:T(8,128)(2,1)S(1)}, u32[]{:S(2)}, u32[]{:S(2)}) collective-permute-start(bf16[288,256]{1,0:T(8,128)(2,1)S(1)} %get-tuple-element.4), channel_id=1, source_target_pairs={{0,25},{2,27},{4,29},{6,31},{1,24},{3,26},{5,28},{7,30},{8,17},{10... | collective-permute-start | bytes 442376 | tf_op jit(solution)/shard_map/ppermute | solution.py:157
  78.3 1.3 %collective-permute-done.21 = bf16[288,256]{1,0:T(8,128)(2,1)S(1)} collective-permute-done((bf16[288,256]{1,0:T(8,128)(2,1)S(1)}, bf16[288,256]{1,0:T(8,128)(2,1)S(1)}, u32[]{:S(2)}, u32[]{:S(2)}) %collective-permute-start.21) | collective-permute-done | bytes 147488 | tf_op jit(solution)/shard_map/ppermute | solution.py:175
  79.6 1.8 %collective-permute-start.22 = (bf16[288,256]{1,0:T(8,128)(2,1)S(1)}, bf16[288,256]{1,0:T(8,128)(2,1)S(1)}, u32[]{:S(2)}, u32[]{:S(2)}) collective-permute-start(bf16[288,256]{1,0:T(8,128)(2,1)S(1)} %get-tuple-element.2), channel_id=1, source_target_pairs={{0,25},{2,27},{4,29},{6,31},{1,24},{3,26},{5,28},{7,30},{8,17},{10... | collective-permute-start | bytes 442376 | tf_op jit(solution)/shard_map/ppermute | solution.py:157
  81.5 2.8 %collective-permute-start.13 = (bf16[4,8,16,256]{3,2,1,0:T(8,128)(2,1)S(1)}, bf16[4,8,16,256]{3,2,1,0:T(8,128)(2,1)S(1)}, u32[]{:S(2)}, u32[]{:S(2)}) collective-permute-start(bf16[4,8,16,256]{3,2,1,0:T(8,128)(2,1)S(1)} %pad_maximum_fusion.5), channel_id=1, source_target_pairs={{0,25},{2,27},{4,29},{6,31},{8,17},{10,19},{12,21},{14,23},{17,8},... | collective-permute-start | bytes 786440 | tf_op jit(solution)/shard_map/ppermute | solution.py:157
  84.3 2.6 %collective-permute-done.22 = bf16[288,256]{1,0:T(8,128)(2,1)S(1)} collective-permute-done((bf16[288,256]{1,0:T(8,128)(2,1)S(1)}, bf16[288,256]{1,0:T(8,128)(2,1)S(1)}, u32[]{:S(2)}, u32[]{:S(2)}) %collective-permute-start.22) | collective-permute-done | bytes 147488 | tf_op jit(solution)/shard_map/ppermute | solution.py:157
  87.0 3.0 %collective-permute-done.13 = bf16[4,8,16,256]{3,2,1,0:T(8,128)(2,1)S(1)} collective-permute-done((bf16[4,8,16,256]{3,2,1,0:T(8,128)(2,1)S(1)}, bf16[4,8,16,256]{3,2,1,0:T(8,128)(2,1)S(1)}, u32[]{:S(2)}, u32[]{:S(2)}) %collective-permute-start.13) | collective-permute-done | bytes 262176 | tf_op jit(solution)/shard_map/ppermute | solution.py:157
  90.8 0.9 fusion.42
  (169 shorter events, 14.8 us)
Async XLA Ops:
  0.6 4.3 %copy-start = (s32[1,1,4,8,16,256]{5,4,3,2,1,0:T(8,128)S(1)}, s32[1,1,4,8,16,256]{5,4,3,2,1,0:T(8,128)}, u32[]{:S(2)}) copy-start(s32[1,1,4,8,16,256]{5,4,3,2,1,0:T(8,128)} %param.6) | copy-start | bytes 1572868
  2.3 4.9 %collective-permute-start.7 = (bf16[2,8,16,256]{3,2,1,0:T(8,128)(2,1)}, bf16[2,8,16,256]{3,2,1,0:T(8,128)(2,1)S(1)}, u32[]{:S(2)}, u32[]{:S(2)}) collective-permute-start(bf16[2,8,16,256]{3,2,1,0:T(8,128)(2,1)} %slice_bitcast_fusion.8), channel_id=1, source_target_pairs={{0,1},{1,0},{2,3},{3,2},{4,5},{5,4},{6,7},{7,6},{8,9},{9,8},{10,11... | collective-permute-start | bytes 393224 | tf_op jit(solution)/shard_map/ppermute | solution.py:160
  3.7 1.3 %copy-start.3 = (bf16[1,4,8,16,256]{4,3,2,1,0:T(8,128)(2,1)S(1)}, bf16[1,4,8,16,256]{4,3,2,1,0:T(8,128)(2,1)}, u32[]{:S(2)}) copy-start(bf16[1,4,8,16,256]{4,3,2,1,0:T(8,128)(2,1)} %param.4) | copy-start | bytes 786436
  4.9 1.4 %copy-start.1 = (bf16[1,1,3,3,256,256]{5,4,3,2,1,0:T(8,128)(2,1)S(1)}, bf16[1,1,3,3,256,256]{5,4,3,2,1,0:T(8,128)(2,1)}, u32[]{:S(2)}) copy-start(bf16[1,1,3,3,256,256]{5,4,3,2,1,0:T(8,128)(2,1)} %param.7) | copy-start | bytes 3538948
  5.8 1.4 %copy-start.2 = (bf16[1,1,4,8,16,256]{5,4,3,2,1,0:T(8,128)(2,1)S(1)}, bf16[1,1,4,8,16,256]{5,4,3,2,1,0:T(8,128)(2,1)}, u32[]{:S(2)}) copy-start(bf16[1,1,4,8,16,256]{5,4,3,2,1,0:T(8,128)(2,1)} %param.5) | copy-start | bytes 786436
  5.8 1.9 %collective-permute-start = (bf16[2,2,8,16,256]{4,3,1,2,0:T(8,128)(2,1)}, bf16[2,2,8,16,256]{4,3,1,2,0:T(8,128)(2,1)}, u32[]{:S(2)}, u32[]{:S(2)}) collective-permute-start(bf16[2,2,8,16,256]{4,3,1,2,0:T(8,128)(2,1)} %fusion.57), channel_id=1, source_target_pairs={{0,1},{1,0},{2,3},{3,2},{4,5},{5,4},{6,7},{7,6},{8,9},{9,8},{10,11... | collective-permute-start | bytes 786440 | tf_op jit(solution)/shard_map/ppermute | solution.py:160
  7.0 31.5 %collective-permute-start.3 = (bf16[2304,256]{1,0:T(8,128)(2,1)S(1)}, bf16[2304,256]{1,0:T(8,128)(2,1)S(1)}, u32[]{:S(2)}, u32[]{:S(2)}) collective-permute-start(bf16[2304,256]{1,0:T(8,128)(2,1)S(1)} %bitcast.271), channel_id=1, source_target_pairs={{0,1},{1,0},{2,3},{3,2},{4,5},{5,4},{6,7},{7,6},{8,9},{9,8},{10,11... | collective-permute-start | bytes 3538952 | tf_op jit(solution)/shard_map/ppermute | solution.py:160
  8.8 8.7 %collective-permute-start.1 = (bf16[2,2,4,16,256]{4,3,1,2,0:T(8,128)(2,1)S(1)}, bf16[2,2,4,16,256]{4,3,1,2,0:T(8,128)(2,1)S(1)}, u32[]{:S(2)}, u32[]{:S(2)}) collective-permute-start(bf16[2,2,4,16,256]{4,3,1,2,0:T(8,128)(2,1)S(1)} %get-tuple-element.28), channel_id=1, source_target_pairs={{2,4},{4,2},{3,5},{5,3},{10,12},{12,10},{11,13},{13,11},{18,20},{2... | collective-permute-start | bytes 393224 | tf_op jit(solution)/shard_map/ppermute | solution.py:190
  9.5 9.3 %collective-permute-start.2 = (bf16[2,2,4,16,256]{4,3,1,2,0:T(8,128)(2,1)S(1)}, bf16[2,2,4,16,256]{4,3,1,2,0:T(8,128)(2,1)S(1)}, u32[]{:S(2)}, u32[]{:S(2)}) collective-permute-start(bf16[2,2,4,16,256]{4,3,1,2,0:T(8,128)(2,1)S(1)} %get-tuple-element.29), channel_id=1, source_target_pairs={{0,2},{4,6},{2,0},{6,4},{1,3},{5,7},{3,1},{7,5},{8,10},{12,14},{10... | collective-permute-start | bytes 393224 | tf_op jit(solution)/shard_map/ppermute | solution.py:189
  15.1 8.9 %collective-permute-start.6 = (bf16[2,2,8,16,256]{4,3,1,2,0:T(8,128)(2,1)S(1)}, bf16[2,2,8,16,256]{4,3,1,2,0:T(8,128)(2,1)S(1)}, u32[]{:S(2)}, u32[]{:S(2)}) collective-permute-start(bf16[2,2,8,16,256]{4,3,1,2,0:T(8,128)(2,1)S(1)} %get-tuple-element.31), channel_id=1, source_target_pairs={{0,24},{2,26},{4,28},{6,30},{1,25},{3,27},{5,29},{7,31},{8,16},{10... | collective-permute-start | bytes 786440 | tf_op jit(solution)/shard_map/ppermute | solution.py:157
  24.1 2.8 %collective-permute-start.8 = (bf16[2,4,16,256]{3,2,1,0:T(8,128)(2,1)S(1)}, bf16[2,4,16,256]{3,2,1,0:T(8,128)(2,1)S(1)}, u32[]{:S(2)}, u32[]{:S(2)}) collective-permute-start(bf16[2,4,16,256]{3,2,1,0:T(8,128)(2,1)S(1)} %get-tuple-element.46), channel_id=1, source_target_pairs={{2,4},{4,2},{3,5},{5,3},{10,12},{12,10},{11,13},{13,11},{18,20},{2... | collective-permute-start | bytes 196616 | tf_op jit(solution)/shard_map/ppermute | solution.py:190
  24.7 4.4 %collective-permute-start.9 = (bf16[2,4,16,256]{3,2,1,0:T(8,128)(2,1)S(1)}, bf16[2,4,16,256]{3,2,1,0:T(8,128)(2,1)S(1)}, u32[]{:S(2)}, u32[]{:S(2)}) collective-permute-start(bf16[2,4,16,256]{3,2,1,0:T(8,128)(2,1)S(1)} %get-tuple-element.47), channel_id=1, source_target_pairs={{0,2},{4,6},{2,0},{6,4},{1,3},{5,7},{3,1},{7,5},{8,10},{12,14},{10... | collective-permute-start | bytes 196616 | tf_op jit(solution)/shard_map/ppermute | solution.py:189
  29.2 7.8 %collective-permute-start.14 = (bf16[1,4,10,16,256]{4,3,2,1,0:T(8,128)(2,1)S(1)}, bf16[1,4,10,16,256]{4,3,2,1,0:T(8,128)(2,1)S(1)}, u32[]{:S(2)}, u32[]{:S(2)}) collective-permute-start(bf16[1,4,10,16,256]{4,3,2,1,0:T(8,128)(2,1)S(1)} %maximum_bitcast_fusion), channel_id=1, source_target_pairs={{0,2},{2,0},{4,6},{6,4},{1,3},{3,1},{5,7},{7,5},{8,10},{10,8},{12,... | collective-permute-start | bytes 983048 | tf_op jit(solution)/shard_map/ppermute | solution.py:175
  39.3 4.9 %collective-permute-start.4 = (bf16[14,16,256]{2,1,0:T(8,128)(2,1)S(1)}, bf16[14,16,256]{2,1,0:T(8,128)(2,1)S(1)}, u32[]{:S(2)}, u32[]{:S(2)}) collective-permute-start(bf16[14,16,256]{2,1,0:T(8,128)(2,1)S(1)} %fusion.25), channel_id=1, source_target_pairs={{0,8},{2,10},{4,12},{6,14},{1,9},{3,11},{5,13},{7,15},{8,0},{10,2}... | collective-permute-start | bytes 344072 | tf_op jit(solution)/shard_map/ppermute | solution.py:157
  41.3 4.9 %collective-permute-start.5 = (bf16[14,16,256]{2,1,0:T(8,128)(2,1)S(1)}, bf16[14,16,256]{2,1,0:T(8,128)(2,1)S(1)}, u32[]{:S(2)}, u32[]{:S(2)}) collective-permute-start(bf16[14,16,256]{2,1,0:T(8,128)(2,1)S(1)} %fusion.22), channel_id=1, source_target_pairs={{0,8},{2,10},{4,12},{6,14},{1,9},{3,11},{5,13},{7,15},{8,0},{10,2}... | collective-permute-start | bytes 344072 | tf_op jit(solution)/shard_map/ppermute | solution.py:157
  48.2 4.6 %collective-permute-start.11 = (bf16[10,16,256]{2,1,0:T(8,128)(2,1)S(1)}, bf16[10,16,256]{2,1,0:T(8,128)(2,1)S(1)}, u32[]{:S(2)}, u32[]{:S(2)}) collective-permute-start(bf16[10,16,256]{2,1,0:T(8,128)(2,1)S(1)} %fusion.34), channel_id=1, source_target_pairs={{0,8},{2,10},{4,12},{6,14},{1,9},{3,11},{5,13},{7,15},{8,0},{10,2}... | collective-permute-start | bytes 245768 | tf_op jit(solution)/shard_map/ppermute | solution.py:157
  49.6 4.5 %collective-permute-start.10 = (bf16[10,16,256]{2,1,0:T(8,128)(2,1)S(1)}, bf16[10,16,256]{2,1,0:T(8,128)(2,1)S(1)}, u32[]{:S(2)}, u32[]{:S(2)}) collective-permute-start(bf16[10,16,256]{2,1,0:T(8,128)(2,1)S(1)} %fusion.37), channel_id=1, source_target_pairs={{0,8},{2,10},{4,12},{6,14},{1,9},{3,11},{5,13},{7,15},{8,0},{10,2}... | collective-permute-start | bytes 245768 | tf_op jit(solution)/shard_map/ppermute | solution.py:157
  51.0 6.2 %collective-permute-start.15 = (bf16[1,2,8,16,256]{4,3,2,1,0:T(8,128)(2,1)S(1)}, bf16[1,2,8,16,256]{4,3,2,1,0:T(8,128)(2,1)S(1)}, u32[]{:S(2)}, u32[]{:S(2)}) collective-permute-start(bf16[1,2,8,16,256]{4,3,2,1,0:T(8,128)(2,1)S(1)} %maximum_bitcast_fusion.1), channel_id=1, source_target_pairs={{0,2},{2,0},{4,6},{6,4},{1,3},{3,1},{5,7},{7,5},{8,10},{10,8},{12,... | collective-permute-start | bytes 393224 | tf_op jit(solution)/shard_map/ppermute | solution.py:175
  55.3 26.2 %collective-permute-start.12 = (bf16[2,8,16,256]{3,2,1,0:T(8,128)(2,1)S(1)}, bf16[2,8,16,256]{3,2,1,0:T(8,128)(2,1)S(1)}, u32[]{:S(2)}, u32[]{:S(2)}) collective-permute-start(bf16[2,8,16,256]{3,2,1,0:T(8,128)(2,1)S(1)} %maximum_select_fusion.3), channel_id=1, source_target_pairs={{0,1},{1,0},{2,3},{3,2},{4,5},{5,4},{6,7},{7,6},{8,9},{9,8},{10,11... | collective-permute-start | bytes 393224 | tf_op jit(solution)/shard_map/ppermute | solution.py:160
  55.4 6.0 %collective-permute-start.19 = (bf16[1,2,8,16,256]{4,3,2,1,0:T(8,128)(2,1)S(1)}, bf16[1,2,8,16,256]{4,3,2,1,0:T(8,128)(2,1)S(1)}, u32[]{:S(2)}, u32[]{:S(2)}) collective-permute-start(bf16[1,2,8,16,256]{4,3,2,1,0:T(8,128)(2,1)S(1)} %maximum_bitcast_fusion.2), channel_id=1, source_target_pairs={{0,2},{2,0},{4,6},{6,4},{1,3},{3,1},{5,7},{7,5},{8,10},{10,8},{12,... | collective-permute-start | bytes 393224 | tf_op jit(solution)/shard_map/ppermute | solution.py:175
  58.1 4.2 %collective-permute-start.16 = (bf16[2,288,256]{2,1,0:T(8,128)(2,1)S(1)}, bf16[2,288,256]{2,1,0:T(8,128)(2,1)S(1)}, u32[]{:S(2)}, u32[]{:S(2)}) collective-permute-start(bf16[2,288,256]{2,1,0:T(8,128)(2,1)S(1)} %fusion.54), channel_id=1, source_target_pairs={{0,1},{1,0},{2,3},{3,2},{4,5},{5,4},{6,7},{7,6},{8,9},{9,8},{10,11... | collective-permute-start | bytes 884744 | tf_op jit(solution)/shard_map/ppermute | solution.py:160
  62.2 3.3 %collective-permute-start.20 = (bf16[2,288,256]{2,1,0:T(8,128)(2,1)S(1)}, bf16[2,288,256]{2,1,0:T(8,128)(2,1)S(1)}, u32[]{:S(2)}, u32[]{:S(2)}) collective-permute-start(bf16[2,288,256]{2,1,0:T(8,128)(2,1)S(1)} %fusion.55), channel_id=1, source_target_pairs={{0,1},{1,0},{2,3},{3,2},{4,5},{5,4},{6,7},{7,6},{8,9},{9,8},{10,11... | collective-permute-start | bytes 884744 | tf_op jit(solution)/shard_map/ppermute | solution.py:160
  62.5 14.1 %collective-permute-start.17 = (bf16[288,256]{1,0:T(8,128)(2,1)S(1)}, bf16[288,256]{1,0:T(8,128)(2,1)S(1)}, u32[]{:S(2)}, u32[]{:S(2)}) collective-permute-start(bf16[288,256]{1,0:T(8,128)(2,1)S(1)} %fusion.60), channel_id=1, source_target_pairs={{0,4},{2,6},{4,0},{6,2},{1,5},{3,7},{5,1},{7,3},{8,12},{10,14},{12... | collective-permute-start | bytes 442376 | tf_op jit(solution)/shard_map/ppermute | solution.py:175
  65.7 13.8 %collective-permute-start.21 = (bf16[288,256]{1,0:T(8,128)(2,1)S(1)}, bf16[288,256]{1,0:T(8,128)(2,1)S(1)}, u32[]{:S(2)}, u32[]{:S(2)}) collective-permute-start(bf16[288,256]{1,0:T(8,128)(2,1)S(1)} %fusion.61), channel_id=1, source_target_pairs={{0,4},{2,6},{4,0},{6,2},{1,5},{3,7},{5,1},{7,3},{8,12},{10,14},{12... | collective-permute-start | bytes 442376 | tf_op jit(solution)/shard_map/ppermute | solution.py:175
  76.6 7.6 %collective-permute-start.18 = (bf16[288,256]{1,0:T(8,128)(2,1)S(1)}, bf16[288,256]{1,0:T(8,128)(2,1)S(1)}, u32[]{:S(2)}, u32[]{:S(2)}) collective-permute-start(bf16[288,256]{1,0:T(8,128)(2,1)S(1)} %get-tuple-element.4), channel_id=1, source_target_pairs={{0,25},{2,27},{4,29},{6,31},{1,24},{3,26},{5,28},{7,30},{8,17},{10... | collective-permute-start | bytes 442376 | tf_op jit(solution)/shard_map/ppermute | solution.py:157
  79.6 7.2 %collective-permute-start.22 = (bf16[288,256]{1,0:T(8,128)(2,1)S(1)}, bf16[288,256]{1,0:T(8,128)(2,1)S(1)}, u32[]{:S(2)}, u32[]{:S(2)}) collective-permute-start(bf16[288,256]{1,0:T(8,128)(2,1)S(1)} %get-tuple-element.2), channel_id=1, source_target_pairs={{0,25},{2,27},{4,29},{6,31},{1,24},{3,26},{5,28},{7,30},{8,17},{10... | collective-permute-start | bytes 442376 | tf_op jit(solution)/shard_map/ppermute | solution.py:157
  81.5 8.6 %collective-permute-start.13 = (bf16[4,8,16,256]{3,2,1,0:T(8,128)(2,1)S(1)}, bf16[4,8,16,256]{3,2,1,0:T(8,128)(2,1)S(1)}, u32[]{:S(2)}, u32[]{:S(2)}) collective-permute-start(bf16[4,8,16,256]{3,2,1,0:T(8,128)(2,1)S(1)} %pad_maximum_fusion.5), channel_id=1, source_target_pairs={{0,25},{2,27},{4,29},{6,31},{8,17},{10,19},{12,21},{14,23},{17,8},... | collective-permute-start | bytes 786440 | tf_op jit(solution)/shard_map/ppermute | solution.py:157
  86.9 3.9 %collective-permute-start.23 = (bf16[288,256]{1,0:T(8,128)(2,1)S(1)}, bf16[288,256]{1,0:T(8,128)(2,1)S(1)}, u32[]{:S(2)}, u32[]{:S(2)}) collective-permute-start(bf16[288,256]{1,0:T(8,128)(2,1)S(1)} %get-tuple-element.19), channel_id=1, source_target_pairs={{0,1},{1,0},{2,3},{3,2},{4,5},{5,4},{6,7},{7,6},{8,9},{9,8},{10,11... | collective-permute-start | bytes 442376 | tf_op jit(solution)/shard_map/ppermute | solution.py:160

commit v3 on v2

--- a/solution.py
+++ b/solution.py
@@ -143,9 +143,6 @@
     def flat(s, z, m):
         return (s * strips + z) * 2 + m
 
-    def is_major(s, m):
-        return m == (0 if s >= half else 1)
-
     cells = [(s, m) for s in range(sections) for m in range(2)]
 
     def permuted(block, target, wanted=lambda s, m: True):
@@ -183,15 +180,24 @@
     even = strip_id % 2 == 0
 
     def rims(first, last):
-        near = [(z, z + 1) for z in range(0, strips - 1, 2)]
-        far = [(z, z + 1) for z in range(1, strips - 1, 2)]
-        near, far = [pairs + [(b, a) for a, b in pairs] for pairs in (near, far)]
-        from_near = lax.ppermute(jnp.where(even, last, first), "strip", near)
-        from_far = lax.ppermute(jnp.where(even, first, last), "strip", far)
-        return jnp.where(even, from_far, from_near), jnp.where(even, from_near, from_far)
-
-    def across_strips(block):
-        return jnp.concatenate([block, stripped(block, 1)])
+        from_near = lax.ppermute(
+            jnp.where(even, last, first), "strip", [(z, z ^ 1) for z in range(strips)]
+        )
+
+        def far(s, z, m):
+            other = z + 1 if z % 2 else z - 1
+            return (s, other, m) if 0 <= other < strips else (s, z, 1 - m)
+
+        route = [
+            (flat(s, z, m), flat(*far(s, z, m))) for s, m in cells for z in range(strips)
+        ]
+        from_far = lax.ppermute(jnp.where(even, first, last), AXES, route)
+        low, high = jnp.where(even, from_far, from_near), jnp.where(even, from_near, from_far)
+        zero = jnp.zeros_like(low)
+        return jnp.where(strip_id == 0, zero, low), jnp.where(strip_id == strips - 1, zero, high)
+
+    def across_strips(block, step):
+        return jnp.stack([block, stripped(block, step)])
 
     top_grads = grad_top[0]
     inputs_all = acts[0, 0]
@@ -229,31 +235,30 @@
         low_masks = jnp.concatenate([low[:, :half], block[0], high[:, :half]], axis=1)
         low_inputs = [low[:, half : half + 1], block[1], high[:, half : half + 1]]
         high_inputs_ext = [low[:, half + 1 :], block[2], high[:, half + 1 :]]
-        inputs = jnp.concatenate(
-            [jnp.concatenate(high_inputs_ext, axis=1), jnp.concatenate(low_inputs, axis=1)]
-        )
-        return low_masks, across_strips(inputs[None])
+        inputs = [jnp.concatenate(high_inputs_ext, axis=1), jnp.concatenate(low_inputs, axis=1)]
+        return low_masks, inputs
 
     column, upper_strip = strip_id % 2, strip_id // 2
 
-    def unfolded(tall):
+    def unfolded(tall, lower):
         wide = jnp.pad(tall, ((0, 0), (0, 0), (0, 0), (1, 1), (0, 0)))
 
         def tap(index):
             a, b = divmod(index, 3)
             return wide[:, :, a : a + tile_rows, b : b + tile_width]
 
-        pieces = [
-            jnp.where(column == 1, tap(first + 2), tap(first)) for first in (0, 1, 2, 4, 5, 6)
-        ]
-        joined = jnp.concatenate(pieces, axis=-1).reshape(2, 2, count * pixels, 6 * channels)
-        return joined.swapaxes(0, 1).reshape(2, 2 * count * pixels, 6 * channels)
-
-    def kept_rows(taps):
-        start = column * (channels // 4)
-        near = lax.dynamic_slice_in_dim(taps, start, rows)
-        far = lax.dynamic_slice_in_dim(taps[3 * channels :], start + channels // 2, rows)
-        return near, far
+        taps, flag, step = (range(5), upper_strip, 4) if lower else ((0, 1, 2, 4, 5, 6), column, 2)
+        pieces = [jnp.where(flag == 1, tap(first + step), tap(first)) for first in taps]
+        return jnp.concatenate(pieces, axis=-1).reshape(2 * count * pixels, len(taps) * channels)
+
+    def kept_rows(taps, lower):
+        if lower:
+            start = upper_strip * (channels // 2)
+            far = lax.dynamic_slice_in_dim(taps, start + rows, rows)
+        else:
+            start = column * (channels // 4)
+            far = lax.dynamic_slice_in_dim(taps[3 * channels :], start + channels // 2, rows)
+        return lax.dynamic_slice_in_dim(taps, start, rows), far
 
     def layer_back(grad_out, mask, kernel):
         height = grad_out.shape[0] - 2
@@ -294,27 +299,29 @@
         return at_depth([table[sections - 1 - q if lower else q][k] for q in range(half)])
 
     results = [jnp.stack([side(outs, lower, k) for k in range(count)]) for lower in range(2)]
-    given = mirrored(jnp.where(major, results[1], results[0]))
-    kept = jnp.concatenate([results[0], given])
-    returned = partnered(jnp.concatenate([given, results[1]]), lambda s, m: not is_major(s, m))
-    input_grads = jnp.where(major, kept, returned)
-
-    patches = unfolded(inputs)
+    moved_back = opposite(results[1])
+    given = mirrored(jnp.where(major, moved_back, results[0]))
+    input_grads = jnp.concatenate([jnp.where(major, results[0], moved_back), given])
+
     sums = []
     for lower in range(2):
-        block = jnp.stack([side(pres, lower, k) for k in range(count)])[None]
-        block = across_strips(block).reshape(-1, channels)
+        gather_step, sum_step = (2, 1) if lower else (1, 2)
+        tall = across_strips(inputs[lower], gather_step)
+        patches = unfolded(tall, lower)
+        block = jnp.stack([side(pres, lower, k) for k in range(count)])
+        block = across_strips(block, gather_step).reshape(-1, channels)
         own = lax.dot_general(
-            patches[lower], block, (((0,), (0,)), ((), ())), preferred_element_type=jnp.float32
-        )
-        own = jnp.stack(kept_rows(own)).reshape(2, 2, rows // 2, channels)
+            patches, block, (((0,), (0,)), ((), ())), preferred_element_type=jnp.float32
+        )
+        own = jnp.stack(kept_rows(own, lower)).reshape(2, 2, rows // 2, channels)
         first, second = own[:, 0], own[:, 1]
         other = jnp.where(major, second, first).astype(bf16)
         own = jnp.where(major, first, second)
         own = own + mirrored(other).astype(jnp.float32)
-        other = jnp.where(upper_strip == 0, own[1], own[0]).astype(bf16)
-        own = jnp.where(upper_strip == 0, own[0], own[1])
-        own = own + stripped(other, 2).astype(jnp.float32)
+        place = column if lower else upper_strip
+        other = jnp.where(place == 0, own[1], own[0]).astype(bf16)
+        own = jnp.where(place == 0, own[0], own[1])
+        own = own + stripped(other, sum_step).astype(jnp.float32)
         sums.append(own + partnered(own.astype(bf16)).astype(jnp.float32))
     factor = 1.0 / math.sqrt(2.0 * micros * tile_rows * strips * tile_width)
     other = mirrored(jnp.where(major, sums[1], sums[0]).astype(bf16)).astype(jnp.float32)

time: 92 us -> 85.7 us (0.932)
  starting transfers between devices: 33.4 us -> 22.4 us
  waiting for transfers between devices: 38.8 us -> 44.3 us
    ppermute x5 -> x6, starting transfers between devices: 10.2 us -> 3.87 us  [stripped(): return lax.ppermute(block, AXES, route)]
    ppermute x8, waiting for transfers between devices: 15.5 us -> 20.3 us  [permuted(): return lax.ppermute(block, AXES, route)]
    ppermute x4, starting transfers between devices: 9.04 us -> 6.39 us  [the longest x2 6.12 us: rims(): lax.ppermute(jnp.where(even, last, first), 'strip', [(z, z ^ 1) for z in...]
    ppermute x8, starting transfers between devices: 13 us -> 11.1 us  [permuted(): return lax.ppermute(block, AXES, route)]
    ppermute x7, waiting for transfers between devices: 0.51 us -> 2.17 us  [mirrored(): return lax.ppermute(block, 'mirror', [(0, 1), (1, 0)])]
    ppermute x5 -> x6, waiting for transfers between devices: 19.3 us -> 18 us  [stripped(): return lax.ppermute(block, AXES, route)]
    another operation x5 -> x11, other arithmetic: 0.14 us -> 1.34 us  [the longest x4 0.09 us: folded(): block = jnp.stack([side(pres, lower, k) for k in range(count)])[None]]
    convert_element_type x1, other arithmetic: 1.13 us -> 0.05 us  [folded(): own_data = jnp.stack([masks_int.astype(bf16), inputs_all])]
  transfers between devices with their start and end apart: 24 -> 25, of which waited for: 13 -> 15; matrix products, arithmetic and copies ran while one was open for 13% -> 14% of each run, Pallas kernels for 0% -> 0%
where the time goes in v3:
time: 85.7 us; the launch traced here: 85.4 us
  waiting for transfers between devices  44.3 us (52%)
  starting transfers between devices  22.4 us (26%)
  other arithmetic  7.29 us (9%)
  local copies, waits for them, and re-layouts  5.48 us (6%)
  matrix products  4.27 us (5%)
  between operations  1.74 us (2%)
    ppermute x8, waiting for transfers between devices, permuted(): return lax.ppermute(block, AXES, route)  20.3 us
    ppermute x6, waiting for transfers between devices, stripped(): return lax.ppermute(block, AXES, route)  18 us
    ppermute x8, starting transfers between devices, permuted(): return lax.ppermute(block, AXES, route)  11.1 us
    ppermute x2, starting transfers between devices, rims(): lax.ppermute(jnp.where(even, last, first), 'strip', [(z, z ^ 1) for z in...  6.12 us
    ppermute x6, starting transfers between devices, stripped(): return lax.ppermute(block, AXES, route)  3.87 us
    ppermute x2, waiting for transfers between devices, rims(): lax.ppermute(jnp.where(even, last, first), 'strip', [(z, z ^ 1) for z in...  3.78 us
    unnamed x71, local copies, waits for them, and re-layouts  3.32 us
    dot_general x8, matrix products, layer_back(): branch = jnp.dot(patch, kernel, preferred_element_type=jnp.float32)  3.12 us
  transfers between devices with their start and end apart: 25, of which 15 were waited for; matrix products, arithmetic and copies ran while one was open for 14% of the time, Pallas kernels for 0%

profile of v3, /device:TPU:0, one launch (start us, length us, event | category | flops | bytes accessed | tf_op | source)
XLA Modules:
  0.0 85.4 jit_solution(9829687726591109075)
XLA Ops:
  0.6 1.6 %slice_bitcast_fusion.8 = bf16[2,8,16,256]{3,2,1,0:T(8,128)(2,1)} fusion(bf16[1,1,4,8,16,256]{5,4,3,2,1,0:T(8,128)(2,1)} %param.5), kind=kLoop, calls=%fused_computation.267 | loop fusion | bytes 262144 | tf_op jit(solution)/shard_map/slice | solution.py:224
  2.8 1.0 %copy.69 = bf16[1,1,4,8,16,256]{5,4,2,3,1,0:T(8,128)(2,1)S(1)} copy(bf16[1,1,4,8,16,256]{5,4,3,2,1,0:T(8,128)(2,1)} %param.5) | data formatting | bytes 524288 | tf_op args[1]
  3.8 1.1 %copy_convert_fusion = bf16[1,1,4,8,16,256]{5,4,2,3,1,0:T(8,128)(2,1)S(1)} fusion(s32[1,1,4,8,16,256]{5,4,3,2,1,0:T(8,128)} %param.6), kind=kLoop, calls=%fused_computation.58 | loop fusion | flops 131072 | bytes 786432 | tf_op jit(solution)/shard_map/convert.4
  5.0 0.8 fusion.61
  6.3 0.7 copy.28
  7.7 1.1 %maximum_select_fusion.1 = (bf16[2,2,8,16,256]{4,3,1,2,0:T(8,128)(2,1)S(1)}, bf16[2,2,8,16,256]{4,3,1,2,0:T(8,128)(2,1)S(1)}) fusion(bf16[2,2,8,16,256]{4,3,1,2,0:T(8,128)(2,1)} %collective-permute-done, bf16[1,2,8,16,256]{4,3,1,2,0:T(8,128)(2,1)S(1)} %get-tuple-element.36, pred[]{:T(512)S(6)} %eq.21, bf16[1,4,8,16,256]{4,3,1,2,0:T(8,128)(2,1)S(1)} %bitcast.289, ...), kind=kLoop, calls=%fused_computation.111 | loop fusion | flops 1310720 | bytes 1572865 | tf_op jit(solution)/shard_map/jit(_where)/select_n | solution.py:214
  9.0 4.1 %collective-permute-start.2 = (bf16[2,2,4,16,256]{4,3,1,2,0:T(8,128)(2,1)S(1)}, bf16[2,2,4,16,256]{4,3,1,2,0:T(8,128)(2,1)S(1)}, u32[]{:S(2)}, u32[]{:S(2)}) collective-permute-start(bf16[2,2,4,16,256]{4,3,1,2,0:T(8,128)(2,1)S(1)} %get-tuple-element.31), channel_id=1, source_target_pairs={{0,2},{2,0},{4,6},{6,4},{1,3},{3,1},{5,7},{7,5},{8,10},{10,8},{12,... | collective-permute-start | bytes 393224 | tf_op jit(solution)/shard_map/ppermute | solution.py:183
  13.2 2.4 %collective-permute-start.6 = (bf16[2,2,8,16,256]{4,3,1,2,0:T(8,128)(2,1)S(1)}, bf16[2,2,8,16,256]{4,3,1,2,0:T(8,128)(2,1)S(1)}, u32[]{:S(2)}, u32[]{:S(2)}) collective-permute-start(bf16[2,2,8,16,256]{4,3,1,2,0:T(8,128)(2,1)S(1)} %get-tuple-element.33), channel_id=1, source_target_pairs={{0,24},{2,26},{4,28},{6,30},{1,25},{3,27},{5,29},{7,31},{8,16},{10... | collective-permute-start | bytes 786440 | tf_op jit(solution)/shard_map/ppermute | solution.py:154
  15.6 1.3 %collective-permute-done.2 = bf16[2,2,4,16,256]{4,3,1,2,0:T(8,128)(2,1)S(1)} collective-permute-done((bf16[2,2,4,16,256]{4,3,1,2,0:T(8,128)(2,1)S(1)}, bf16[2,2,4,16,256]{4,3,1,2,0:T(8,128)(2,1)S(1)}, u32[]{:S(2)}, u32[]{:S(2)}) %collective-permute-start.2) | collective-permute-done | bytes 131104 | tf_op jit(solution)/shard_map/ppermute | solution.py:183
  17.6 4.5 %collective-permute-done.6 = bf16[2,2,8,16,256]{4,3,1,2,0:T(8,128)(2,1)S(1)} collective-permute-done((bf16[2,2,8,16,256]{4,3,1,2,0:T(8,128)(2,1)S(1)}, bf16[2,2,8,16,256]{4,3,1,2,0:T(8,128)(2,1)S(1)}, u32[]{:S(2)}, u32[]{:S(2)}) %collective-permute-start.6) | collective-permute-done | bytes 262176 | tf_op jit(solution)/shard_map/ppermute | solution.py:154
  22.2 2.0 %collective-permute-start.9 = (bf16[2,4,16,256]{3,2,1,0:T(8,128)(2,1)S(1)}, bf16[2,4,16,256]{3,2,1,0:T(8,128)(2,1)S(1)}, u32[]{:S(2)}, u32[]{:S(2)}) collective-permute-start(bf16[2,4,16,256]{3,2,1,0:T(8,128)(2,1)S(1)} %get-tuple-element.57), channel_id=1, source_target_pairs={{0,2},{2,0},{4,6},{6,4},{1,3},{3,1},{5,7},{7,5},{8,10},{10,8},{12,... | collective-permute-start | bytes 196616 | tf_op jit(solution)/shard_map/ppermute | solution.py:183
  24.2 2.5 %collective-permute-done.9 = bf16[2,4,16,256]{3,2,1,0:T(8,128)(2,1)S(1)} collective-permute-done((bf16[2,4,16,256]{3,2,1,0:T(8,128)(2,1)S(1)}, bf16[2,4,16,256]{3,2,1,0:T(8,128)(2,1)S(1)}, u32[]{:S(2)}, u32[]{:S(2)}) %collective-permute-start.9) | collective-permute-done | bytes 65568 | tf_op jit(solution)/shard_map/ppermute | solution.py:183
  26.8 1.6 %collective-permute-start.19 = (bf16[2,10,16,256]{3,2,0,1:T(8,128)(2,1)S(1)}, bf16[2,10,16,256]{3,2,0,1:T(8,128)(2,1)S(1)}, u32[]{:S(2)}, u32[]{:S(2)}) collective-permute-start(bf16[2,10,16,256]{3,2,0,1:T(8,128)(2,1)S(1)} %get-tuple-element.47), channel_id=1, source_target_pairs={{0,4},{2,6},{4,0},{6,2},{1,5},{3,7},{5,1},{7,3},{8,12},{10,14},{12... | collective-permute-start | bytes 491528 | tf_op jit(solution)/shard_map/ppermute | solution.py:172
  28.9 7.6 %collective-permute-done.19 = bf16[2,10,16,256]{3,2,0,1:T(8,128)(2,1)S(1)} collective-permute-done((bf16[2,10,16,256]{3,2,0,1:T(8,128)(2,1)S(1)}, bf16[2,10,16,256]{3,2,0,1:T(8,128)(2,1)S(1)}, u32[]{:S(2)}, u32[]{:S(2)}) %collective-permute-start.19) | collective-permute-done | bytes 163872 | tf_op jit(solution)/shard_map/ppermute | solution.py:172
  38.5 1.6 %collective-permute-start.5 = (bf16[14,16,256]{2,1,0:T(8,128)(2,1)S(1)}, bf16[14,16,256]{2,1,0:T(8,128)(2,1)S(1)}, u32[]{:S(2)}, u32[]{:S(2)}) collective-permute-start(bf16[14,16,256]{2,1,0:T(8,128)(2,1)S(1)} %fusion.23), channel_id=1, source_target_pairs={{0,8},{2,10},{4,12},{6,14},{1,9},{3,11},{5,13},{7,15},{8,0},{10,2}... | collective-permute-start | bytes 344072 | tf_op jit(solution)/shard_map/ppermute | solution.py:154
  41.2 3.1 %collective-permute-done.5 = bf16[14,16,256]{2,1,0:T(8,128)(2,1)S(1)} collective-permute-done((bf16[14,16,256]{2,1,0:T(8,128)(2,1)S(1)}, bf16[14,16,256]{2,1,0:T(8,128)(2,1)S(1)}, u32[]{:S(2)}, u32[]{:S(2)}) %collective-permute-start.5) | collective-permute-done | bytes 114720 | tf_op jit(solution)/shard_map/ppermute | solution.py:154
  44.4 1.7 %collective-permute-done.4 = bf16[14,16,256]{2,1,0:T(8,128)(2,1)S(1)} collective-permute-done((bf16[14,16,256]{2,1,0:T(8,128)(2,1)S(1)}, bf16[14,16,256]{2,1,0:T(8,128)(2,1)S(1)}, u32[]{:S(2)}, u32[]{:S(2)}) %collective-permute-start.4) | collective-permute-done | bytes 114720 | tf_op jit(solution)/shard_map/ppermute | solution.py:154
  48.2 1.6 %collective-permute-start.10 = (bf16[10,16,256]{2,1,0:T(8,128)(2,1)S(1)}, bf16[10,16,256]{2,1,0:T(8,128)(2,1)S(1)}, u32[]{:S(2)}, u32[]{:S(2)}) collective-permute-start(bf16[10,16,256]{2,1,0:T(8,128)(2,1)S(1)} %fusion.38), channel_id=1, source_target_pairs={{0,8},{2,10},{4,12},{6,14},{1,9},{3,11},{5,13},{7,15},{8,0},{10,2}... | collective-permute-start | bytes 245768 | tf_op jit(solution)/shard_map/ppermute | solution.py:154
  51.0 2.4 %collective-permute-done.10 = bf16[10,16,256]{2,1,0:T(8,128)(2,1)S(1)} collective-permute-done((bf16[10,16,256]{2,1,0:T(8,128)(2,1)S(1)}, bf16[10,16,256]{2,1,0:T(8,128)(2,1)S(1)}, u32[]{:S(2)}, u32[]{:S(2)}) %collective-permute-start.10) | collective-permute-done | bytes 81952 | tf_op jit(solution)/shard_map/ppermute | solution.py:154
  53.5 1.4 %collective-permute-done.11 = bf16[10,16,256]{2,1,0:T(8,128)(2,1)S(1)} collective-permute-done((bf16[10,16,256]{2,1,0:T(8,128)(2,1)S(1)}, bf16[10,16,256]{2,1,0:T(8,128)(2,1)S(1)}, u32[]{:S(2)}, u32[]{:S(2)}) %collective-permute-start.11) | collective-permute-done | bytes 81952 | tf_op jit(solution)/shard_map/ppermute | solution.py:154
  56.1 1.6 %collective-permute-start.12 = (bf16[2,8,16,256]{3,2,1,0:T(8,128)(2,1)S(1)}, bf16[2,8,16,256]{3,2,1,0:T(8,128)(2,1)S(1)}, u32[]{:S(2)}, u32[]{:S(2)}) collective-permute-start(bf16[2,8,16,256]{3,2,1,0:T(8,128)(2,1)S(1)} %pad_maximum_fusion.10), channel_id=1, source_target_pairs={{0,24},{2,26},{4,28},{6,30},{1,25},{3,27},{5,29},{7,31},{8,16},{10... | collective-permute-start | bytes 393224 | tf_op jit(solution)/shard_map/ppermute | solution.py:154
  57.7 0.6 convolution_bitcast_fusion.1
  58.6 3.4 %collective-permute-done.20 = bf16[2,8,16,256]{3,2,1,0:T(8,128)(2,1)S(1)} collective-permute-done((bf16[2,8,16,256]{3,2,1,0:T(8,128)(2,1)S(1)}, bf16[2,8,16,256]{3,2,1,0:T(8,128)(2,1)S(1)}, u32[]{:S(2)}, u32[]{:S(2)}) %collective-permute-start.20) | collective-permute-done | bytes 131104 | tf_op jit(solution)/shard_map/ppermute | solution.py:172
  63.3 1.1 %collective-permute-done.21 = bf16[2,288,256]{2,1,0:T(8,128)(2,1)S(1)} collective-permute-done((bf16[2,288,256]{2,1,0:T(8,128)(2,1)S(1)}, bf16[2,288,256]{2,1,0:T(8,128)(2,1)S(1)}, u32[]{:S(2)}, u32[]{:S(2)}) %collective-permute-start.21) | collective-permute-done | bytes 294944 | tf_op jit(solution)/shard_map/ppermute | solution.py:157
  64.5 1.4 %collective-permute-start.22 = (bf16[288,256]{1,0:T(8,128)(2,1)S(1)}, bf16[288,256]{1,0:T(8,128)(2,1)S(1)}, u32[]{:S(2)}, u32[]{:S(2)}) collective-permute-start(bf16[288,256]{1,0:T(8,128)(2,1)S(1)} %fusion.80), channel_id=1, source_target_pairs={{0,2},{2,0},{4,6},{6,4},{1,3},{3,1},{5,7},{7,5},{8,10},{10,8},{12,... | collective-permute-start | bytes 442376 | tf_op jit(solution)/shard_map/ppermute | solution.py:172
  65.9 7.0 %collective-permute-done.17 = bf16[288,256]{1,0:T(8,128)(2,1)S(1)} collective-permute-done((bf16[288,256]{1,0:T(8,128)(2,1)S(1)}, bf16[288,256]{1,0:T(8,128)(2,1)S(1)}, u32[]{:S(2)}, u32[]{:S(2)}) %collective-permute-start.17) | collective-permute-done | bytes 147488 | tf_op jit(solution)/shard_map/ppermute | solution.py:172
  73.0 1.2 %collective-permute-start.18 = (bf16[288,256]{1,0:T(8,128)(2,1)S(1)}, bf16[288,256]{1,0:T(8,128)(2,1)S(1)}, u32[]{:S(2)}, u32[]{:S(2)}) collective-permute-start(bf16[288,256]{1,0:T(8,128)(2,1)S(1)} %get-tuple-element.4), channel_id=1, source_target_pairs={{0,25},{2,27},{4,29},{6,31},{1,24},{3,26},{5,28},{7,30},{8,17},{10... | collective-permute-start | bytes 442376 | tf_op jit(solution)/shard_map/ppermute | solution.py:154
  74.2 1.6 %collective-permute-start.23 = (bf16[288,256]{1,0:T(8,128)(2,1)S(1)}, bf16[288,256]{1,0:T(8,128)(2,1)S(1)}, u32[]{:S(2)}, u32[]{:S(2)}) collective-permute-start(bf16[288,256]{1,0:T(8,128)(2,1)S(1)} %get-tuple-element.2), channel_id=1, source_target_pairs={{0,25},{2,27},{4,29},{6,31},{1,24},{3,26},{5,28},{7,30},{8,17},{10... | collective-permute-start | bytes 442376 | tf_op jit(solution)/shard_map/ppermute | solution.py:154
  75.9 4.0 %collective-permute-done.18 = bf16[288,256]{1,0:T(8,128)(2,1)S(1)} collective-permute-done((bf16[288,256]{1,0:T(8,128)(2,1)S(1)}, bf16[288,256]{1,0:T(8,128)(2,1)S(1)}, u32[]{:S(2)}, u32[]{:S(2)}) %collective-permute-start.18) | collective-permute-done | bytes 147488 | tf_op jit(solution)/shard_map/ppermute | solution.py:154
  79.9 3.2 %collective-permute-done.23 = bf16[288,256]{1,0:T(8,128)(2,1)S(1)} collective-permute-done((bf16[288,256]{1,0:T(8,128)(2,1)S(1)}, bf16[288,256]{1,0:T(8,128)(2,1)S(1)}, u32[]{:S(2)}, u32[]{:S(2)}) %collective-permute-start.23) | collective-permute-done | bytes 147488 | tf_op jit(solution)/shard_map/ppermute | solution.py:154
  83.3 0.7 maximum_bitcast_fusion
  84.6 0.9 %fusion.43 = f32[1,1,576,256]{3,2,1,0:T(8,128)} fusion(f32[1,1,288,256]{3,2,1,0:T(8,128)S(1)} %bitcast_convert_fusion, f32[1,1,288,256]{3,2,1,0:T(8,128)S(1)} %get-tuple-element.18, pred[]{:T(512)S(6)} %eq.21), kind=kLoop, calls=%fused_computation.50 | loop fusion | flops 589824 | bytes 1179649 | tf_op jit(solution)/shard_map/mul | solution.py:332
  (173 shorter events, 13.1 us)
Async XLA Ops:
  0.6 4.2 %copy-start = (s32[1,1,4,8,16,256]{5,4,3,2,1,0:T(8,128)S(1)}, s32[1,1,4,8,16,256]{5,4,3,2,1,0:T(8,128)}, u32[]{:S(2)}) copy-start(s32[1,1,4,8,16,256]{5,4,3,2,1,0:T(8,128)} %param.6) | copy-start | bytes 1572868
  2.3 4.9 %collective-permute-start.7 = (bf16[2,8,16,256]{3,2,1,0:T(8,128)(2,1)}, bf16[2,8,16,256]{3,2,1,0:T(8,128)(2,1)S(1)}, u32[]{:S(2)}, u32[]{:S(2)}) collective-permute-start(bf16[2,8,16,256]{3,2,1,0:T(8,128)(2,1)} %slice_bitcast_fusion.8), channel_id=1, source_target_pairs={{0,1},{1,0},{2,3},{3,2},{4,5},{5,4},{6,7},{7,6},{8,9},{9,8},{10,11... | collective-permute-start | bytes 393224 | tf_op jit(solution)/shard_map/ppermute | solution.py:157
  2.8 2.2 %copy-start.3 = (bf16[1,4,8,16,256]{4,3,2,1,0:T(8,128)(2,1)S(1)}, bf16[1,4,8,16,256]{4,3,2,1,0:T(8,128)(2,1)}, u32[]{:S(2)}) copy-start(bf16[1,4,8,16,256]{4,3,2,1,0:T(8,128)(2,1)} %param.4) | copy-start | bytes 786436
  4.9 1.4 %copy-start.1 = (bf16[1,1,3,3,256,256]{5,4,3,2,1,0:T(8,128)(2,1)S(1)}, bf16[1,1,3,3,256,256]{5,4,3,2,1,0:T(8,128)(2,1)}, u32[]{:S(2)}) copy-start(bf16[1,1,3,3,256,256]{5,4,3,2,1,0:T(8,128)(2,1)} %param.7) | copy-start | bytes 3538948
  5.8 1.3 %copy-start.2 = (bf16[1,1,4,8,16,256]{5,4,3,2,1,0:T(8,128)(2,1)S(1)}, bf16[1,1,4,8,16,256]{5,4,3,2,1,0:T(8,128)(2,1)}, u32[]{:S(2)}) copy-start(bf16[1,1,4,8,16,256]{5,4,3,2,1,0:T(8,128)(2,1)} %param.5) | copy-start | bytes 786436
  5.8 1.9 %collective-permute-start = (bf16[2,2,8,16,256]{4,3,1,2,0:T(8,128)(2,1)}, bf16[2,2,8,16,256]{4,3,1,2,0:T(8,128)(2,1)}, u32[]{:S(2)}, u32[]{:S(2)}) collective-permute-start(bf16[2,2,8,16,256]{4,3,1,2,0:T(8,128)(2,1)} %fusion.61), channel_id=1, source_target_pairs={{0,1},{1,0},{2,3},{3,2},{4,5},{5,4},{6,7},{7,6},{8,9},{9,8},{10,11... | collective-permute-start | bytes 786440 | tf_op jit(solution)/shard_map/ppermute | solution.py:157
  7.0 30.8 %collective-permute-start.3 = (bf16[2304,256]{1,0:T(8,128)(2,1)S(1)}, bf16[2304,256]{1,0:T(8,128)(2,1)S(1)}, u32[]{:S(2)}, u32[]{:S(2)}) collective-permute-start(bf16[2304,256]{1,0:T(8,128)(2,1)S(1)} %bitcast.277), channel_id=1, source_target_pairs={{0,1},{1,0},{2,3},{3,2},{4,5},{5,4},{6,7},{7,6},{8,9},{9,8},{10,11... | collective-permute-start | bytes 3538952 | tf_op jit(solution)/shard_map/ppermute | solution.py:157
  8.8 6.8 %collective-permute-start.1 = (bf16[2,2,4,16,256]{4,3,1,2,0:T(8,128)(2,1)S(1)}, bf16[2,2,4,16,256]{4,3,1,2,0:T(8,128)(2,1)S(1)}, u32[]{:S(2)}, u32[]{:S(2)}) collective-permute-start(bf16[2,2,4,16,256]{4,3,1,2,0:T(8,128)(2,1)S(1)} %get-tuple-element.30), channel_id=1, source_target_pairs={{0,1},{2,4},{4,2},{6,7},{1,0},{3,5},{5,3},{7,6},{8,9},{10,12},{12,... | collective-permute-start | bytes 393224 | tf_op jit(solution)/shard_map/ppermute | solution.py:194
  9.0 7.9 %collective-permute-start.2 = (bf16[2,2,4,16,256]{4,3,1,2,0:T(8,128)(2,1)S(1)}, bf16[2,2,4,16,256]{4,3,1,2,0:T(8,128)(2,1)S(1)}, u32[]{:S(2)}, u32[]{:S(2)}) collective-permute-start(bf16[2,2,4,16,256]{4,3,1,2,0:T(8,128)(2,1)S(1)} %get-tuple-element.31), channel_id=1, source_target_pairs={{0,2},{2,0},{4,6},{6,4},{1,3},{3,1},{5,7},{7,5},{8,10},{10,8},{12,... | collective-permute-start | bytes 393224 | tf_op jit(solution)/shard_map/ppermute | solution.py:183
  13.2 8.9 %collective-permute-start.6 = (bf16[2,2,8,16,256]{4,3,1,2,0:T(8,128)(2,1)S(1)}, bf16[2,2,8,16,256]{4,3,1,2,0:T(8,128)(2,1)S(1)}, u32[]{:S(2)}, u32[]{:S(2)}) collective-permute-start(bf16[2,2,8,16,256]{4,3,1,2,0:T(8,128)(2,1)S(1)} %get-tuple-element.33), channel_id=1, source_target_pairs={{0,24},{2,26},{4,28},{6,30},{1,25},{3,27},{5,29},{7,31},{8,16},{10... | collective-permute-start | bytes 786440 | tf_op jit(solution)/shard_map/ppermute | solution.py:154
  22.1 2.1 %collective-permute-start.8 = (bf16[2,4,16,256]{3,2,1,0:T(8,128)(2,1)S(1)}, bf16[2,4,16,256]{3,2,1,0:T(8,128)(2,1)S(1)}, u32[]{:S(2)}, u32[]{:S(2)}) collective-permute-start(bf16[2,4,16,256]{3,2,1,0:T(8,128)(2,1)S(1)} %get-tuple-element.56), channel_id=1, source_target_pairs={{0,1},{2,4},{4,2},{6,7},{1,0},{3,5},{5,3},{7,6},{8,9},{10,12},{12,... | collective-permute-start | bytes 196616 | tf_op jit(solution)/shard_map/ppermute | solution.py:194
  22.2 4.5 %collective-permute-start.9 = (bf16[2,4,16,256]{3,2,1,0:T(8,128)(2,1)S(1)}, bf16[2,4,16,256]{3,2,1,0:T(8,128)(2,1)S(1)}, u32[]{:S(2)}, u32[]{:S(2)}) collective-permute-start(bf16[2,4,16,256]{3,2,1,0:T(8,128)(2,1)S(1)} %get-tuple-element.57), channel_id=1, source_target_pairs={{0,2},{2,0},{4,6},{6,4},{1,3},{3,1},{5,7},{7,5},{8,10},{10,8},{12,... | collective-permute-start | bytes 196616 | tf_op jit(solution)/shard_map/ppermute | solution.py:183
  26.8 9.7 %collective-permute-start.19 = (bf16[2,10,16,256]{3,2,0,1:T(8,128)(2,1)S(1)}, bf16[2,10,16,256]{3,2,0,1:T(8,128)(2,1)S(1)}, u32[]{:S(2)}, u32[]{:S(2)}) collective-permute-start(bf16[2,10,16,256]{3,2,0,1:T(8,128)(2,1)S(1)} %get-tuple-element.47), channel_id=1, source_target_pairs={{0,4},{2,6},{4,0},{6,2},{1,5},{3,7},{5,1},{7,3},{8,12},{10,14},{12... | collective-permute-start | bytes 491528 | tf_op jit(solution)/shard_map/ppermute | solution.py:172
  28.4 8.8 %collective-permute-start.14 = (bf16[2,10,16,256]{3,2,1,0:T(8,128)(2,1)S(1)}, bf16[2,10,16,256]{3,2,1,0:T(8,128)(2,1)S(1)}, u32[]{:S(2)}, u32[]{:S(2)}) collective-permute-start(bf16[2,10,16,256]{3,2,1,0:T(8,128)(2,1)S(1)} %get-tuple-element.49), channel_id=1, source_target_pairs={{0,2},{2,0},{4,6},{6,4},{1,3},{3,1},{5,7},{7,5},{8,10},{10,8},{12,... | collective-permute-start | bytes 491528 | tf_op jit(solution)/shard_map/ppermute | solution.py:172
  38.5 5.9 %collective-permute-start.5 = (bf16[14,16,256]{2,1,0:T(8,128)(2,1)S(1)}, bf16[14,16,256]{2,1,0:T(8,128)(2,1)S(1)}, u32[]{:S(2)}, u32[]{:S(2)}) collective-permute-start(bf16[14,16,256]{2,1,0:T(8,128)(2,1)S(1)} %fusion.23), channel_id=1, source_target_pairs={{0,8},{2,10},{4,12},{6,14},{1,9},{3,11},{5,13},{7,15},{8,0},{10,2}... | collective-permute-start | bytes 344072 | tf_op jit(solution)/shard_map/ppermute | solution.py:154
  40.5 5.6 %collective-permute-start.4 = (bf16[14,16,256]{2,1,0:T(8,128)(2,1)S(1)}, bf16[14,16,256]{2,1,0:T(8,128)(2,1)S(1)}, u32[]{:S(2)}, u32[]{:S(2)}) collective-permute-start(bf16[14,16,256]{2,1,0:T(8,128)(2,1)S(1)} %fusion.26), channel_id=1, source_target_pairs={{0,8},{2,10},{4,12},{6,14},{1,9},{3,11},{5,13},{7,15},{8,0},{10,2}... | collective-permute-start | bytes 344072 | tf_op jit(solution)/shard_map/ppermute | solution.py:154
  48.2 5.3 %collective-permute-start.10 = (bf16[10,16,256]{2,1,0:T(8,128)(2,1)S(1)}, bf16[10,16,256]{2,1,0:T(8,128)(2,1)S(1)}, u32[]{:S(2)}, u32[]{:S(2)}) collective-permute-start(bf16[10,16,256]{2,1,0:T(8,128)(2,1)S(1)} %fusion.38), channel_id=1, source_target_pairs={{0,8},{2,10},{4,12},{6,14},{1,9},{3,11},{5,13},{7,15},{8,0},{10,2}... | collective-permute-start | bytes 245768 | tf_op jit(solution)/shard_map/ppermute | solution.py:154
  50.3 4.5 %collective-permute-start.11 = (bf16[10,16,256]{2,1,0:T(8,128)(2,1)S(1)}, bf16[10,16,256]{2,1,0:T(8,128)(2,1)S(1)}, u32[]{:S(2)}, u32[]{:S(2)}) collective-permute-start(bf16[10,16,256]{2,1,0:T(8,128)(2,1)S(1)} %fusion.35), channel_id=1, source_target_pairs={{0,8},{2,10},{4,12},{6,14},{1,9},{3,11},{5,13},{7,15},{8,0},{10,2}... | collective-permute-start | bytes 245768 | tf_op jit(solution)/shard_map/ppermute | solution.py:154
  51.0 6.7 %collective-permute-start.15 = (bf16[2,8,16,256]{3,2,1,0:T(8,128)(2,1)S(1)}, bf16[2,8,16,256]{3,2,1,0:T(8,128)(2,1)S(1)}, u32[]{:S(2)}, u32[]{:S(2)}) collective-permute-start(bf16[2,8,16,256]{3,2,1,0:T(8,128)(2,1)S(1)} %get-tuple-element.53), channel_id=1, source_target_pairs={{0,2},{2,0},{4,6},{6,4},{1,3},{3,1},{5,7},{7,5},{8,10},{10,8},{12,... | collective-permute-start | bytes 393224 | tf_op jit(solution)/shard_map/ppermute | solution.py:172
  55.1 7.0 %collective-permute-start.20 = (bf16[2,8,16,256]{3,2,1,0:T(8,128)(2,1)S(1)}, bf16[2,8,16,256]{3,2,1,0:T(8,128)(2,1)S(1)}, u32[]{:S(2)}, u32[]{:S(2)}) collective-permute-start(bf16[2,8,16,256]{3,2,1,0:T(8,128)(2,1)S(1)} %get-tuple-element.51), channel_id=1, source_target_pairs={{0,4},{2,6},{4,0},{6,2},{1,5},{3,7},{5,1},{7,3},{8,12},{10,14},{12... | collective-permute-start | bytes 393224 | tf_op jit(solution)/shard_map/ppermute | solution.py:172
  56.1 19.7 %collective-permute-start.12 = (bf16[2,8,16,256]{3,2,1,0:T(8,128)(2,1)S(1)}, bf16[2,8,16,256]{3,2,1,0:T(8,128)(2,1)S(1)}, u32[]{:S(2)}, u32[]{:S(2)}) collective-permute-start(bf16[2,8,16,256]{3,2,1,0:T(8,128)(2,1)S(1)} %pad_maximum_fusion.10), channel_id=1, source_target_pairs={{0,24},{2,26},{4,28},{6,30},{1,25},{3,27},{5,29},{7,31},{8,16},{10... | collective-permute-start | bytes 393224 | tf_op jit(solution)/shard_map/ppermute | solution.py:154
  58.5 4.3 %collective-permute-start.16 = (bf16[2,288,256]{2,1,0:T(8,128)(2,1)S(1)}, bf16[2,288,256]{2,1,0:T(8,128)(2,1)S(1)}, u32[]{:S(2)}, u32[]{:S(2)}) collective-permute-start(bf16[2,288,256]{2,1,0:T(8,128)(2,1)S(1)} %fusion.44), channel_id=1, source_target_pairs={{0,1},{1,0},{2,3},{3,2},{4,5},{5,4},{6,7},{7,6},{8,9},{9,8},{10,11... | collective-permute-start | bytes 884744 | tf_op jit(solution)/shard_map/ppermute | solution.py:157
  62.8 1.6 %collective-permute-start.21 = (bf16[2,288,256]{2,1,0:T(8,128)(2,1)S(1)}, bf16[2,288,256]{2,1,0:T(8,128)(2,1)S(1)}, u32[]{:S(2)}, u32[]{:S(2)}) collective-permute-start(bf16[2,288,256]{2,1,0:T(8,128)(2,1)S(1)} %fusion.45), channel_id=1, source_target_pairs={{0,1},{1,0},{2,3},{3,2},{4,5},{5,4},{6,7},{7,6},{8,9},{9,8},{10,11... | collective-permute-start | bytes 884744 | tf_op jit(solution)/shard_map/ppermute | solution.py:157
  63.0 9.9 %collective-permute-start.17 = (bf16[288,256]{1,0:T(8,128)(2,1)S(1)}, bf16[288,256]{1,0:T(8,128)(2,1)S(1)}, u32[]{:S(2)}, u32[]{:S(2)}) collective-permute-start(bf16[288,256]{1,0:T(8,128)(2,1)S(1)} %fusion.79), channel_id=1, source_target_pairs={{0,4},{2,6},{4,0},{6,2},{1,5},{3,7},{5,1},{7,3},{8,12},{10,14},{12... | collective-permute-start | bytes 442376 | tf_op jit(solution)/shard_map/ppermute | solution.py:172
  64.5 9.6 %collective-permute-start.22 = (bf16[288,256]{1,0:T(8,128)(2,1)S(1)}, bf16[288,256]{1,0:T(8,128)(2,1)S(1)}, u32[]{:S(2)}, u32[]{:S(2)}) collective-permute-start(bf16[288,256]{1,0:T(8,128)(2,1)S(1)} %fusion.80), channel_id=1, source_target_pairs={{0,2},{2,0},{4,6},{6,4},{1,3},{3,1},{5,7},{7,5},{8,10},{10,8},{12,... | collective-permute-start | bytes 442376 | tf_op jit(solution)/shard_map/ppermute | solution.py:172
  73.0 6.9 %collective-permute-start.18 = (bf16[288,256]{1,0:T(8,128)(2,1)S(1)}, bf16[288,256]{1,0:T(8,128)(2,1)S(1)}, u32[]{:S(2)}, u32[]{:S(2)}) collective-permute-start(bf16[288,256]{1,0:T(8,128)(2,1)S(1)} %get-tuple-element.4), channel_id=1, source_target_pairs={{0,25},{2,27},{4,29},{6,31},{1,24},{3,26},{5,28},{7,30},{8,17},{10... | collective-permute-start | bytes 442376 | tf_op jit(solution)/shard_map/ppermute | solution.py:154
  74.2 8.9 %collective-permute-start.23 = (bf16[288,256]{1,0:T(8,128)(2,1)S(1)}, bf16[288,256]{1,0:T(8,128)(2,1)S(1)}, u32[]{:S(2)}, u32[]{:S(2)}) collective-permute-start(bf16[288,256]{1,0:T(8,128)(2,1)S(1)} %get-tuple-element.2), channel_id=1, source_target_pairs={{0,25},{2,27},{4,29},{6,31},{1,24},{3,26},{5,28},{7,30},{8,17},{10... | collective-permute-start | bytes 442376 | tf_op jit(solution)/shard_map/ppermute | solution.py:154
  75.8 7.5 %collective-permute-start.13 = (bf16[2,8,16,256]{3,2,1,0:T(8,128)(2,1)S(1)}, bf16[2,8,16,256]{3,2,1,0:T(8,128)(2,1)S(1)}, u32[]{:S(2)}, u32[]{:S(2)}) collective-permute-start(bf16[2,8,16,256]{3,2,1,0:T(8,128)(2,1)S(1)} %get-tuple-element.27), channel_id=1, source_target_pairs={{0,1},{1,0},{2,3},{3,2},{4,5},{5,4},{6,7},{7,6},{8,9},{9,8},{10,11... | collective-permute-start | bytes 393224 | tf_op jit(solution)/shard_map/ppermute | solution.py:157
  83.1 1.4 %collective-permute-start.24 = (bf16[288,256]{1,0:T(8,128)(2,1)S(1)}, bf16[288,256]{1,0:T(8,128)(2,1)S(1)}, u32[]{:S(2)}, u32[]{:S(2)}) collective-permute-start(bf16[288,256]{1,0:T(8,128)(2,1)S(1)} %get-tuple-element.19), channel_id=1, source_target_pairs={{0,1},{1,0},{2,3},{3,2},{4,5},{5,4},{6,7},{7,6},{8,9},{9,8},{10,11... | collective-permute-start | bytes 442376 | tf_op jit(solution)/shard_map/ppermute | solution.py:157

commit v4 on v3

--- a/solution.py
+++ b/solution.py
@@ -215,10 +215,14 @@
     low, high = rims(mine[:, :, :sections], mine[:, :, tile_rows - sections :])
     top_ext, high_masks = jnp.concatenate([low, mine, high], axis=2)
 
-    own_kernel = jnp.transpose(kernels[0, 0], (0, 1, 3, 2)).reshape(9 * channels, channels)
+    own_kernel = kernels[0, 0]
     other_kernel = mirrored(own_kernel)
-    high_kernel = jnp.where(major, own_kernel, other_kernel)
-    low_kernel = jnp.where(major, other_kernel, own_kernel)
+
+    def transposed(kernel):
+        return jnp.transpose(kernel, (0, 1, 3, 2)).reshape(9 * channels, channels)
+
+    high_kernel = transposed(jnp.where(major, own_kernel, other_kernel))
+    low_kernel = transposed(jnp.where(major, other_kernel, own_kernel))
 
     moved = opposite(jnp.where(major, received, own_data[:, :count]))
     given_inputs = mirrored(inputs_all[count:])
@@ -261,33 +265,32 @@
         return lax.dynamic_slice_in_dim(taps, start, rows), far
 
     def layer_back(grad_out, mask, kernel):
-        height = grad_out.shape[0] - 2
+        height = grad_out.shape[1] - 2
         grad_pre = grad_out * mask
-        padded = jnp.pad(grad_pre, ((0, 0), (1, 1), (0, 0)))
-        patch = unfold(padded, height, tile_width, True)
+        padded = jnp.pad(grad_pre, ((0, 0), (0, 0), (1, 1), (0, 0)))
+        patch = jnp.concatenate([unfold(one, height, tile_width, True) for one in padded])
         branch = jnp.dot(patch, kernel, preferred_element_type=jnp.float32)
-        grad_in = grad_out[1:-1].astype(jnp.float32) + branch.reshape(height, tile_width, channels)
+        centre = grad_out[:, 1:-1]
+        grad_in = centre.astype(jnp.float32) + branch.reshape(centre.shape)
         return grad_in.astype(bf16), grad_pre
 
-    grads = [top_ext[k] for k in range(count)]
-    pres = [[None] * count for _ in range(sections)]
-    outs = [[None] * count for _ in range(sections)]
+    grads = top_ext
     low_masks, inputs = later_rims()
+    pres, outs = [], []
     for position in range(sections):
-        for k in range(count):
-            lower = position >= half
-            trim = position - half if lower else position
-            mask = (low_masks if lower else high_masks)[k]
-            mask = mask[trim : mask.shape[0] - trim]
-            kernel = low_kernel if lower else high_kernel
-            grad_in, grad_pre = layer_back(grads[k], mask, kernel)
-            rim = sections - position
-            pres[position][k] = grad_pre[rim : rim + tile_rows]
-            outs[position][k] = grad_in[rim - 1 : rim - 1 + tile_rows]
-            grads[k] = grad_in
-            if position + 1 < sections and position + 1 != half:
-                hop = hopped(grad_in, position)
-                grads[k] = hop if position else jnp.where(depth == 0, grad_in, hop)
+        lower = position >= half
+        trim = position - half if lower else position
+        mask = low_masks if lower else high_masks
+        mask = mask[:, trim : mask.shape[1] - trim]
+        kernel = low_kernel if lower else high_kernel
+        grad_in, grad_pre = layer_back(grads, mask, kernel)
+        rim = sections - position
+        pres.append(grad_pre[:, rim : rim + tile_rows])
+        outs.append(grad_in[:, rim - 1 : rim - 1 + tile_rows])
+        grads = grad_in
+        if position + 1 < sections and position + 1 != half:
+            hop = hopped(grad_in, position)
+            grads = jnp.where(depth <= position, grad_in, hop) if position + 1 < half else hop
 
     def at_depth(pieces):
         chosen = pieces[0]
@@ -295,10 +298,10 @@
             chosen = jnp.where(depth == q, pieces[q], chosen)
         return chosen
 
-    def side(table, lower, k):
-        return at_depth([table[sections - 1 - q if lower else q][k] for q in range(half)])
-
-    results = [jnp.stack([side(outs, lower, k) for k in range(count)]) for lower in range(2)]
+    def side(table, lower):
+        return at_depth([table[sections - 1 - q if lower else q] for q in range(half)])
+
+    results = [side(outs, lower) for lower in range(2)]
     moved_back = opposite(results[1])
     given = mirrored(jnp.where(major, moved_back, results[0]))
     input_grads = jnp.concatenate([jnp.where(major, results[0], moved_back), given])
@@ -308,7 +311,7 @@
         gather_step, sum_step = (2, 1) if lower else (1, 2)
         tall = across_strips(inputs[lower], gather_step)
         patches = unfolded(tall, lower)
-        block = jnp.stack([side(pres, lower, k) for k in range(count)])
+        block = side(pres, lower)
         block = across_strips(block, gather_step).reshape(-1, channels)
         own = lax.dot_general(
             patches, block, (((0,), (0,)), ((), ())), preferred_element_type=jnp.float32

time: 85.7 us -> 84.8 us (0.989)
  starting transfers between devices: 22.4 us -> 24.7 us
  waiting for transfers between devices: 44.3 us -> 42.8 us
    ppermute x8 -> x6, waiting for transfers between devices: 20.3 us -> 16.4 us  [permuted(): return lax.ppermute(block, AXES, route)]
    ppermute x6, waiting for transfers between devices: 18 us -> 20.4 us  [stripped(): return lax.ppermute(block, AXES, route)]
    ppermute x6, starting transfers between devices: 3.87 us -> 5.51 us  [stripped(): return lax.ppermute(block, AXES, route)]
    select_n x2 -> x4, other arithmetic: 1.32 us -> 0.32 us  [the longest x1 0.16 us: folded(): high_kernel = transposed(jnp.where(major, own_kernel, other_kernel))]
    slice x1, local copies, waits for them, and re-layouts: 1.63 us -> 0.66 us  [folded(): given_inputs = mirrored(inputs_all[count:])]
    ppermute x7, starting transfers between devices: 1.06 us -> 1.96 us  [mirrored(): return lax.ppermute(block, 'mirror', [(0, 1), (1, 0)])]
    dot_general x8 -> x4, matrix products: 3.12 us -> 2.38 us  [layer_back(): branch = jnp.dot(patch, kernel, preferred_element_type=jnp.float32)]
    unnamed x71 -> x72, local copies, waits for them, and re-layouts: 3.32 us -> 3.69 us
  transfers between devices with their start and end apart: 25 -> 23, of which waited for: 15 -> 14; matrix products, arithmetic and copies ran while one was open for 14% -> 11% of each run, Pallas kernels for 0% -> 0%
where the time goes in v4:
time: 84.8 us; the launch traced here: 84.6 us
  waiting for transfers between devices  42.8 us (50%)
  starting transfers between devices  24.7 us (29%)
  other arithmetic  6.66 us (8%)
  local copies, waits for them, and re-layouts  5.17 us (6%)
  matrix products  3.53 us (4%)
  between operations  1.75 us (2%)
    ppermute x6, waiting for transfers between devices, stripped(): return lax.ppermute(block, AXES, route)  20.4 us
    ppermute x6, waiting for transfers between devices, permuted(): return lax.ppermute(block, AXES, route)  16.4 us
    ppermute x6, starting transfers between devices, permuted(): return lax.ppermute(block, AXES, route)  10.9 us
    ppermute x2, starting transfers between devices, rims(): lax.ppermute(jnp.where(even, last, first), 'strip', [(z, z ^ 1) for z in...  6.12 us
    ppermute x6, starting transfers between devices, stripped(): return lax.ppermute(block, AXES, route)  5.51 us
    ppermute x2, waiting for transfers between devices, rims(): lax.ppermute(jnp.where(even, last, first), 'strip', [(z, z ^ 1) for z in...  3.78 us
    unnamed x72, local copies, waits for them, and re-layouts  3.69 us
    dot_general x4, matrix products, layer_back(): branch = jnp.dot(patch, kernel, preferred_element_type=jnp.float32)  2.38 us
  transfers between devices with their start and end apart: 23, of which 14 were waited for; matrix products, arithmetic and copies ran while one was open for 11% of the time, Pallas kernels for 0%

profile of v4, /device:TPU:0, one launch (start us, length us, event | category | flops | bytes accessed | tf_op | source)
XLA Modules:
  0.0 84.6 jit_solution(13620187748748143715)
XLA Ops:
  0.7 1.0 %copy.122 = bf16[1,1,4,8,16,256]{5,4,2,3,1,0:T(8,128)(2,1)S(1)} copy(bf16[1,1,4,8,16,256]{5,4,3,2,1,0:T(8,128)(2,1)} %param.5) | data formatting | bytes 524288 | tf_op args[1]
  1.7 0.7 slice_bitcast_fusion.4
  2.9 1.1 %copy_convert_fusion = bf16[1,1,4,8,16,256]{5,4,2,3,1,0:T(8,128)(2,1)S(1)} fusion(s32[1,1,4,8,16,256]{5,4,3,2,1,0:T(8,128)} %param.6), kind=kLoop, calls=%fused_computation.47 | loop fusion | flops 131072 | bytes 786432 | tf_op jit(solution)/shard_map/convert.2
  4.1 0.8 fusion.33
  5.3 0.7 copy.42
  7.0 4.1 %collective-permute-start.2 = (bf16[2,2,4,16,256]{4,3,1,2,0:T(8,128)(2,1)S(1)}, bf16[2,2,4,16,256]{4,3,1,2,0:T(8,128)(2,1)S(1)}, u32[]{:S(2)}, u32[]{:S(2)}) collective-permute-start(bf16[2,2,4,16,256]{4,3,1,2,0:T(8,128)(2,1)S(1)} %get-tuple-element.33), channel_id=1, source_target_pairs={{0,2},{2,0},{4,6},{6,4},{1,3},{3,1},{5,7},{7,5},{8,10},{10,8},{12,... | collective-permute-start | bytes 393224 | tf_op jit(solution)/shard_map/ppermute | solution.py:183
  11.1 2.4 %collective-permute-start.5 = (bf16[2,2,8,16,256]{4,3,1,2,0:T(8,128)(2,1)S(1)}, bf16[2,2,8,16,256]{4,3,1,2,0:T(8,128)(2,1)S(1)}, u32[]{:S(2)}, u32[]{:S(2)}) collective-permute-start(bf16[2,2,8,16,256]{4,3,1,2,0:T(8,128)(2,1)S(1)} %get-tuple-element.24), channel_id=1, source_target_pairs={{0,24},{2,26},{4,28},{6,30},{1,25},{3,27},{5,29},{7,31},{8,16},{10... | collective-permute-start | bytes 786440 | tf_op jit(solution)/shard_map/ppermute | solution.py:154
  13.6 1.3 %collective-permute-done.2 = bf16[2,2,4,16,256]{4,3,1,2,0:T(8,128)(2,1)S(1)} collective-permute-done((bf16[2,2,4,16,256]{4,3,1,2,0:T(8,128)(2,1)S(1)}, bf16[2,2,4,16,256]{4,3,1,2,0:T(8,128)(2,1)S(1)}, u32[]{:S(2)}, u32[]{:S(2)}) %collective-permute-start.2) | collective-permute-done | bytes 131104 | tf_op jit(solution)/shard_map/ppermute | solution.py:183
  15.9 4.2 %collective-permute-done.5 = bf16[2,2,8,16,256]{4,3,1,2,0:T(8,128)(2,1)S(1)} collective-permute-done((bf16[2,2,8,16,256]{4,3,1,2,0:T(8,128)(2,1)S(1)}, bf16[2,2,8,16,256]{4,3,1,2,0:T(8,128)(2,1)S(1)}, u32[]{:S(2)}, u32[]{:S(2)}) %collective-permute-start.5) | collective-permute-done | bytes 262176 | tf_op jit(solution)/shard_map/ppermute | solution.py:154
  20.2 2.0 %collective-permute-start.8 = (bf16[2,4,16,256]{3,2,1,0:T(8,128)(2,1)S(1)}, bf16[2,4,16,256]{3,2,1,0:T(8,128)(2,1)S(1)}, u32[]{:S(2)}, u32[]{:S(2)}) collective-permute-start(bf16[2,4,16,256]{3,2,1,0:T(8,128)(2,1)S(1)} %get-tuple-element.53), channel_id=1, source_target_pairs={{0,2},{2,0},{4,6},{6,4},{1,3},{3,1},{5,7},{7,5},{8,10},{10,8},{12,... | collective-permute-start | bytes 196616 | tf_op jit(solution)/shard_map/ppermute | solution.py:183
  22.2 2.5 %collective-permute-done.8 = bf16[2,4,16,256]{3,2,1,0:T(8,128)(2,1)S(1)} collective-permute-done((bf16[2,4,16,256]{3,2,1,0:T(8,128)(2,1)S(1)}, bf16[2,4,16,256]{3,2,1,0:T(8,128)(2,1)S(1)}, u32[]{:S(2)}, u32[]{:S(2)}) %collective-permute-start.8) | collective-permute-done | bytes 65568 | tf_op jit(solution)/shard_map/ppermute | solution.py:183
  24.8 1.6 %collective-permute-start.17 = (bf16[2,10,16,256]{3,2,0,1:T(8,128)(2,1)S(1)}, bf16[2,10,16,256]{3,2,0,1:T(8,128)(2,1)S(1)}, u32[]{:S(2)}, u32[]{:S(2)}) collective-permute-start(bf16[2,10,16,256]{3,2,0,1:T(8,128)(2,1)S(1)} %get-tuple-element.45), channel_id=1, source_target_pairs={{0,4},{2,6},{4,0},{6,2},{1,5},{3,7},{5,1},{7,3},{8,12},{10,14},{12... | collective-permute-start | bytes 491528 | tf_op jit(solution)/shard_map/ppermute | solution.py:172
  26.9 7.6 %collective-permute-done.17 = bf16[2,10,16,256]{3,2,0,1:T(8,128)(2,1)S(1)} collective-permute-done((bf16[2,10,16,256]{3,2,0,1:T(8,128)(2,1)S(1)}, bf16[2,10,16,256]{3,2,0,1:T(8,128)(2,1)S(1)}, u32[]{:S(2)}, u32[]{:S(2)}) %collective-permute-start.17) | collective-permute-done | bytes 163872 | tf_op jit(solution)/shard_map/ppermute | solution.py:172
  35.8 0.7 fusion.6
  36.6 1.6 %collective-permute-start.4 = (bf16[2,14,16,256]{3,2,0,1:T(8,128)(2,1)S(1)}, bf16[2,14,16,256]{3,2,0,1:T(8,128)(2,1)S(1)}, u32[]{:S(2)}, u32[]{:S(2)}) collective-permute-start(bf16[2,14,16,256]{3,2,0,1:T(8,128)(2,1)S(1)} %copy.45), channel_id=1, source_target_pairs={{0,8},{2,10},{4,12},{6,14},{1,9},{3,11},{5,13},{7,15},{8,0},{10,2}... | collective-permute-start | bytes 688136 | tf_op jit(solution)/shard_map/ppermute | solution.py:154
  38.3 5.8 %collective-permute-done.4 = bf16[2,14,16,256]{3,2,0,1:T(8,128)(2,1)S(1)} collective-permute-done((bf16[2,14,16,256]{3,2,0,1:T(8,128)(2,1)S(1)}, bf16[2,14,16,256]{3,2,0,1:T(8,128)(2,1)S(1)}, u32[]{:S(2)}, u32[]{:S(2)}) %collective-permute-start.4) | collective-permute-done | bytes 229408 | tf_op jit(solution)/shard_map/ppermute | solution.py:154
  45.0 0.6 add_convert_fusion
  47.1 1.6 %collective-permute-start.9 = (bf16[2,10,16,256]{3,2,1,0:T(8,128)(2,1)S(1)}, bf16[2,10,16,256]{3,2,1,0:T(8,128)(2,1)S(1)}, u32[]{:S(2)}, u32[]{:S(2)}) collective-permute-start(bf16[2,10,16,256]{3,2,1,0:T(8,128)(2,1)S(1)} %copy.58), channel_id=1, source_target_pairs={{0,8},{2,10},{4,12},{6,14},{1,9},{3,11},{5,13},{7,15},{8,0},{10,2}... | collective-permute-start | bytes 491528 | tf_op jit(solution)/shard_map/ppermute | solution.py:154
  48.6 2.7 %collective-permute-done.13 = bf16[2,8,16,256]{3,2,0,1:T(8,128)(2,1)S(1)} collective-permute-done((bf16[2,8,16,256]{3,2,0,1:T(8,128)(2,1)S(1)}, bf16[2,8,16,256]{3,2,0,1:T(8,128)(2,1)S(1)}, u32[]{:S(2)}, u32[]{:S(2)}) %collective-permute-start.13) | collective-permute-done | bytes 131104 | tf_op jit(solution)/shard_map/ppermute | solution.py:172
  52.6 2.3 %collective-permute-start.18 = (bf16[2,8,16,256]{3,2,1,0:T(8,128)(2,1)S(1)}, bf16[2,8,16,256]{3,2,1,0:T(8,128)(2,1)S(1)}, u32[]{:S(2)}, u32[]{:S(2)}) collective-permute-start(bf16[2,8,16,256]{3,2,1,0:T(8,128)(2,1)S(1)} %slice_select_fusion), channel_id=1, source_target_pairs={{0,4},{2,6},{4,0},{6,2},{1,5},{3,7},{5,1},{7,3},{8,12},{10,14},{12... | collective-permute-start | bytes 393224 | tf_op jit(solution)/shard_map/ppermute | solution.py:172
  55.9 2.5 %collective-permute-start.10 = (bf16[2,8,16,256]{3,2,1,0:T(8,128)(2,1)S(1)}, bf16[2,8,16,256]{3,2,1,0:T(8,128)(2,1)S(1)}, u32[]{:S(2)}, u32[]{:S(2)}) collective-permute-start(bf16[2,8,16,256]{3,2,1,0:T(8,128)(2,1)S(1)} %fusion.57), channel_id=1, source_target_pairs={{0,24},{2,26},{4,28},{6,30},{1,25},{3,27},{5,29},{7,31},{8,16},{10... | collective-permute-start | bytes 393224 | tf_op jit(solution)/shard_map/ppermute | solution.py:154
  58.4 3.1 %collective-permute-done.18 = bf16[2,8,16,256]{3,2,1,0:T(8,128)(2,1)S(1)} collective-permute-done((bf16[2,8,16,256]{3,2,1,0:T(8,128)(2,1)S(1)}, bf16[2,8,16,256]{3,2,1,0:T(8,128)(2,1)S(1)}, u32[]{:S(2)}, u32[]{:S(2)}) %collective-permute-start.18) | collective-permute-done | bytes 131104 | tf_op jit(solution)/shard_map/ppermute | solution.py:172
  62.6 1.3 %collective-permute-done.19 = bf16[2,288,256]{2,1,0:T(8,128)(2,1)S(1)} collective-permute-done((bf16[2,288,256]{2,1,0:T(8,128)(2,1)S(1)}, bf16[2,288,256]{2,1,0:T(8,128)(2,1)S(1)}, u32[]{:S(2)}, u32[]{:S(2)}) %collective-permute-start.19) | collective-permute-done | bytes 294944 | tf_op jit(solution)/shard_map/ppermute | solution.py:157
  64.0 1.1 %collective-permute-start.20 = (bf16[288,256]{1,0:T(8,128)(2,1)S(1)}, bf16[288,256]{1,0:T(8,128)(2,1)S(1)}, u32[]{:S(2)}, u32[]{:S(2)}) collective-permute-start(bf16[288,256]{1,0:T(8,128)(2,1)S(1)} %fusion.54), channel_id=1, source_target_pairs={{0,2},{2,0},{4,6},{6,4},{1,3},{3,1},{5,7},{7,5},{8,10},{10,8},{12,... | collective-permute-start | bytes 442376 | tf_op jit(solution)/shard_map/ppermute | solution.py:172
  65.1 6.9 %collective-permute-done.15 = bf16[288,256]{1,0:T(8,128)(2,1)S(1)} collective-permute-done((bf16[288,256]{1,0:T(8,128)(2,1)S(1)}, bf16[288,256]{1,0:T(8,128)(2,1)S(1)}, u32[]{:S(2)}, u32[]{:S(2)}) %collective-permute-start.15) | collective-permute-done | bytes 147488 | tf_op jit(solution)/shard_map/ppermute | solution.py:172
  72.1 2.1 %collective-permute-start.16 = (bf16[288,256]{1,0:T(8,128)(2,1)S(1)}, bf16[288,256]{1,0:T(8,128)(2,1)S(1)}, u32[]{:S(2)}, u32[]{:S(2)}) collective-permute-start(bf16[288,256]{1,0:T(8,128)(2,1)S(1)} %get-tuple-element.4), channel_id=1, source_target_pairs={{0,25},{2,27},{4,29},{6,31},{1,24},{3,26},{5,28},{7,30},{8,17},{10... | collective-permute-start | bytes 442376 | tf_op jit(solution)/shard_map/ppermute | solution.py:154
  74.3 0.7 collective-permute-start.21
  75.0 0.9 %collective-permute-start.11 = (bf16[2,8,16,256]{3,2,1,0:T(8,128)(2,1)S(1)}, bf16[2,8,16,256]{3,2,1,0:T(8,128)(2,1)S(1)}, u32[]{:S(2)}, u32[]{:S(2)}) collective-permute-start(bf16[2,8,16,256]{3,2,1,0:T(8,128)(2,1)S(1)} %get-tuple-element.17), channel_id=1, source_target_pairs={{0,1},{1,0},{2,3},{3,2},{4,5},{5,4},{6,7},{7,6},{8,9},{9,8},{10,11... | collective-permute-start | bytes 393224 | tf_op jit(solution)/shard_map/ppermute | solution.py:157
  75.9 3.1 %collective-permute-done.16 = bf16[288,256]{1,0:T(8,128)(2,1)S(1)} collective-permute-done((bf16[288,256]{1,0:T(8,128)(2,1)S(1)}, bf16[288,256]{1,0:T(8,128)(2,1)S(1)}, u32[]{:S(2)}, u32[]{:S(2)}) %collective-permute-start.16) | collective-permute-done | bytes 147488 | tf_op jit(solution)/shard_map/ppermute | solution.py:154
  79.0 3.2 %collective-permute-done.21 = bf16[288,256]{1,0:T(8,128)(2,1)S(1)} collective-permute-done((bf16[288,256]{1,0:T(8,128)(2,1)S(1)}, bf16[288,256]{1,0:T(8,128)(2,1)S(1)}, u32[]{:S(2)}, u32[]{:S(2)}) %collective-permute-start.21) | collective-permute-done | bytes 147488 | tf_op jit(solution)/shard_map/ppermute | solution.py:154
  82.4 0.7 maximum_bitcast_fusion
  83.7 0.9 %fusion.15 = f32[1,1,576,256]{3,2,1,0:T(8,128)} fusion(f32[1,1,288,256]{3,2,1,0:T(8,128)S(1)} %bitcast_convert_fusion, f32[1,1,288,256]{3,2,1,0:T(8,128)S(1)} %get-tuple-element.12, pred[]{:T(512)S(6)} %eq.19), kind=kLoop, calls=%fused_computation.39 | loop fusion | flops 589824 | bytes 1179649 | tf_op jit(solution)/shard_map/mul | solution.py:335
  (169 shorter events, 11.2 us)
Async XLA Ops:
  0.6 3.3 %copy-start = (s32[1,1,4,8,16,256]{5,4,3,2,1,0:T(8,128)S(1)}, s32[1,1,4,8,16,256]{5,4,3,2,1,0:T(8,128)}, u32[]{:S(2)}) copy-start(s32[1,1,4,8,16,256]{5,4,3,2,1,0:T(8,128)} %param.6) | copy-start | bytes 1572868
  0.6 3.4 %copy-start.2 = (bf16[1,4,8,16,256]{4,3,2,1,0:T(8,128)(2,1)S(1)}, bf16[1,4,8,16,256]{4,3,2,1,0:T(8,128)(2,1)}, u32[]{:S(2)}) copy-start(bf16[1,4,8,16,256]{4,3,2,1,0:T(8,128)(2,1)} %param.4) | copy-start | bytes 786436
  2.4 3.8 %collective-permute-start.6 = (bf16[2,8,16,256]{3,2,0,1:T(8,128)(2,1)}, bf16[2,8,16,256]{3,2,0,1:T(8,128)(2,1)S(1)}, u32[]{:S(2)}, u32[]{:S(2)}) collective-permute-start(bf16[2,8,16,256]{3,2,0,1:T(8,128)(2,1)} %slice_bitcast_fusion.4), channel_id=1, source_target_pairs={{0,1},{1,0},{2,3},{3,2},{4,5},{5,4},{6,7},{7,6},{8,9},{9,8},{10,11... | collective-permute-start | bytes 393224 | tf_op jit(solution)/shard_map/ppermute | solution.py:157
  4.0 1.4 %copy-start.1 = (bf16[1,1,3,3,256,256]{5,4,3,2,1,0:T(8,128)(2,1)S(1)}, bf16[1,1,3,3,256,256]{5,4,3,2,1,0:T(8,128)(2,1)}, u32[]{:S(2)}) copy-start(bf16[1,1,3,3,256,256]{5,4,3,2,1,0:T(8,128)(2,1)} %param.7) | copy-start | bytes 3538948
  4.9 1.7 %collective-permute-start = (bf16[2,2,8,16,256]{4,3,1,2,0:T(8,128)(2,1)}, bf16[2,2,8,16,256]{4,3,1,2,0:T(8,128)(2,1)S(1)}, u32[]{:S(2)}, u32[]{:S(2)}) collective-permute-start(bf16[2,2,8,16,256]{4,3,1,2,0:T(8,128)(2,1)} %fusion.33), channel_id=1, source_target_pairs={{0,1},{1,0},{2,3},{3,2},{4,5},{5,4},{6,7},{7,6},{8,9},{9,8},{10,11... | collective-permute-start | bytes 786440 | tf_op jit(solution)/shard_map/ppermute | solution.py:157
  6.0 29.6 %collective-permute-start.3 = (bf16[3,3,256,256]{2,3,1,0:T(8,128)(2,1)S(1)}, bf16[3,3,256,256]{2,3,1,0:T(8,128)(2,1)S(1)}, u32[]{:S(2)}, u32[]{:S(2)}) collective-permute-start(bf16[3,3,256,256]{2,3,1,0:T(8,128)(2,1)S(1)} %bitcast.157), channel_id=1, source_target_pairs={{0,1},{1,0},{2,3},{3,2},{4,5},{5,4},{6,7},{7,6},{8,9},{9,8},{10,11... | collective-permute-start | bytes 3538952 | tf_op jit(solution)/shard_map/ppermute | solution.py:157
  6.8 6.8 %collective-permute-start.1 = (bf16[2,2,4,16,256]{4,3,1,2,0:T(8,128)(2,1)S(1)}, bf16[2,2,4,16,256]{4,3,1,2,0:T(8,128)(2,1)S(1)}, u32[]{:S(2)}, u32[]{:S(2)}) collective-permute-start(bf16[2,2,4,16,256]{4,3,1,2,0:T(8,128)(2,1)S(1)} %get-tuple-element.32), channel_id=1, source_target_pairs={{0,1},{2,4},{4,2},{6,7},{1,0},{3,5},{5,3},{7,6},{8,9},{10,12},{12,... | collective-permute-start | bytes 393224 | tf_op jit(solution)/shard_map/ppermute | solution.py:194
  7.0 7.9 %collective-permute-start.2 = (bf16[2,2,4,16,256]{4,3,1,2,0:T(8,128)(2,1)S(1)}, bf16[2,2,4,16,256]{4,3,1,2,0:T(8,128)(2,1)S(1)}, u32[]{:S(2)}, u32[]{:S(2)}) collective-permute-start(bf16[2,2,4,16,256]{4,3,1,2,0:T(8,128)(2,1)S(1)} %get-tuple-element.33), channel_id=1, source_target_pairs={{0,2},{2,0},{4,6},{6,4},{1,3},{3,1},{5,7},{7,5},{8,10},{10,8},{12,... | collective-permute-start | bytes 393224 | tf_op jit(solution)/shard_map/ppermute | solution.py:183
  11.1 8.9 %collective-permute-start.5 = (bf16[2,2,8,16,256]{4,3,1,2,0:T(8,128)(2,1)S(1)}, bf16[2,2,8,16,256]{4,3,1,2,0:T(8,128)(2,1)S(1)}, u32[]{:S(2)}, u32[]{:S(2)}) collective-permute-start(bf16[2,2,8,16,256]{4,3,1,2,0:T(8,128)(2,1)S(1)} %get-tuple-element.24), channel_id=1, source_target_pairs={{0,24},{2,26},{4,28},{6,30},{1,25},{3,27},{5,29},{7,31},{8,16},{10... | collective-permute-start | bytes 786440 | tf_op jit(solution)/shard_map/ppermute | solution.py:154
  20.1 2.1 %collective-permute-start.7 = (bf16[2,4,16,256]{3,2,1,0:T(8,128)(2,1)S(1)}, bf16[2,4,16,256]{3,2,1,0:T(8,128)(2,1)S(1)}, u32[]{:S(2)}, u32[]{:S(2)}) collective-permute-start(bf16[2,4,16,256]{3,2,1,0:T(8,128)(2,1)S(1)} %get-tuple-element.52), channel_id=1, source_target_pairs={{0,1},{2,4},{4,2},{6,7},{1,0},{3,5},{5,3},{7,6},{8,9},{10,12},{12,... | collective-permute-start | bytes 196616 | tf_op jit(solution)/shard_map/ppermute | solution.py:194
  20.2 4.5 %collective-permute-start.8 = (bf16[2,4,16,256]{3,2,1,0:T(8,128)(2,1)S(1)}, bf16[2,4,16,256]{3,2,1,0:T(8,128)(2,1)S(1)}, u32[]{:S(2)}, u32[]{:S(2)}) collective-permute-start(bf16[2,4,16,256]{3,2,1,0:T(8,128)(2,1)S(1)} %get-tuple-element.53), channel_id=1, source_target_pairs={{0,2},{2,0},{4,6},{6,4},{1,3},{3,1},{5,7},{7,5},{8,10},{10,8},{12,... | collective-permute-start | bytes 196616 | tf_op jit(solution)/shard_map/ppermute | solution.py:183
  24.8 9.7 %collective-permute-start.17 = (bf16[2,10,16,256]{3,2,0,1:T(8,128)(2,1)S(1)}, bf16[2,10,16,256]{3,2,0,1:T(8,128)(2,1)S(1)}, u32[]{:S(2)}, u32[]{:S(2)}) collective-permute-start(bf16[2,10,16,256]{3,2,0,1:T(8,128)(2,1)S(1)} %get-tuple-element.45), channel_id=1, source_target_pairs={{0,4},{2,6},{4,0},{6,2},{1,5},{3,7},{5,1},{7,3},{8,12},{10,14},{12... | collective-permute-start | bytes 491528 | tf_op jit(solution)/shard_map/ppermute | solution.py:172
  26.4 8.7 %collective-permute-start.12 = (bf16[2,10,16,256]{3,2,0,1:T(8,128)(2,1)S(1)}, bf16[2,10,16,256]{3,2,0,1:T(8,128)(2,1)S(1)}, u32[]{:S(2)}, u32[]{:S(2)}) collective-permute-start(bf16[2,10,16,256]{3,2,0,1:T(8,128)(2,1)S(1)} %get-tuple-element.47), channel_id=1, source_target_pairs={{0,2},{2,0},{4,6},{6,4},{1,3},{3,1},{5,7},{7,5},{8,10},{10,8},{12,... | collective-permute-start | bytes 491528 | tf_op jit(solution)/shard_map/ppermute | solution.py:172
  36.6 7.6 %collective-permute-start.4 = (bf16[2,14,16,256]{3,2,0,1:T(8,128)(2,1)S(1)}, bf16[2,14,16,256]{3,2,0,1:T(8,128)(2,1)S(1)}, u32[]{:S(2)}, u32[]{:S(2)}) collective-permute-start(bf16[2,14,16,256]{3,2,0,1:T(8,128)(2,1)S(1)} %copy.45), channel_id=1, source_target_pairs={{0,8},{2,10},{4,12},{6,14},{1,9},{3,11},{5,13},{7,15},{8,0},{10,2}... | collective-permute-start | bytes 688136 | tf_op jit(solution)/shard_map/ppermute | solution.py:154
  46.3 5.0 %collective-permute-start.13 = (bf16[2,8,16,256]{3,2,0,1:T(8,128)(2,1)S(1)}, bf16[2,8,16,256]{3,2,0,1:T(8,128)(2,1)S(1)}, u32[]{:S(2)}, u32[]{:S(2)}) collective-permute-start(bf16[2,8,16,256]{3,2,0,1:T(8,128)(2,1)S(1)} %slice_select_fusion.1), channel_id=1, source_target_pairs={{0,2},{2,0},{4,6},{6,4},{1,3},{3,1},{5,7},{7,5},{8,10},{10,8},{12,... | collective-permute-start | bytes 393224 | tf_op jit(solution)/shard_map/ppermute | solution.py:172
  47.1 5.4 %collective-permute-start.9 = (bf16[2,10,16,256]{3,2,1,0:T(8,128)(2,1)S(1)}, bf16[2,10,16,256]{3,2,1,0:T(8,128)(2,1)S(1)}, u32[]{:S(2)}, u32[]{:S(2)}) collective-permute-start(bf16[2,10,16,256]{3,2,1,0:T(8,128)(2,1)S(1)} %copy.58), channel_id=1, source_target_pairs={{0,8},{2,10},{4,12},{6,14},{1,9},{3,11},{5,13},{7,15},{8,0},{10,2}... | collective-permute-start | bytes 491528 | tf_op jit(solution)/shard_map/ppermute | solution.py:154
  52.2 10.2 %collective-permute-start.14 = (bf16[2,288,256]{2,1,0:T(8,128)(2,1)S(1)}, bf16[2,288,256]{2,1,0:T(8,128)(2,1)S(1)}, u32[]{:S(2)}, u32[]{:S(2)}) collective-permute-start(bf16[2,288,256]{2,1,0:T(8,128)(2,1)S(1)} %fusion.16), channel_id=1, source_target_pairs={{0,1},{1,0},{2,3},{3,2},{4,5},{5,4},{6,7},{7,6},{8,9},{9,8},{10,11... | collective-permute-start | bytes 884744 | tf_op jit(solution)/shard_map/ppermute | solution.py:157
  52.6 8.9 %collective-permute-start.18 = (bf16[2,8,16,256]{3,2,1,0:T(8,128)(2,1)S(1)}, bf16[2,8,16,256]{3,2,1,0:T(8,128)(2,1)S(1)}, u32[]{:S(2)}, u32[]{:S(2)}) collective-permute-start(bf16[2,8,16,256]{3,2,1,0:T(8,128)(2,1)S(1)} %slice_select_fusion), channel_id=1, source_target_pairs={{0,4},{2,6},{4,0},{6,2},{1,5},{3,7},{5,1},{7,3},{8,12},{10,14},{12... | collective-permute-start | bytes 393224 | tf_op jit(solution)/shard_map/ppermute | solution.py:172
  55.9 19.1 %collective-permute-start.10 = (bf16[2,8,16,256]{3,2,1,0:T(8,128)(2,1)S(1)}, bf16[2,8,16,256]{3,2,1,0:T(8,128)(2,1)S(1)}, u32[]{:S(2)}, u32[]{:S(2)}) collective-permute-start(bf16[2,8,16,256]{3,2,1,0:T(8,128)(2,1)S(1)} %fusion.57), channel_id=1, source_target_pairs={{0,24},{2,26},{4,28},{6,30},{1,25},{3,27},{5,29},{7,31},{8,16},{10... | collective-permute-start | bytes 393224 | tf_op jit(solution)/shard_map/ppermute | solution.py:154
  62.2 1.6 %collective-permute-start.19 = (bf16[2,288,256]{2,1,0:T(8,128)(2,1)S(1)}, bf16[2,288,256]{2,1,0:T(8,128)(2,1)S(1)}, u32[]{:S(2)}, u32[]{:S(2)}) collective-permute-start(bf16[2,288,256]{2,1,0:T(8,128)(2,1)S(1)} %fusion.17), channel_id=1, source_target_pairs={{0,1},{1,0},{2,3},{3,2},{4,5},{5,4},{6,7},{7,6},{8,9},{9,8},{10,11... | collective-permute-start | bytes 884744 | tf_op jit(solution)/shard_map/ppermute | solution.py:157
  62.5 9.5 %collective-permute-start.15 = (bf16[288,256]{1,0:T(8,128)(2,1)S(1)}, bf16[288,256]{1,0:T(8,128)(2,1)S(1)}, u32[]{:S(2)}, u32[]{:S(2)}) collective-permute-start(bf16[288,256]{1,0:T(8,128)(2,1)S(1)} %fusion.53), channel_id=1, source_target_pairs={{0,4},{2,6},{4,0},{6,2},{1,5},{3,7},{5,1},{7,3},{8,12},{10,14},{12... | collective-permute-start | bytes 442376 | tf_op jit(solution)/shard_map/ppermute | solution.py:172
  64.0 10.2 %collective-permute-start.20 = (bf16[288,256]{1,0:T(8,128)(2,1)S(1)}, bf16[288,256]{1,0:T(8,128)(2,1)S(1)}, u32[]{:S(2)}, u32[]{:S(2)}) collective-permute-start(bf16[288,256]{1,0:T(8,128)(2,1)S(1)} %fusion.54), channel_id=1, source_target_pairs={{0,2},{2,0},{4,6},{6,4},{1,3},{3,1},{5,7},{7,5},{8,10},{10,8},{12,... | collective-permute-start | bytes 442376 | tf_op jit(solution)/shard_map/ppermute | solution.py:172
  72.1 6.9 %collective-permute-start.16 = (bf16[288,256]{1,0:T(8,128)(2,1)S(1)}, bf16[288,256]{1,0:T(8,128)(2,1)S(1)}, u32[]{:S(2)}, u32[]{:S(2)}) collective-permute-start(bf16[288,256]{1,0:T(8,128)(2,1)S(1)} %get-tuple-element.4), channel_id=1, source_target_pairs={{0,25},{2,27},{4,29},{6,31},{1,24},{3,26},{5,28},{7,30},{8,17},{10... | collective-permute-start | bytes 442376 | tf_op jit(solution)/shard_map/ppermute | solution.py:154
  74.3 7.9 %collective-permute-start.21 = (bf16[288,256]{1,0:T(8,128)(2,1)S(1)}, bf16[288,256]{1,0:T(8,128)(2,1)S(1)}, u32[]{:S(2)}, u32[]{:S(2)}) collective-permute-start(bf16[288,256]{1,0:T(8,128)(2,1)S(1)} %get-tuple-element.2), channel_id=1, source_target_pairs={{0,25},{2,27},{4,29},{6,31},{1,24},{3,26},{5,28},{7,30},{8,17},{10... | collective-permute-start | bytes 442376 | tf_op jit(solution)/shard_map/ppermute | solution.py:154
  75.0 7.4 %collective-permute-start.11 = (bf16[2,8,16,256]{3,2,1,0:T(8,128)(2,1)S(1)}, bf16[2,8,16,256]{3,2,1,0:T(8,128)(2,1)S(1)}, u32[]{:S(2)}, u32[]{:S(2)}) collective-permute-start(bf16[2,8,16,256]{3,2,1,0:T(8,128)(2,1)S(1)} %get-tuple-element.17), channel_id=1, source_target_pairs={{0,1},{1,0},{2,3},{3,2},{4,5},{5,4},{6,7},{7,6},{8,9},{9,8},{10,11... | collective-permute-start | bytes 393224 | tf_op jit(solution)/shard_map/ppermute | solution.py:157
  82.3 1.4 %collective-permute-start.22 = (bf16[288,256]{1,0:T(8,128)(2,1)S(1)}, bf16[288,256]{1,0:T(8,128)(2,1)S(1)}, u32[]{:S(2)}, u32[]{:S(2)}) collective-permute-start(bf16[288,256]{1,0:T(8,128)(2,1)S(1)} %get-tuple-element.13), channel_id=1, source_target_pairs={{0,1},{1,0},{2,3},{3,2},{4,5},{5,4},{6,7},{7,6},{8,9},{9,8},{10,11... | collective-permute-start | bytes 442376 | tf_op jit(solution)/shard_map/ppermute | solution.py:157
